TPU v7x, 512 devices: a whole 4x4x16 slice. The times are simulated.
512 devices in a mesh: seq: 64 (over y, z_lo, core), strand: 2 (over z_hi), head: 4 (over x).
Axes of the slice: x: 4, y: 4, z: 16 (z_hi: 2, z_lo: 8; z = z_hi * 8 + z_lo), core: 2. Of those that a mesh axis runs over, the one named last changes fastest.
Arguments:
- top: bfloat16 [4, 2, 16384, 1536], P('head', 'strand', 'seq'), may hold values from -6 to 6
- grad_heads: bfloat16 [4, 2, 16384, 1536], P(None, 'strand', 'seq', 'head'), may hold values from -6 to 6
- tap_weight_grid: bfloat16 [3, 768, 768], P(None, 'seq'), may hold values from -0.125 to 0.125
- out_w: bfloat16 [768, 768], P('seq'), may hold values from -0.21875 to 0.21875
- mix_w: bfloat16 [768, 768], P('seq'), may hold values from -0.21875 to 0.21875
- rc_perm: int32 [768], replicated, may hold values from 0 to 767, each once
Outputs:
- restored: bfloat16 [4, 2, 16384, 1536], P('head', 'strand', 'seq')
- grad_input: bfloat16 [4, 2, 16384, 1536], P('head', 'strand', 'seq')
Inputs may be any that keep to these rules, and one draw needn't show every extreme that they name: `rc_perm`: every channel index appears exactly once.
All inputs are finite; a program needn't handle non-finite values.
Results may differ from a plain program's by a relative error of at most 0.008.
Values may be sent and summed in bfloat16 or wider, within the bound.
No kernel may reach another device: no remote copies, remote signals or barrier semaphores. Data moves between devices by JAX's collectives and lax.ppermute only.
A program may use at most 64 MiB of HBM per device.

v0:
```python
import jax
import jax.numpy as jnp
from jax import lax
from jax.sharding import PartitionSpec as P


def rows_first(arrays, axis, dims):
    turned = [jnp.moveaxis(a, dim, 0) for a, dim in zip(arrays, dims)]
    widths = [t[0].size for t in turned]
    both = jnp.concatenate([t.reshape(-1, w) for t, w in zip(turned, widths)], axis=1)
    result = lax.all_gather(both, axis, axis=0, tiled=True)
    pieces = jnp.split(result, [sum(widths[:k]) for k in range(1, len(widths))], axis=1)
    return tuple(
        (
            jnp.moveaxis(b.reshape(-1, *t.shape[1:]), 0, dim)
            for b, t, dim in zip(pieces, turned, dims)
        )
    )


def swapped(value, axis, bit):
    mask = 2**bit
    pairs = [(source, source ^ mask) for source in range(lax.axis_size(axis))]
    return lax.ppermute(value, axis, pairs)


def with_halo(array, sides, width):
    for axis, dim in sides:
        devices, length = (lax.axis_size(axis), array.shape[dim])
        up = [(i, (i + 1) % devices) for i in range(devices - 1)]
        down = [(j, i) for i, j in up]
        last = lax.slice_in_dim(array, length - width, length, axis=dim)
        first = lax.slice_in_dim(array, 0, width, axis=dim)
        before = lax.ppermute(last, axis, up)
        after = lax.ppermute(first, axis, down)
        array = jnp.concatenate([before, array, after], axis=dim)
    return array


def taps_forward(padded, kernel, length, dilation):
    total = jnp.dot(padded[0:length], kernel[0], preferred_element_type=jnp.float32)
    total = total + jnp.dot(
        padded[dilation : dilation + length], kernel[1], preferred_element_type=jnp.float32
    )
    return total + jnp.dot(
        padded[2 * dilation : 2 * dilation + length], kernel[2], preferred_element_type=jnp.float32
    )


def taps_backward(padded, kernel, length, dilation):
    total = jnp.einsum(
        "pd,cd->pc",
        padded[2 * dilation : 2 * dilation + length],
        kernel[0],
        preferred_element_type=jnp.float32,
    )
    total = total + jnp.einsum(
        "pd,cd->pc",
        padded[dilation : dilation + length],
        kernel[1],
        preferred_element_type=jnp.float32,
    )
    return total + jnp.einsum(
        "pd,cd->pc", padded[0:length], kernel[2], preferred_element_type=jnp.float32
    )


def shards(top, grad_heads, tap_weight_grid, out_w, mix_w, rc_perm):
    length = top.shape[2]
    dilation = length // 2
    half = top.shape[3] // 2
    cotan = lax.all_to_all(grad_heads, "head", split_axis=0, concat_axis=3, tiled=True)[0, 0]
    conv_full, out_full, mix_full = rows_first((tap_weight_grid, out_w, mix_w), "seq", (1, 0, 0))
    top_a = top[0, 0, :, :half]
    top_b = top[0, 0, :, half:]
    grad_a = cotan[:, :half]
    second_gradient = cotan[:, half:]
    inverse = jnp.zeros((half,), jnp.int32).at[rc_perm].set(jnp.arange(half, dtype=jnp.int32))
    other_a = swapped(top_a, "strand", 0)
    mirror = jnp.take(other_a, rc_perm, axis=1)
    paired = (top_a.astype(jnp.float32) + mirror.astype(jnp.float32)).astype(jnp.bfloat16)
    mixing = jnp.dot(paired, mix_full, preferred_element_type=jnp.float32)
    second_input = (top_b.astype(jnp.float32) - mixing).astype(jnp.bfloat16)
    padded_b = with_halo(second_input, (("seq", 0),), dilation)
    preactivation_rows = taps_forward(padded_b, conv_full, length, dilation)
    hidden = jax.nn.gelu(preactivation_rows).astype(jnp.bfloat16)
    branch_out = jnp.dot(hidden, out_full, preferred_element_type=jnp.float32)
    input_a = (top_a.astype(jnp.float32) - branch_out).astype(jnp.bfloat16)
    backed = jnp.einsum(
        "pd,cd->pc", second_gradient, mix_full, preferred_element_type=jnp.float32
    ).astype(jnp.bfloat16)
    returned = swapped(jnp.take(backed, inverse, axis=1), "strand", 0)
    cot_a = (
        grad_a.astype(jnp.float32) + backed.astype(jnp.float32) + returned.astype(jnp.float32)
    ).astype(jnp.bfloat16)
    pulled = jnp.einsum("pd,cd->pc", cot_a, out_full, preferred_element_type=jnp.float32)
    unused, slope = jax.vjp(jax.nn.gelu, preactivation_rows)
    preactivation_cotangent = slope(pulled)[0].astype(jnp.bfloat16)
    padded_cot = with_halo(preactivation_cotangent, (("seq", 0),), dilation)
    cotangent_second = (
        second_gradient.astype(jnp.float32) + taps_backward(padded_cot, conv_full, length, dilation)
    ).astype(jnp.bfloat16)
    restored = jnp.concatenate([input_a, second_input], axis=1)[None, None]
    grad_input = jnp.concatenate([cot_a, cotangent_second], axis=1)[None, None]
    return (restored, grad_input)


def solution(mesh):
    placed = (
        P("head", "strand", "seq", None),
        P(None, "strand", "seq", "head"),
        P(None, "seq", None),
        P("seq", None),
        P("seq", None),
        P(),
    )
    return jax.shard_map(
        shards,
        mesh=mesh,
        in_specs=placed,
        out_specs=(P("head", "strand", "seq", None), P("head", "strand", "seq", None)),
        check_vma=False,
    )
```

profile of v0, /device:TPU:107, one launch (start us, length us, event | category | flops | bytes accessed | tf_op | source)
XLA Modules:
  0.0 258.3 jit_solution(8820897414289662014)
XLA Ops:
  7.2 0.0 all-gather.3.cloned.1.call-start
  7.2 0.9 copy.29
  8.1 0.0 copy-start.3
  8.2 1.4 maximum_bitcast_fusion.2
  9.6 0.0 all-gather.3.cloned.1.call-update
  9.7 1.0 slice_bitcast_fusion.9
  10.7 12.7 %collective-permute-start = (bf16[256,768]{1,0:T(8,128)(2,1)S(1)}, bf16[256,768]{1,0:T(8,128)(2,1)S(1)}, u32[]{:S(2)}, u32[]{:S(2)}) collective-permute-start(bf16[256,768]{1,0:T(8,128)(2,1)S(1)} %slice_bitcast_fusion.9), channel_id=1, source_target_pairs={{0,4},{4,0},{1,5},{5,1},{2,6},{6,2},{3,7},{7,3},{8,12},{12,8},{9,1... | collective-permute-start | bytes 1179656 | tf_op jit(solution)/shard_map/ppermute | solution.py:24
  23.4 4.3 %all-to-all-start = ((bf16[4,1,256,384]{3,2,1,0:T(8,128)(2,1)}), bf16[4,1,256,384]{3,2,1,0:T(8,128)(2,1)S(1)}, u32[]{:S(2)}, u32[]{:S(2)}) async-start(bf16[4,1,256,384]{3,2,1,0:T(8,128)(2,1)} %param.9), calls=%async_computation | async-start | bytes 1572864 | tf_op jit(solution)/shard_map/all_to_all | solution.py:72
  27.7 0.0 copy-done.3
  27.7 3.4 %scatter_custom_fusion = s32[768]{0:T(1024)S(1)} fusion(s32[768]{0:T(1024)S(1)} %compare_select_fusion.1, s32[768]{0:T(1024)S(1)} %iota.3, s32[]{:T(128)} %constant.9.clone.1), kind=kCustom, calls=%fused_computation.68 | custom fusion | bytes 3076 | tf_op jit(solution)/shard_map/scatter | solution.py:78
  31.2 16.3 %collective-permute-done = bf16[256,768]{1,0:T(8,128)(2,1)S(1)} collective-permute-done((bf16[256,768]{1,0:T(8,128)(2,1)S(1)}, bf16[256,768]{1,0:T(8,128)(2,1)S(1)}, u32[]{:S(2)}, u32[]{:S(2)}) %collective-permute-start) | collective-permute-done | bytes 393248 | tf_op jit(solution)/shard_map/ppermute | solution.py:24
  47.5 0.2 copy.27
  47.7 2.7 %gather_fusion = bf16[768,256]{1,0:T(8,128)(2,1)S(1)} fusion(bf16[256,768]{0,1:T(8,128)(2,1)S(1)} %copy.27, s32[1024]{0:T(1024)S(1)} %pad_clamp_fusion.1), kind=kCustom, calls=%fused_computation.clone | custom fusion | bytes 789504 | tf_op jit(solution)/shard_map/jit(_take)/gather | solution.py:80
  50.4 0.9 copy.28
  51.3 0.0 all-to-all-done
  51.3 1.2 copy.34
  52.4 111.7 %all-gather.3.cloned.1.call-done = bf16[64,12,3840]{2,1,0:T(8,128)(2,1)} async-done(((bf16[1,12,3840]{2,1,0:T(8,128)(2,1)}), bf16[64,12,3840]{2,1,0:T(8,128)(2,1)}) %all-gather.3.cloned.1.call-update) | async-done | bytes 5898256 | tf_op jit(solution)/shard_map/all_gather | solution.py:11
  164.1 9.6 %reshape.49 = bf16[768,3840]{1,0:T(8,128)(2,1)} reshape(bf16[64,12,3840]{2,1,0:T(8,128)(2,1)} %all-gather.3.cloned.1.call-done) | data formatting | bytes 11796480
  173.7 0.0 slice-start.2
  173.7 2.0 slice-done.2
  175.7 3.6 %copy.30 = bf16[768,2304]{0,1:T(8,128)(2,1)} copy(bf16[768,2304]{1,0:T(8,128)(2,1)S(1)} %slice-done.2) | data formatting | bytes 7077888 | tf_op jit(solution)/shard_map/split | solution.py:12
  179.3 0.0 copy-start.1
  179.3 2.2 fusion.3
  181.5 2.2 collective-permute-start.2
  183.7 4.6 %collective-permute-start.1 = (bf16[128,768]{1,0:T(8,128)(2,1)S(1)}, bf16[128,768]{1,0:T(8,128)(2,1)S(1)}, u32[]{:S(2)}, u32[]{:S(2)}) collective-permute-start(bf16[128,768]{1,0:T(8,128)(2,1)S(1)} %get-tuple-element.11), channel_id=1, source_target_pairs={{0,8},{8,16},{16,24},{24,32},{32,40},{40,48},{48,56},{56,64},{64,7... | collective-permute-start | bytes 589832 | tf_op jit(solution)/shard_map/ppermute | solution.py:34
  188.3 0.0 copy-done.1
  188.3 1.7 fusion.6
  190.0 2.7 %gather_fusion.1 = bf16[768,256]{1,0:T(8,128)(2,1)S(1)} fusion(bf16[256,768]{0,1:T(8,128)(2,1)S(1)} %fusion.6, s32[1024]{0:T(1024)S(1)} %pad_clamp_fusion), kind=kCustom, calls=%fused_computation.1.clone | custom fusion | bytes 789504 | tf_op jit(solution)/shard_map/jit(_take)/gather | solution.py:92
  192.7 0.2 select_bitcast_fusion
  192.9 2.5 collective-permute-start.3
  195.4 0.0 copy-start
  195.4 1.9 fusion.8
  197.3 0.0 collective-permute-done.2
  197.3 1.8 fusion.10
  199.1 0.0 copy-start.2
  199.1 0.0 collective-permute-done.1
  199.1 0.0 copy-done
  199.1 0.0 slice-start
  199.1 0.5 fusion.2
  199.7 0.6 copy-done.2
  200.2 0.0 slice-start.1
  200.2 2.3 fusion.4
  202.5 0.9 maximum_bitcast_fusion
  203.4 32.8 %collective-permute-done.3 = bf16[256,768]{0,1:T(8,128)(2,1)S(1)} collective-permute-done((bf16[256,768]{0,1:T(8,128)(2,1)S(1)}, bf16[256,768]{0,1:T(8,128)(2,1)S(1)}, u32[]{:S(2)}, u32[]{:S(2)}) %collective-permute-start.3) | collective-permute-done | bytes 393248 | tf_op jit(solution)/shard_map/ppermute | solution.py:24
  236.2 0.2 add_convert_fusion
  236.4 0.0 slice-done
  236.4 0.0 slice-done.1
  236.4 0.8 fusion.23
  237.2 4.1 %collective-permute-start.5 = (bf16[128,768]{1,0:T(8,128)(2,1)S(1)}, bf16[128,768]{1,0:T(8,128)(2,1)S(1)}, u32[]{:S(2)}, u32[]{:S(2)}) collective-permute-start(bf16[128,768]{1,0:T(8,128)(2,1)S(1)} %get-tuple-element.10), channel_id=1, source_target_pairs={{0,8},{8,16},{16,24},{24,32},{32,40},{40,48},{48,56},{56,64},{64,7... | collective-permute-start | bytes 589832 | tf_op jit(solution)/shard_map/ppermute | solution.py:34
  241.4 1.9 collective-permute-start.4
  243.3 0.6 fusion.7
  243.9 0.1 collective-permute-done.5
  244.0 0.6 fusion.9
  244.6 5.0 %collective-permute-done.4 = bf16[128,768]{1,0:T(8,128)(2,1)S(1)} collective-permute-done((bf16[128,768]{1,0:T(8,128)(2,1)S(1)}, bf16[128,768]{1,0:T(8,128)(2,1)S(1)}, u32[]{:S(2)}, u32[]{:S(2)}) %collective-permute-start.4) | collective-permute-done | bytes 196640 | tf_op jit(solution)/shard_map/ppermute | solution.py:35
  249.6 0.6 fusion.5
  250.2 0.1 maximum_bitcast_fusion.1
  250.3 1.2 copy.38
  (12 shorter events, 0.1 us)
Async XLA Ops:
  7.2 157.0 %all-gather.3.cloned.1.call-start = ((), (), s32[]{:S(2)}) async-start(), calls=%async_computation.1 | async-start | bytes 7987200 | tf_op jit(solution)/shard_map/all_gather | solution.py:11
  8.1 19.6 %copy-start.3 = (s32[768]{0:T(1024)S(1)}, s32[768]{0:T(1024)}, u32[]{:S(2)}) copy-start(s32[768]{0:T(1024)} %param.13) | copy-start | bytes 9220
  10.7 36.8 %collective-permute-start = (bf16[256,768]{1,0:T(8,128)(2,1)S(1)}, bf16[256,768]{1,0:T(8,128)(2,1)S(1)}, u32[]{:S(2)}, u32[]{:S(2)}) collective-permute-start(bf16[256,768]{1,0:T(8,128)(2,1)S(1)} %slice_bitcast_fusion.9), channel_id=1, source_target_pairs={{0,4},{4,0},{1,5},{5,1},{2,6},{6,2},{3,7},{7,3},{8,12},{12,8},{9,1... | collective-permute-start | bytes 1179656 | tf_op jit(solution)/shard_map/ppermute | solution.py:24
  23.4 27.8 %all-to-all-start = ((bf16[4,1,256,384]{3,2,1,0:T(8,128)(2,1)}), bf16[4,1,256,384]{3,2,1,0:T(8,128)(2,1)S(1)}, u32[]{:S(2)}, u32[]{:S(2)}) async-start(bf16[4,1,256,384]{3,2,1,0:T(8,128)(2,1)} %param.9), calls=%async_computation | async-start | bytes 1572864 | tf_op jit(solution)/shard_map/all_to_all | solution.py:72
  173.7 2.0 slice-start.2
  179.3 9.0 %copy-start.1 = (bf16[1,1,256,4,384]{2,4,3,1,0:T(8,128)(2,1)S(1)}, bf16[1,1,256,4,384]{2,4,3,1,0:T(8,128)(2,1)}, u32[]{:S(2)}) copy-start(bf16[1,1,256,4,384]{2,4,3,1,0:T(8,128)(2,1)} %copy.34) | copy-start | bytes 2359300
  181.5 15.8 %collective-permute-start.2 = (bf16[128,768]{1,0:T(8,128)(2,1)S(1)}, bf16[128,768]{1,0:T(8,128)(2,1)S(1)}, u32[]{:S(2)}, u32[]{:S(2)}) collective-permute-start(bf16[128,768]{1,0:T(8,128)(2,1)S(1)} %get-tuple-element.12), channel_id=1, source_target_pairs={{8,0},{16,8},{24,16},{32,24},{40,32},{48,40},{56,48},{64,56},{72,6... | collective-permute-start | bytes 589832 | tf_op jit(solution)/shard_map/ppermute | solution.py:35
  183.7 15.4 %collective-permute-start.1 = (bf16[128,768]{1,0:T(8,128)(2,1)S(1)}, bf16[128,768]{1,0:T(8,128)(2,1)S(1)}, u32[]{:S(2)}, u32[]{:S(2)}) collective-permute-start(bf16[128,768]{1,0:T(8,128)(2,1)S(1)} %get-tuple-element.11), channel_id=1, source_target_pairs={{0,8},{8,16},{16,24},{24,32},{32,40},{40,48},{48,56},{56,64},{64,7... | collective-permute-start | bytes 589832 | tf_op jit(solution)/shard_map/ppermute | solution.py:34
  192.9 43.3 %collective-permute-start.3 = (bf16[256,768]{0,1:T(8,128)(2,1)S(1)}, bf16[256,768]{0,1:T(8,128)(2,1)S(1)}, u32[]{:S(2)}, u32[]{:S(2)}) collective-permute-start(bf16[256,768]{0,1:T(8,128)(2,1)S(1)} %select_bitcast_fusion), channel_id=1, source_target_pairs={{0,4},{4,0},{1,5},{5,1},{2,6},{6,2},{3,7},{7,3},{8,12},{12,8},{9,1... | collective-permute-start | bytes 1179656 | tf_op jit(solution)/shard_map/ppermute | solution.py:24
  195.4 3.8 %copy-start = (bf16[768,2304]{0,1:T(8,128)(2,1)S(1)}, bf16[768,2304]{0,1:T(8,128)(2,1)}, u32[]{:S(2)}) copy-start(bf16[768,2304]{0,1:T(8,128)(2,1)} %copy.30) | copy-start | bytes 10616836
  199.1 1.1 copy-start.2
  199.1 37.2 %slice-start = ((s8[5898240]{0:T(1024)(128)(4,1)}), s8[4194304]{0:T(1024)(128)(4,1)S(1)}, s32[]{:S(2)}) async-start(s8[5898240]{0:T(1024)(128)(4,1)} %bitcast.63), calls=%async_computation.2 | async-start | bytes 8388608
  200.2 36.1 %slice-start.1 = ((s8[5898240]{0:T(1024)(128)(4,1)}), s8[1703936]{0:T(1024)(128)(4,1)S(1)}, s32[]{:S(2)}) async-start(s8[5898240]{0:T(1024)(128)(4,1)} %bitcast.63), calls=%async_computation.3 | async-start | bytes 3407872
  237.2 6.7 %collective-permute-start.5 = (bf16[128,768]{1,0:T(8,128)(2,1)S(1)}, bf16[128,768]{1,0:T(8,128)(2,1)S(1)}, u32[]{:S(2)}, u32[]{:S(2)}) collective-permute-start(bf16[128,768]{1,0:T(8,128)(2,1)S(1)} %get-tuple-element.10), channel_id=1, source_target_pairs={{0,8},{8,16},{16,24},{24,32},{32,40},{40,48},{48,56},{56,64},{64,7... | collective-permute-start | bytes 589832 | tf_op jit(solution)/shard_map/ppermute | solution.py:34
  241.4 8.2 %collective-permute-start.4 = (bf16[128,768]{1,0:T(8,128)(2,1)S(1)}, bf16[128,768]{1,0:T(8,128)(2,1)S(1)}, u32[]{:S(2)}, u32[]{:S(2)}) collective-permute-start(bf16[128,768]{1,0:T(8,128)(2,1)S(1)} %get-tuple-element.9), channel_id=1, source_target_pairs={{8,0},{16,8},{24,16},{32,24},{40,32},{48,40},{56,48},{64,56},{72,6... | collective-permute-start | bytes 589832 | tf_op jit(solution)/shard_map/ppermute | solution.py:35
Sparse Core Ops, SparseCore 0:
  10.1 153.9 all-gather.2
where the time goes:
time: 259 us; the launch traced here: 258 us
  waiting for transfers between devices  166 us (64%)
  starting transfers between devices  32.4 us (13%)
  local copies, waits for them, and re-layouts  29.9 us (12%)
  between operations  14.4 us (6%)
  matrix products  13 us (5%)
  other arithmetic  2.79 us (1%)
    all_gather x1, waiting for transfers between devices, rows_first(): result = lax.all_gather(both, axis, axis=0, tiled=True)  112 us
    ppermute x2, waiting for transfers between devices, swapped(): return lax.ppermute(value, axis, pairs)  49.1 us
    ppermute x2, starting transfers between devices, swapped(): return lax.ppermute(value, axis, pairs)  15.2 us
    unnamed x16, local copies, waits for them, and re-layouts  11.4 us
    ppermute x2, starting transfers between devices, with_halo(): before = lax.ppermute(last, axis, up)  8.7 us
    split x3, local copies, waits for them, and re-layouts, rows_first(): jnp.split(result, [sum(widths[:k]) for k in range(1, len(widths))], axis=1)  5.56 us
  transfers between devices with their start and end apart: 8, of which 5 were waited for; matrix products, arithmetic and copies ran while one was open for 9% of the time, Pallas kernels for 0%

commit v1 on v0

v1 whole, which is shorter than its diff:
```python
import jax
import jax.numpy as jnp
from jax import lax
from jax.experimental import pallas as pl
from jax.experimental.pallas import tpu as pltpu
from jax.sharding import PartitionSpec as P

BF16, F32 = jnp.bfloat16, jnp.float32
SHARE = 2


def pairwise(value, bit):
    count = lax.axis_size("seq")
    if bit == 0:
        pairs = [(i, i ^ 1) for i in range(count)]
    else:
        pairs = [(i, i + 1) for i in range(1, count - 1, 2)] + [(i + 1, i) for i in range(1, count - 1, 2)]
    return lax.ppermute(value, "seq", pairs)


def mirrored(value):
    return lax.ppermute(value, "strand", [(0, 1), (1, 0)])


def spread(piece, axes, groups):
    count = len(groups[0])
    sent = jnp.broadcast_to(piece[None], (count, *piece.shape))
    return lax.all_to_all(sent, axes, 0, 0, axis_index_groups=groups, tiled=True)


def piece_of(tap_weight_grid, out_w, mix_w, core):
    heads = lax.axis_size("head")
    own = jnp.concatenate([tap_weight_grid, out_w[None], mix_w[None]], axis=0)
    other = pairwise(own, 0)
    low = jnp.where(core == 0, own, other)
    high = jnp.where(core == 0, other, own)
    mats, rows, width = own.shape
    slabs = jnp.concatenate([low, high], axis=1).reshape(mats * 2 * rows // 8, 8, width)
    slabs = jnp.pad(slabs, ((0, 2 * heads * SHARE - slabs.shape[0]), (0, 0), (0, 0)))
    return lax.dynamic_slice_in_dim(slabs, (2 * lax.axis_index("head") + core) * SHARE, SHARE, 0)


def assemble_kernel(core_ref, own_ref, other_ref, mats_ref, sems):
    core = core_ref[0]
    thirds = mats_ref.shape[2]

    def copies(flag):
        made = []
        for k in range(mats_ref.shape[0] * thirds):
            mat, third = k // thirds, k % thirds
            head, side, slot = k // (2 * SHARE), k // SHARE % 2, k % SHARE
            source = own_ref if side == flag else other_ref
            place = (2 - mat if flag and mat < 3 else mat)
            made.append(
                pltpu.make_async_copy(source.at[head, :, slot], mats_ref.at[place, :, third], sems.at[k])
            )
        return made

    for flag in range(2):

        @pl.when(core == flag)
        def _():
            made = copies(flag)
            for copy in made:
                copy.start()
            for copy in made:
                copy.wait()


def assembled(own, other, core, mats):
    _, blocks, _, eight, width = own.shape
    thirds = width // (blocks * eight)
    out = pl.pallas_call(
        assemble_kernel,
        out_shape=jax.ShapeDtypeStruct((mats, blocks, thirds, eight, width), own.dtype),
        in_specs=[
            pl.BlockSpec(memory_space=pltpu.SMEM),
            pl.BlockSpec(memory_space=pl.ANY),
            pl.BlockSpec(memory_space=pl.ANY),
        ],
        out_specs=pl.BlockSpec(memory_space=pltpu.VMEM),
        scratch_shapes=[pltpu.SemaphoreType.DMA((mats * thirds,))],
        cost_estimate=pl.CostEstimate(flops=0, bytes_accessed=4 * own.size * 2, transcendentals=0),
        name="assemble",
    )(core[None], own, other)
    return out.reshape(mats, blocks * thirds * eight, width)


def dot(a, b):
    return jnp.dot(a, b, preferred_element_type=F32)


def dot_t(a, b):
    return jnp.einsum("pd,cd->pc", a, b, preferred_element_type=F32)


def shards(top, grad_heads, tap_weight_grid, out_w, mix_w, rc_perm):
    half = top.shape[3] // 2
    rows = top.shape[2] // 2
    ranks, heads = 4, lax.axis_size("head")
    lines = lax.axis_size("seq") // (2 * ranks)
    core = lax.axis_index("seq") % 2
    outer, inner = core * rows, (1 - core) * rows

    def cut(array, start):
        return lax.dynamic_slice_in_dim(array, start, rows, 0)

    top = top[0, 0]
    a_out, b_out = cut(top, outer)[:, :half], cut(top, outer)[:, half:]
    a_in, b_in = cut(top, inner)[:, :half], cut(top, inner)[:, half:]
    ao_out = mirrored(a_out)
    ao_in = mirrored(a_in)
    cotan = lax.all_to_all(grad_heads, "head", split_axis=0, concat_axis=0, tiled=True)[:, 0]
    cotan = cotan.transpose(1, 0, 2).reshape(2 * rows, 2 * half)
    ga_out, gb_out = cut(cotan, outer)[:, :half], cut(cotan, outer)[:, half:]
    ga_in, gb_in = cut(cotan, inner)[:, :half], cut(cotan, inner)[:, half:]
    go_out = mirrored(gb_out)
    go_in = mirrored(gb_in)

    piece = piece_of(tap_weight_grid, out_w, mix_w, core)
    along = [[(y * lines + z) * 2 + c for z in range(lines)] for y in range(ranks) for c in range(2)]
    line = spread(piece, "seq", along)
    plane = [
        [h * 2 * lines * ranks + (y * lines + z) * 2 + c for h in range(heads) for y in range(ranks)]
        for z in range(lines)
        for c in range(2)
    ]
    part = spread(line, ("head", "seq"), plane)
    part = part.reshape(heads, ranks * lines, *part.shape[2:])
    partner = pairwise(part, 0)
    mats = assembled(part, partner, core, 5)
    first, middle, last, out_full, mix_full = (mats[k] for k in range(5))
    onehot = (lax.broadcasted_iota(jnp.int32, (half, half), 0) == rc_perm[None, :]).astype(BF16)
    turned = dot(onehot, mix_full).astype(BF16)

    def restore_b(b, a, ao):
        return (b.astype(F32) - (dot(a, mix_full) + dot(ao, turned))).astype(BF16)

    sb_out = restore_b(b_out, a_out, ao_out)
    ext = pairwise(sb_out, 1)
    sb_in = restore_b(b_in, a_in, ao_in)
    across = pairwise(sb_in, 0)
    pre_out = dot(ext, first) + dot(sb_out, middle) + dot(sb_in, last)
    pre_in = dot(sb_out, first) + dot(sb_in, middle) + dot(across, last)

    def branch(pre, a):
        value, slope = jax.vjp(jax.nn.gelu, pre)
        ia = (a.astype(F32) - dot(value.astype(BF16), out_full)).astype(BF16)
        return ia, slope(jnp.ones_like(pre))[0]

    ia_out, slope_out = branch(pre_out, a_out)
    ia_in, slope_in = branch(pre_in, a_in)

    def pull(ga, gb, go, slope):
        cot = (ga.astype(F32) + dot_t(gb, mix_full) + dot_t(go, turned)).astype(BF16)
        return cot, (dot_t(cot, out_full) * slope).astype(BF16)

    ca_out, cp_out = pull(ga_out, gb_out, go_out, slope_out)
    cext = pairwise(cp_out, 1)
    ca_in, cp_in = pull(ga_in, gb_in, go_in, slope_in)
    cacross = pairwise(cp_in, 0)
    cb_out = (
        gb_out.astype(F32) + dot_t(cp_in, first) + dot_t(cp_out, middle) + dot_t(cext, last)
    ).astype(BF16)
    cb_in = (
        gb_in.astype(F32) + dot_t(cacross, first) + dot_t(cp_in, middle) + dot_t(cp_out, last)
    ).astype(BF16)

    def placed(a_o, b_o, a_i, b_i):
        o, i = jnp.concatenate([a_o, b_o], 1), jnp.concatenate([a_i, b_i], 1)
        return jnp.where(core == 0, jnp.concatenate([o, i], 0), jnp.concatenate([i, o], 0))[None, None]

    return placed(ia_out, sb_out, ia_in, sb_in), placed(ca_out, cb_out, ca_in, cb_in)


def solution(mesh):
    placed = (
        P("head", "strand", "seq", None),
        P(None, "strand", "seq", "head"),
        P(None, "seq", None),
        P("seq", None),
        P("seq", None),
        P(),
    )
    return jax.shard_map(
        shards,
        mesh=mesh,
        in_specs=placed,
        out_specs=(P("head", "strand", "seq", None), P("head", "strand", "seq", None)),
        check_vma=False,
    )
```

time: 259 us -> 193 us (0.75)
  the two profiles are of different devices: /device:TPU:107 before, /device:TPU:11 now
where the time goes in v1:
time: 193 us
  starting transfers between devices  91 us (47%)
  blocking collectives  62.8 us (33%)
  matrix products  15.6 us (8%)
  local copies, waits for them, and re-layouts  7.34 us (4%)
  Pallas kernels  5.36 us (3%)
  waiting for transfers between devices  5.19 us (3%)
  other arithmetic  4.15 us (2%)
    all_to_all x2, blocking collectives, spread(): lax.all_to_all(sent, axes, 0, 0, axis_index_groups=groups, tiled=True)  62.8 us
    ppermute x6, starting transfers between devices, pairwise(): return lax.ppermute(value, 'seq', pairs)  57.4 us
    ppermute x4, starting transfers between devices, mirrored(): return lax.ppermute(value, 'strand', [(0, 1), (1, 0)])  28 us
    dot_general x12, matrix products, dot_t(): return jnp.einsum('pd,cd->pc', a, b, preferred_element_type=F32)  8.48 us
    dot_general x13, matrix products, dot(): return jnp.dot(a, b, preferred_element_type=F32)  7.17 us
    all_to_all x1, starting transfers between devices, shards(): lax.all_to_all(grad_heads, 'head', split_axis=0, concat_axis=0, tiled=True)  5.64 us
    pallas_call x1, Pallas kernels, assembled(): pl.pallas_call(assemble_kernel, out_shape=jax.ShapeDtypeStruct((mats, blo...  5.36 us
    ppermute x4, waiting for transfers between devices, mirrored(): return lax.ppermute(value, 'strand', [(0, 1), (1, 0)])  4.24 us
  transfers between devices with their start and end apart: 11, of which 2 were waited for; matrix products, arithmetic and copies ran while one was open for 12% of the time, Pallas kernels for 3%

profile of v1, /device:TPU:11, one launch (start us, length us, event | category | flops | bytes accessed | tf_op | source)
XLA Modules:
  0.0 192.6 jit_solution(18135535288375314771)
XLA Ops:
  0.6 0.9 pad_maximum_fusion.1
  1.6 2.6 %collective-permute-start = (bf16[5,12,768]{2,1,0:T(8,128)(2,1)S(1)}, bf16[5,12,768]{2,1,0:T(8,128)(2,1)S(1)}, u32[]{:S(2)}, u32[]{:S(2)}) collective-permute-start(bf16[5,12,768]{2,1,0:T(8,128)(2,1)S(1)} %pad_maximum_fusion.1), channel_id=1, source_target_pairs={{0,8},{8,0},{16,24},{24,16},{32,40},{40,32},{48,56},{56,48},{64,72... | collective-permute-start | bytes 276488 | tf_op jit(solution)/shard_map/ppermute | solution.py:18
  4.2 0.9 collective-permute-done
  5.1 0.9 broadcast_select_fusion.1
  6.1 0.1 pad_maximum_fusion
  6.2 23.3 %all_to_all.15 = bf16[8,2,8,768]{3,2,1,0:T(8,128)(2,1)S(1)} all-to-all(bf16[8,2,8,768]{3,2,1,0:T(8,128)(2,1)S(1)} %broadcast_in_dim.13), channel_id=1, replica_groups={{0,16,32,48,64,80,96,112},{8,24,40,56,72,88,104,120},{128,144,160,176,1..., dimensions={0} | all-to-all | bytes 393216 | tf_op jit(solution)/shard_map/all_to_all | solution.py:28
  29.5 0.3 broadcast_in_dim.28
  29.8 39.5 %all_to_all.16 = bf16[16,8,2,8,768]{4,3,2,1,0:T(8,128)(2,1)S(1)} all-to-all(bf16[16,8,2,8,768]{4,3,2,1,0:T(8,128)(2,1)S(1)} %broadcast_in_dim.28), channel_id=1, replica_groups={{0,128,256,384,1,129,257,385,2,130,258,386,3,131,259,387},{8,136,264,39..., dimensions={0} | all-to-all | bytes 6291456 | tf_op jit(solution)/shard_map/all_to_all | solution.py:28
  69.3 7.0 %collective-permute-start.1 = (bf16[4,32,2,8,768]{4,3,2,1,0:T(8,128)(2,1)S(1)}, bf16[4,32,2,8,768]{4,3,2,1,0:T(8,128)(2,1)}, u32[]{:S(2)}, u32[]{:S(2)}) collective-permute-start(bf16[4,32,2,8,768]{4,3,2,1,0:T(8,128)(2,1)S(1)} %bitcast.89), channel_id=1, source_target_pairs={{0,8},{8,0},{16,24},{24,16},{32,40},{40,32},{48,56},{56,48},{64,72... | collective-permute-start | bytes 9437192 | tf_op jit(solution)/shard_map/ppermute | solution.py:18
  76.3 5.6 %all-to-all-start.2 = ((bf16[4,1,256,384]{3,2,1,0:T(8,128)(2,1)}), bf16[4,1,256,384]{3,2,1,0:T(8,128)(2,1)}, u32[]{:S(2)}, u32[]{:S(2)}) async-start(bf16[4,1,256,384]{3,2,1,0:T(8,128)(2,1)} %param.7), calls=%async_computation.2 | async-start | bytes 1572864 | tf_op jit(solution)/shard_map/all_to_all | solution.py:113
  81.9 1.2 dynamic-slice_bitcast_fusion.1
  83.1 0.0 copy-start.3
  83.1 0.8 slice.57
  83.9 7.9 %collective-permute-start.2 = (bf16[128,768]{1,0:T(8,128)(2,1)}, bf16[128,768]{1,0:T(8,128)(2,1)}, u32[]{:S(2)}, u32[]{:S(2)}) collective-permute-start(bf16[128,768]{1,0:T(8,128)(2,1)} %slice.57), channel_id=1, source_target_pairs={{0,4},{4,0},{1,5},{5,1},{2,6},{6,2},{3,7},{7,3},{8,12},{12,8},{9,1... | collective-permute-start | bytes 589832 | tf_op jit(solution)/shard_map/ppermute | solution.py:22
  91.8 0.7 slice.63
  92.5 6.0 %collective-permute-start.4 = (bf16[128,768]{1,0:T(8,128)(2,1)}, bf16[128,768]{1,0:T(8,128)(2,1)}, u32[]{:S(2)}, u32[]{:S(2)}) collective-permute-start(bf16[128,768]{1,0:T(8,128)(2,1)} %slice.63), channel_id=1, source_target_pairs={{0,4},{4,0},{1,5},{5,1},{2,6},{6,2},{3,7},{7,3},{8,12},{12,8},{9,1... | collective-permute-start | bytes 589832 | tf_op jit(solution)/shard_map/ppermute | solution.py:22
  98.6 0.0 all-to-all-done.2
  98.6 1.2 copy.9
  99.8 0.0 copy-start.1
  99.9 7.9 %collective-permute-start.6 = (bf16[128,768]{1,0:T(8,128)(2,1)S(1)}, bf16[128,768]{1,0:T(8,128)(2,1)}, u32[]{:S(2)}, u32[]{:S(2)}) collective-permute-start(bf16[128,768]{1,0:T(8,128)(2,1)S(1)} %get-tuple-element.8), channel_id=1, source_target_pairs={{0,4},{4,0},{1,5},{5,1},{2,6},{6,2},{3,7},{7,3},{8,12},{12,8},{9,1... | collective-permute-start | bytes 589832 | tf_op jit(solution)/shard_map/ppermute | solution.py:22
  107.8 6.1 %collective-permute-start.7 = (bf16[128,768]{1,0:T(8,128)(2,1)S(1)}, bf16[128,768]{1,0:T(8,128)(2,1)}, u32[]{:S(2)}, u32[]{:S(2)}) collective-permute-start(bf16[128,768]{1,0:T(8,128)(2,1)S(1)} %get-tuple-element.7), channel_id=1, source_target_pairs={{0,4},{4,0},{1,5},{5,1},{2,6},{6,2},{3,7},{7,3},{8,12},{12,8},{9,1... | collective-permute-start | bytes 589832 | tf_op jit(solution)/shard_map/ppermute | solution.py:22
  113.9 0.0 collective-permute-done.1.other_ref
  113.9 5.4 %assemble.1 = bf16[5,32,3,8,768]{4,3,2,1,0:T(8,128)(2,1)} custom-call(s32[1]{0:T(128)} %bitcast.1.core_ref, bf16[4,32,2,8,768]{4,3,2,1,0:T(8,128)(2,1)} %bitcast.90, bf16[4,32,2,8,768]{4,3,2,1,0:T(8,128)(2,1)} %collective-permute-done.1.other_ref), custom_call_target="tpu_custom_call" | custom-call | bytes 12582912 | tf_op jit(solution)/shard_map/assemble/pallas_call | solution.py:73
  119.3 0.0 copy-start.7
  119.3 3.1 %fusion.53 = (bf16[1,32,3,8,768]{4,3,2,1,0:T(8,128)(2,1)S(1)}, bf16[1,32,3,8,768]{4,3,2,1,0:T(8,128)(2,1)S(1)}, bf16[1,32,3,8,768]{4,3,2,1,0:T(8,128)(2,1)S(1)},...) fusion(bf16[5,32,3,8,768]{4,3,2,1,0:T(8,128)(2,1)} %assemble.1), kind=kLoop, calls=%fused_computation.85 | loop fusion | bytes 11796480 | tf_op jit(solution)/shard_map/slice | solution.py:132
  122.4 1.2 fusion.1
  123.5 0.0 copy-start.2
  123.6 4.2 %collective-permute-done.6 = bf16[128,768]{1,0:T(8,128)(2,1)} collective-permute-done((bf16[128,768]{1,0:T(8,128)(2,1)S(1)}, bf16[128,768]{1,0:T(8,128)(2,1)}, u32[]{:S(2)}, u32[]{:S(2)}) %collective-permute-start.6) | collective-permute-done | bytes 196640 | tf_op jit(solution)/shard_map/ppermute | solution.py:22
  127.8 1.5 fusion.61
  129.3 0.6 fusion.14
  129.8 0.0 collective-permute-done.2
  129.8 1.3 fusion.55
  131.2 0.3 fusion.16
  131.5 9.3 %collective-permute-start.3 = (bf16[128,768]{1,0:T(8,128)(2,1)S(1)}, bf16[128,768]{1,0:T(8,128)(2,1)S(1)}, u32[]{:S(2)}, u32[]{:S(2)}) collective-permute-start(bf16[128,768]{1,0:T(8,128)(2,1)S(1)} %fusion.16), channel_id=1, source_target_pairs={{8,16},{24,32},{40,48},{56,64},{72,80},{88,96},{104,112},{120,128}... | collective-permute-start | bytes 589832 | tf_op jit(solution)/shard_map/ppermute | solution.py:18
  140.8 0.3 fusion.56
  141.1 0.0 copy-start.4
  141.1 1.3 fusion.57
  142.4 0.3 fusion.15
  142.8 23.9 %collective-permute-start.5 = (bf16[128,768]{1,0:T(8,128)(2,1)S(1)}, bf16[128,768]{1,0:T(8,128)(2,1)S(1)}, u32[]{:S(2)}, u32[]{:S(2)}) collective-permute-start(bf16[128,768]{1,0:T(8,128)(2,1)S(1)} %fusion.15), channel_id=1, source_target_pairs={{0,8},{8,0},{16,24},{24,16},{32,40},{40,32},{48,56},{56,48},{64,72... | collective-permute-start | bytes 589832 | tf_op jit(solution)/shard_map/ppermute | solution.py:18
  166.7 0.3 fusion.59
  167.0 1.5 fusion.62
  168.5 0.6 fusion.13
  169.0 0.3 fusion.58
  169.4 0.0 collective-permute-done.3
  169.4 0.3 fusion.3
  169.7 0.6 fusion.22
  170.3 1.9 collective-permute-start.8
  172.2 0.5 fusion.63
  172.8 0.0 collective-permute-done.5
  172.8 0.3 fusion.60
  173.1 0.3 fusion.5
  173.5 0.6 fusion.21
  174.0 0.5 fusion.65
  174.6 12.8 %collective-permute-start.9 = (bf16[128,768]{1,0:T(8,128)(2,1)S(1)}, bf16[128,768]{1,0:T(8,128)(2,1)S(1)}, u32[]{:S(2)}, u32[]{:S(2)}) collective-permute-start(bf16[128,768]{1,0:T(8,128)(2,1)S(1)} %fusion.21), channel_id=1, source_target_pairs={{0,8},{8,0},{16,24},{24,16},{32,40},{40,32},{48,56},{56,48},{64,72... | collective-permute-start | bytes 589832 | tf_op jit(solution)/shard_map/ppermute | solution.py:18
  187.4 0.5 fusion.66
  187.9 0.4 fusion.19
  188.3 0.4 fusion.20
  188.8 1.0 maximum_select_fusion
  189.8 0.0 collective-permute-done.8
  189.8 0.5 fusion.64
  190.3 0.6 fusion.18
  191.0 0.0 collective-permute-done.9
  191.0 0.6 fusion.17
  191.6 1.0 maximum_select_fusion.1
  (20 shorter events, 0.2 us)
Async XLA Ops:
  1.6 3.5 %collective-permute-start = (bf16[5,12,768]{2,1,0:T(8,128)(2,1)S(1)}, bf16[5,12,768]{2,1,0:T(8,128)(2,1)S(1)}, u32[]{:S(2)}, u32[]{:S(2)}) collective-permute-start(bf16[5,12,768]{2,1,0:T(8,128)(2,1)S(1)} %pad_maximum_fusion.1), channel_id=1, source_target_pairs={{0,8},{8,0},{16,24},{24,16},{32,40},{40,32},{48,56},{56,48},{64,72... | collective-permute-start | bytes 276488 | tf_op jit(solution)/shard_map/ppermute | solution.py:18
  69.3 13.8 %copy-start = (bf16[16,8,2,8,768]{4,3,2,1,0:T(8,128)(2,1)}, bf16[16,8,2,8,768]{4,3,2,1,0:T(8,128)(2,1)S(1)}, u32[]{:S(2)}) copy-start(bf16[16,8,2,8,768]{4,3,2,1,0:T(8,128)(2,1)S(1)} %all_to_all.16) | copy-start | bytes 9437188
  69.3 44.6 %collective-permute-start.1 = (bf16[4,32,2,8,768]{4,3,2,1,0:T(8,128)(2,1)S(1)}, bf16[4,32,2,8,768]{4,3,2,1,0:T(8,128)(2,1)}, u32[]{:S(2)}, u32[]{:S(2)}) collective-permute-start(bf16[4,32,2,8,768]{4,3,2,1,0:T(8,128)(2,1)S(1)} %bitcast.89), channel_id=1, source_target_pairs={{0,8},{8,0},{16,24},{24,16},{32,40},{40,32},{48,56},{56,48},{64,72... | collective-permute-start | bytes 9437192 | tf_op jit(solution)/shard_map/ppermute | solution.py:18
  76.3 22.3 %all-to-all-start.2 = ((bf16[4,1,256,384]{3,2,1,0:T(8,128)(2,1)}), bf16[4,1,256,384]{3,2,1,0:T(8,128)(2,1)}, u32[]{:S(2)}, u32[]{:S(2)}) async-start(bf16[4,1,256,384]{3,2,1,0:T(8,128)(2,1)} %param.7), calls=%async_computation.2 | async-start | bytes 1572864 | tf_op jit(solution)/shard_map/all_to_all | solution.py:113
  83.1 8.7 %copy-start.3 = (bf16[128,1536]{1,0:T(8,128)(2,1)}, bf16[128,1536]{1,0:T(8,128)(2,1)S(1)}, u32[]{:S(2)}) copy-start(bf16[128,1536]{1,0:T(8,128)(2,1)S(1)} %get-tuple-element.10) | copy-start | bytes 1179652
  83.1 9.4 %copy-start.5 = (bf16[128,1536]{1,0:T(8,128)(2,1)}, bf16[128,1536]{1,0:T(8,128)(2,1)S(1)}, u32[]{:S(2)}) copy-start(bf16[128,1536]{1,0:T(8,128)(2,1)S(1)} %get-tuple-element.9) | copy-start | bytes 1179652
  83.9 46.0 %collective-permute-start.2 = (bf16[128,768]{1,0:T(8,128)(2,1)}, bf16[128,768]{1,0:T(8,128)(2,1)}, u32[]{:S(2)}, u32[]{:S(2)}) collective-permute-start(bf16[128,768]{1,0:T(8,128)(2,1)} %slice.57), channel_id=1, source_target_pairs={{0,4},{4,0},{1,5},{5,1},{2,6},{6,2},{3,7},{7,3},{8,12},{12,8},{9,1... | collective-permute-start | bytes 589832 | tf_op jit(solution)/shard_map/ppermute | solution.py:22
  92.5 48.6 %collective-permute-start.4 = (bf16[128,768]{1,0:T(8,128)(2,1)}, bf16[128,768]{1,0:T(8,128)(2,1)}, u32[]{:S(2)}, u32[]{:S(2)}) collective-permute-start(bf16[128,768]{1,0:T(8,128)(2,1)} %slice.63), channel_id=1, source_target_pairs={{0,4},{4,0},{1,5},{5,1},{2,6},{6,2},{3,7},{7,3},{8,12},{12,8},{9,1... | collective-permute-start | bytes 589832 | tf_op jit(solution)/shard_map/ppermute | solution.py:22
  99.8 14.1 %copy-start.1 = (bf16[4,32,8,384]{3,2,0,1:T(8,128)(2,1)}, bf16[4,32,8,384]{3,2,0,1:T(8,128)(2,1)S(1)}, u32[]{:S(2)}) copy-start(bf16[4,32,8,384]{3,2,0,1:T(8,128)(2,1)S(1)} %copy.9) | copy-start | bytes 2359300
  99.9 27.9 %collective-permute-start.6 = (bf16[128,768]{1,0:T(8,128)(2,1)S(1)}, bf16[128,768]{1,0:T(8,128)(2,1)}, u32[]{:S(2)}, u32[]{:S(2)}) collective-permute-start(bf16[128,768]{1,0:T(8,128)(2,1)S(1)} %get-tuple-element.8), channel_id=1, source_target_pairs={{0,4},{4,0},{1,5},{5,1},{2,6},{6,2},{3,7},{7,3},{8,12},{12,8},{9,1... | collective-permute-start | bytes 589832 | tf_op jit(solution)/shard_map/ppermute | solution.py:22
  107.8 59.2 %collective-permute-start.7 = (bf16[128,768]{1,0:T(8,128)(2,1)S(1)}, bf16[128,768]{1,0:T(8,128)(2,1)}, u32[]{:S(2)}, u32[]{:S(2)}) collective-permute-start(bf16[128,768]{1,0:T(8,128)(2,1)S(1)} %get-tuple-element.7), channel_id=1, source_target_pairs={{0,4},{4,0},{1,5},{5,1},{2,6},{6,2},{3,7},{7,3},{8,12},{12,8},{9,1... | collective-permute-start | bytes 589832 | tf_op jit(solution)/shard_map/ppermute | solution.py:22
  119.3 3.1 %copy-start.7 = (s32[768]{0:T(1024)S(1)}, s32[768]{0:T(1024)}, u32[]{:S(2)}) copy-start(s32[768]{0:T(1024)} %param.11) | copy-start | bytes 9220
  123.5 5.7 %copy-start.2 = (bf16[4,32,8,384]{3,2,0,1:T(8,128)(2,1)S(1)}, bf16[4,32,8,384]{3,2,0,1:T(8,128)(2,1)}, u32[]{:S(2)}) copy-start(bf16[4,32,8,384]{3,2,0,1:T(8,128)(2,1)} %copy-done.1) | copy-start | bytes 2359300
  129.8 1.3 copy-start.6
  131.5 37.9 %collective-permute-start.3 = (bf16[128,768]{1,0:T(8,128)(2,1)S(1)}, bf16[128,768]{1,0:T(8,128)(2,1)S(1)}, u32[]{:S(2)}, u32[]{:S(2)}) collective-permute-start(bf16[128,768]{1,0:T(8,128)(2,1)S(1)} %fusion.16), channel_id=1, source_target_pairs={{8,16},{24,32},{40,48},{56,64},{72,80},{88,96},{104,112},{120,128}... | collective-permute-start | bytes 589832 | tf_op jit(solution)/shard_map/ppermute | solution.py:18
  141.1 1.3 copy-start.4
  142.8 30.0 %collective-permute-start.5 = (bf16[128,768]{1,0:T(8,128)(2,1)S(1)}, bf16[128,768]{1,0:T(8,128)(2,1)S(1)}, u32[]{:S(2)}, u32[]{:S(2)}) collective-permute-start(bf16[128,768]{1,0:T(8,128)(2,1)S(1)} %fusion.15), channel_id=1, source_target_pairs={{0,8},{8,0},{16,24},{24,16},{32,40},{40,32},{48,56},{56,48},{64,72... | collective-permute-start | bytes 589832 | tf_op jit(solution)/shard_map/ppermute | solution.py:18
  170.3 19.5 %collective-permute-start.8 = (bf16[128,768]{1,0:T(8,128)(2,1)S(1)}, bf16[128,768]{1,0:T(8,128)(2,1)S(1)}, u32[]{:S(2)}, u32[]{:S(2)}) collective-permute-start(bf16[128,768]{1,0:T(8,128)(2,1)S(1)} %fusion.22), channel_id=1, source_target_pairs={{8,16},{24,32},{40,48},{56,64},{72,80},{88,96},{104,112},{120,128}... | collective-permute-start | bytes 589832 | tf_op jit(solution)/shard_map/ppermute | solution.py:18
  174.6 16.4 %collective-permute-start.9 = (bf16[128,768]{1,0:T(8,128)(2,1)S(1)}, bf16[128,768]{1,0:T(8,128)(2,1)S(1)}, u32[]{:S(2)}, u32[]{:S(2)}) collective-permute-start(bf16[128,768]{1,0:T(8,128)(2,1)S(1)} %fusion.21), channel_id=1, source_target_pairs={{0,8},{8,0},{16,24},{24,16},{32,40},{40,32},{48,56},{56,48},{64,72... | collective-permute-start | bytes 589832 | tf_op jit(solution)/shard_map/ppermute | solution.py:18

commit v2 on v0

v2 whole, which is shorter than its diff:
```python
import functools

import jax
import jax.numpy as jnp
from jax import lax
from jax.experimental import pallas as pl
from jax.experimental.pallas import tpu as pltpu
from jax.sharding import PartitionSpec as P

BF16, F32 = jnp.bfloat16, jnp.float32
LANES = 128


def pairwise(value, bit):
    count = lax.axis_size("seq")
    if bit == 0:
        pairs = [(i, i ^ 1) for i in range(count)]
    else:
        pairs = [(i, i + 1) for i in range(1, count - 1, 2)] + [(i + 1, i) for i in range(1, count - 1, 2)]
    return lax.ppermute(value, "seq", pairs)


def mirrored(value):
    return lax.ppermute(value, "strand", [(0, 1), (1, 0)])


def dot(a, b):
    return lax.dot_general(a, b, (((1,), (0,)), ((), ())), preferred_element_type=F32)


def dot_t(a, b):
    return lax.dot_general(a, b, (((1,), (1,)), ((), ())), preferred_element_type=F32)


def at(start, size):
    return pl.ds(pl.multiple_of(start, LANES), size)


def call(kernel, place, ins, outs, flops, scratch=(), limit=24):
    moved = sum(a.size * a.dtype.itemsize for a in ins) + sum(
        o.size * jnp.dtype(o.dtype).itemsize for o in outs
    )
    return pl.pallas_call(
        kernel,
        out_shape=outs,
        in_specs=[pl.BlockSpec(memory_space=pltpu.SMEM)]
        + [pl.BlockSpec(memory_space=pltpu.VMEM)] * len(ins),
        out_specs=[pl.BlockSpec(memory_space=pltpu.VMEM)] * len(outs),
        scratch_shapes=list(scratch),
        compiler_params=pltpu.CompilerParams(vmem_limit_bytes=limit << 20),
        cost_estimate=pl.CostEstimate(flops=flops, bytes_accessed=moved, transcendentals=0),
    )(place, *ins)


def shape(dims, kind):
    return jax.ShapeDtypeStruct(dims, kind)


def split(place, taps, out, mix, sent):
    head = place[1]
    wide = sent.shape[3] - LANES
    carried = jnp.where(head == 3, out[...], taps[jnp.minimum(head, 2)])
    for c in range(2):
        column = (2 * jnp.minimum(head, 2) + c) * LANES
        sent[0, c, :, :wide] = carried[:, c * wide : (c + 1) * wide]
        sent[0, c, :, wide:] = mix[:, at(column, LANES)]
    for k in range(1, sent.shape[0]):
        sent[k] = sent[0]


def repack(place, line, sent):
    deep = line.shape[1]
    for z in range(sent.shape[1]):
        sent[0, z, :deep, :] = line[2 * z]
        sent[0, z, deep:, :] = line[2 * z + 1]
    for k in range(1, sent.shape[0]):
        sent[k] = sent[0]


def turn(core, perm, grads, own, other, mix, turned, base):
    c = core[0]
    side = mix.shape[0]
    wide = grads.shape[2]
    hot = (lax.broadcasted_iota(jnp.int32, (side, side), 0) == perm[...]).astype(BF16)
    for k in range(side // (2 * LANES)):
        for place, source in ((c, own), (1 - c, other)):
            column = at((2 * k + place) * LANES, LANES)
            block = source[k, :, wide:]
            mix[:, column] = block
            turned[:, column] = dot(hot, block).astype(BF16)
    head = core[1]
    backed = dot_t(grads[head ^ 2], mix[:, :wide]) + dot_t(grads[head ^ 3], mix[:, wide:])
    for k in range(2):
        lane = slice(k * wide, (k + 1) * wide)
        base[:, lane] = grads[head ^ k].astype(F32) + backed[:, lane]


def restore(core, top, mirror, mix, turned, edge, inner):
    c = core[0]
    rows, half = edge.shape
    for result, place in ((edge, c), (inner, 1 - c)):
        line = at(place * rows, rows)
        mixing = dot(top[line, :half], mix[...]) + dot(mirror[line, :], turned[...])
        result[...] = (top[line, half:].astype(F32) - mixing).astype(BF16)


def branch(core, top, beyond, edge, inner, across, own, other, restored, slope, out, near):
    c = core[0]
    rows, half = edge.shape
    before = jnp.concatenate([beyond[...], edge[...]], axis=0)
    here = jnp.concatenate([edge[...], inner[...]], axis=0)
    after = jnp.concatenate([inner[...], across[...]], axis=0)
    wide = half // 2
    lines = (at(c * rows, rows), at((1 - c) * rows, rows))
    hidden = []
    root = 0.7978845608028654
    for place, taps in ((c, own), (1 - c, other)):
        lane = at(place * wide, wide)
        pre = dot(before, taps[2 * c, :, :wide]) + dot(here, taps[1, :, :wide]) + dot(after, taps[2 - 2 * c, :, :wide])
        squared = pre * pre
        bent = jnp.tanh(root * (pre + 0.044715 * (pre * squared)))
        share = 0.5 * (1.0 + bent)
        gain = share + pre * (0.5 * (1.0 - bent * bent)) * (root * (1.0 + 3.0 * 0.044715 * squared))
        hidden.append((pre * share).astype(BF16))
        for k in range(2):
            slope[k, :, lane] = gain[k * rows : (k + 1) * rows]
        out[:, lane] = taps[3, :, :wide]
        near[:, lane] = taps[2 * c, :, :wide]
    for place in (c, 1 - c):
        lane = at(place * wide, wide)
        made = dot(hidden[0], out[at(c * wide, wide), lane]) + dot(
            hidden[1], out[at((1 - c) * wide, wide), lane]
        )
        for k, line in enumerate(lines):
            restored[line, lane] = (
                top[line, lane].astype(F32) - made[k * rows : (k + 1) * rows]
            ).astype(BF16)
    restored[lines[0], half:] = edge[...]
    restored[lines[1], half:] = inner[...]


def pull(which, core, mirror, turned, base, slope, out, cot, held):
    c = core[0]
    rows = cot.shape[0]
    line = at((c if which == 0 else 1 - c) * rows, rows)
    wide = mirror.shape[2]
    odd = core[1] & 1
    total = base[line, :]
    for k in range(mirror.shape[0]):
        total += dot_t(mirror[k ^ odd], turned[:, k * wide : (k + 1) * wide])
    rounded = total.astype(BF16)
    cot[...] = rounded
    held[...] = (dot_t(rounded, out[...]) * slope[which]).astype(BF16)


def gather(core, grads, beyond, edge, inner, own, other, result, rest):
    c = core[0]
    rows, half = edge.shape
    wide = half // 2
    head = core[1]
    total = jnp.zeros((2 * rows, half), F32)
    low = jnp.zeros((rows, half), F32)
    for place, taps in ((c, own), (1 - c, other)):
        lane = at(place * wide, wide)
        e, i = edge[:, lane], inner[:, lane]
        total += dot_t(jnp.concatenate([e, i], axis=0), taps[1, :, :wide])
        total += dot_t(jnp.concatenate([beyond[:, lane], e], axis=0), taps[2 - 2 * c, :, :wide])
        low += dot_t(i, taps[2 * c, :, :wide])
    lines = (at(c * rows, rows), at((1 - c) * rows, rows))
    plain = [
        jnp.concatenate([grads[head ^ 2, line, :], grads[head ^ 3, line, :]], axis=1).astype(F32)
        for line in lines
    ]
    result[...] = (plain[0] + total[:rows] + low).astype(BF16)
    rest[...] = plain[1] + total[rows:]


def finish(core, across, near, edge_a, inner_a, edge_b, rest, result):
    c = core[0]
    rows, half = edge_a.shape
    first, second = at(c * rows, rows), at((1 - c) * rows, rows)
    result[first, :half] = edge_a[...]
    result[second, :half] = inner_a[...]
    result[first, half:] = edge_b[...]
    result[second, half:] = (rest[...] + dot_t(across[...], near[...])).astype(BF16)


def shards(top, grad_heads, tap_weight_grid, out_w, mix_w, rc_perm):
    half = top.shape[3] // 2
    rows = top.shape[2] // 2
    heads = lax.axis_size("head")
    ranks = 4
    lines = lax.axis_size("seq") // (2 * ranks)
    core = lax.axis_index("seq") % 2
    head = lax.axis_index("head")
    top = top[0, 0]

    place = jnp.stack([core, head]).astype(jnp.int32)
    deep = out_w.shape[0]
    (sent,) = call(
        split,
        place,
        (tap_weight_grid, out_w, mix_w),
        (shape((lines, 2, deep, half // 2 + LANES), BF16),),
        0,
    )
    along = [[(y * lines + z) * 2 + c for z in range(lines) for c in range(2)] for y in range(ranks)]
    line = lax.all_to_all(sent.reshape(2 * lines, *sent.shape[2:]), "seq", 0, 0, axis_index_groups=along, tiled=True)
    ao = mirrored(top[:, :half])
    blocks = [lax.dynamic_index_in_dim(grad_heads[:, 0], head ^ k, 0, False) for k in range(heads)]
    grads = [blocks[0]]
    for k in range(1, heads):
        grads.append(lax.ppermute(blocks[k], "head", [(i, i ^ k) for i in range(heads)]))
    grads = jnp.stack(grads)

    def sent_chunk(start):
        return lax.dynamic_slice(grads, (2 - (head // 2) * 2, start, 0), (2, rows, grads.shape[2]))

    go_edge = mirrored(sent_chunk(core * rows))
    go_inner = mirrored(sent_chunk((1 - core) * rows))
    plane = [
        [h * 2 * lines * ranks + (y * lines + z) * 2 + c for h in range(heads) for y in range(ranks)]
        for z in range(lines)
        for c in range(2)
    ]
    (sent,) = call(
        repack, place, (line,), (shape((heads * ranks, lines, 2 * deep, line.shape[2]), BF16),), 0
    )
    mine = lax.all_to_all(sent, ("head", "seq"), 0, 0, axis_index_groups=plane, tiled=True)
    mine = mine.reshape(heads, half, mine.shape[3])
    theirs = pairwise(mine, 0)

    unit = 2 * rows * half * half
    square, tall, chunk = (half, half), (2 * rows, half), (rows, half)
    mix, turned, base = call(
        turn,
        place,
        (rc_perm[None, :], grads, mine, theirs),
        (shape(square, BF16), shape(square, BF16), shape(tall, F32)),
        8 * unit,
    )
    edge, inner = call(
        restore, place, (top, ao, mix, turned), (shape(chunk, BF16), shape(chunk, BF16)), 4 * unit
    )
    beyond = pairwise(edge, 1)
    across = pairwise(inner, 0)
    restored, slope, out, near = call(
        branch,
        place,
        (top, beyond, edge, inner, across, mine, theirs),
        (shape(top.shape, BF16), shape((2, *chunk), F32), shape(square, BF16), shape(square, BF16)),
        8 * unit,
        limit=32,
    )
    pulls = []
    for which, mirror in ((0, go_edge), (1, go_inner)):
        cot, held = call(
            functools.partial(pull, which),
            place,
            (mirror, turned, base, slope, out),
            (shape(chunk, BF16), shape(chunk, BF16)),
            2 * unit,
        )
        pulls.append((cot, held))
    cot_beyond = pairwise(pulls[0][1], 1)
    cot_across = pairwise(pulls[1][1], 0)
    edge_b, rest = call(
        gather,
        place,
        (grads, cot_beyond, pulls[0][1], pulls[1][1], mine, theirs),
        (shape(chunk, BF16), shape(chunk, F32)),
        5 * unit,
        limit=32,
    )
    (result,) = call(
        finish,
        place,
        (cot_across, near, pulls[0][0], pulls[1][0], edge_b, rest),
        (shape(top.shape, BF16),),
        unit,
    )
    return restored[None, None], result[None, None]


def solution(mesh):
    placed = (
        P("head", "strand", "seq", None),
        P(None, "strand", "seq", "head"),
        P(None, "seq", None),
        P("seq", None),
        P("seq", None),
        P(),
    )
    return jax.shard_map(
        shards,
        mesh=mesh,
        in_specs=placed,
        out_specs=(P("head", "strand", "seq", None), P("head", "strand", "seq", None)),
        check_vma=False,
    )
```

time: 259 us -> 205 us (0.79)
  the two profiles are of different devices: /device:TPU:107 before, /device:TPU:1 now
where the time goes in v2:
time: 205 us
  starting transfers between devices  87.1 us (42%)
  blocking collectives  75.9 us (37%)
  Pallas kernels  20.5 us (10%)
  waiting for transfers between devices  13.3 us (6%)
  local copies, waits for them, and re-layouts  5.39 us (3%)
    ppermute x5, starting transfers between devices, pairwise(): return lax.ppermute(value, 'seq', pairs)  56.2 us
    all_to_all x1, blocking collectives, shards(): lax.all_to_all(sent, ('head', 'seq'), 0, 0, axis_index_groups=plane, tile...  45.1 us
    all_to_all x1, blocking collectives, shards(): lax.all_to_all(sent.reshape(2 * lines, *sent.shape[2:]), 'seq', 0, 0, axi...  30.8 us
    ppermute x3, starting transfers between devices, mirrored(): return lax.ppermute(value, 'strand', [(0, 1), (1, 0)])  21.9 us
    pallas_call x9, Pallas kernels, call(): pl.pallas_call(kernel, out_shape=outs, in_specs=[pl.BlockSpec(memory_spac...  20.5 us
    ppermute x3, waiting for transfers between devices, mirrored(): return lax.ppermute(value, 'strand', [(0, 1), (1, 0)])  12.1 us
    ppermute x3, starting transfers between devices, shards(): lax.ppermute(blocks[k], 'head', [(i, i ^ k) for i in range(heads)])  8.97 us
  transfers between devices with their start and end apart: 11, of which 2 were waited for; matrix products, arithmetic and copies ran while one was open for 2% of the time, Pallas kernels for 8%

profile of v2, /device:TPU:1, one launch (start us, length us, event | category | flops | bytes accessed | tf_op | source)
XLA Modules:
  0.0 204.6 jit_solution(6945686803316819058)
XLA Ops:
  0.6 0.1 pad_add_fusion.place.core
  0.7 0.0 copy-start.2
  0.7 0.9 copy-done.2
  1.6 0.0 copy-start.3
  1.6 0.7 copy-done.3
  2.3 0.0 copy-start.4
  2.3 0.7 copy-done.4
  3.1 0.6 shard_map.77
  3.7 30.8 %all_to_all.10.line = bf16[16,12,512]{2,1,0:T(8,128)(2,1)S(1)} all-to-all(bf16[16,12,512]{2,1,0:T(8,128)(2,1)S(1)} %bitcast.25), channel_id=1, replica_groups={{0,8,16,24,32,40,48,56,64,72,80,88,96,104,112,120},{128,136,144,152,160..., dimensions={0} | all-to-all | bytes 393216 | tf_op jit(solution)/shard_map/all_to_all | solution.py:208
  34.5 0.8 shard_map.78
  35.3 45.1 %all_to_all.11 = bf16[16,8,24,512]{3,2,1,0:T(8,128)(2,1)S(1)} all-to-all(bf16[16,8,24,512]{3,2,1,0:T(8,128)(2,1)S(1)} %shard_map.78), channel_id=1, replica_groups={{0,128,256,384,1,129,257,385,2,130,258,386,3,131,259,387},{8,136,264,39..., dimensions={0} | all-to-all | bytes 6291456 | tf_op jit(solution)/shard_map/all_to_all | solution.py:229
  80.3 1.9 collective-permute-start.4
  82.3 0.0 copy-start
  82.3 0.0 copy-start.5
  82.3 2.2 %dynamic-slice_bitcast_fusion.3 = (bf16[1,256,384]{2,1,0:T(8,128)(2,1)}, bf16[256,384]{1,0:T(8,128)(2,1)}, bf16[256,384]{1,0:T(8,128)(2,1)}, bf16[256,384]{1,0:T(8,128)(2,1)}) fusion(bf16[4,1,256,384]{3,2,1,0:T(8,128)(2,1)} %param.7, s32[]{:T(128)S(6)} %select_n.36, s32[]{:T(128)S(6)} %select_n.37, s32[]{:T(128)S(6)} %select_n.39, s32[]{:T(128)S(6)} %select_n.38), kind=kLoop, calls=%fused_computation.4 | loop fusion | bytes 1572880 | tf_op jit(solution)/shard_map/jit(dynamic_index_in_dim)/dynamic_slice | solution.py:210
  84.5 1.9 collective-permute-start.1
  86.4 3.3 %collective-permute-start.3 = (bf16[256,384]{1,0:T(8,128)(2,1)}, bf16[256,384]{1,0:T(8,128)(2,1)}, u32[]{:S(2)}, u32[]{:S(2)}) collective-permute-start(bf16[256,384]{1,0:T(8,128)(2,1)} %get-tuple-element.36), channel_id=1, source_target_pairs={{0,3},{1,2},{2,1},{3,0},{4,7},{5,6},{6,5},{7,4},{8,11},{9,10},{10,... | collective-permute-start | bytes 589832 | tf_op jit(solution)/shard_map/ppermute | solution.py:213
  89.7 3.8 %collective-permute-start.2 = (bf16[256,384]{1,0:T(8,128)(2,1)}, bf16[256,384]{1,0:T(8,128)(2,1)}, u32[]{:S(2)}, u32[]{:S(2)}) collective-permute-start(bf16[256,384]{1,0:T(8,128)(2,1)} %get-tuple-element.37), channel_id=1, source_target_pairs={{0,2},{1,3},{2,0},{3,1},{4,6},{5,7},{6,4},{7,5},{8,10},{9,11},{10,... | collective-permute-start | bytes 589832 | tf_op jit(solution)/shard_map/ppermute | solution.py:213
  93.5 0.0 copy-done
  93.5 0.8 slice.4
  94.3 7.9 %collective-permute-start = (bf16[256,768]{1,0:T(8,128)(2,1)}, bf16[256,768]{1,0:T(8,128)(2,1)S(1)}, u32[]{:S(2)}, u32[]{:S(2)}) collective-permute-start(bf16[256,768]{1,0:T(8,128)(2,1)} %slice.4), channel_id=1, source_target_pairs={{0,4},{4,0},{1,5},{5,1},{2,6},{6,2},{3,7},{7,3},{8,12},{12,8},{9,1... | collective-permute-start | bytes 1179656 | tf_op jit(solution)/shard_map/ppermute | solution.py:24
  102.2 0.0 copy-done.5
  102.3 0.0 collective-permute-done.1
  102.3 0.0 collective-permute-done.3
  102.3 0.0 collective-permute-done.2
  102.3 1.3 pad_maximum_fusion.grads
  103.6 0.0 copy-start.1
  103.7 0.0 collective-permute-done.4.other
  103.7 4.5 %shard_map.79 = (bf16[768,768]{1,0:T(8,128)(2,1)S(1)}, bf16[768,768]{1,0:T(8,128)(2,1)S(1)}, f32[256,768]{1,0:T(8,128)S(1)}) custom-call(s32[2]{0:T(128)S(1)} %pad_add_fusion.place.core, s32[1,768]{1,0:T(1,128)S(1)} %broadcast_in_dim.9.perm, bf16[4,256,384]{2,1,0:T(8,128)(2,1)S(1)} %pad_maximum_fusion.grads, bf16[4,768,512]{2,1,0:T(8,128)(2,1)S(1)} %bitcast.19, ...), custom_call_target="tpu_custom_call" | custom-call | flops 1207959552 | bytes 10226688 | tf_op jit(solution)/shard_map/pallas_call | solution.py:43
  108.2 12.1 %collective-permute-done.mirror = bf16[256,768]{1,0:T(8,128)(2,1)S(1)} collective-permute-done((bf16[256,768]{1,0:T(8,128)(2,1)}, bf16[256,768]{1,0:T(8,128)(2,1)S(1)}, u32[]{:S(2)}, u32[]{:S(2)}) %collective-permute-start) | collective-permute-done | bytes 393248 | tf_op jit(solution)/shard_map/ppermute | solution.py:24
  120.3 0.0 copy-done.1
  120.3 1.3 shard_map.80
  121.6 9.6 %collective-permute-start.5 = (bf16[128,768]{1,0:T(8,128)(2,1)S(1)}, bf16[128,768]{1,0:T(8,128)(2,1)S(1)}, u32[]{:S(2)}, u32[]{:S(2)}) collective-permute-start(bf16[128,768]{1,0:T(8,128)(2,1)S(1)} %get-tuple-element.19.edge), channel_id=1, source_target_pairs={{8,16},{24,32},{40,48},{56,64},{72,80},{88,96},{104,112},{120,128}... | collective-permute-start | bytes 589832 | tf_op jit(solution)/shard_map/ppermute | solution.py:20
  131.2 1.9 collective-permute-start.6
  133.2 0.1 constant_dynamic-slice_fusion
  133.2 5.9 %collective-permute-start.9 = (bf16[2,128,384]{2,1,0:T(8,128)(2,1)S(1)}, bf16[2,128,384]{2,1,0:T(8,128)(2,1)S(1)}, u32[]{:S(2)}, u32[]{:S(2)}) collective-permute-start(bf16[2,128,384]{2,1,0:T(8,128)(2,1)S(1)} %get-tuple-element.32), channel_id=1, source_target_pairs={{0,4},{4,0},{1,5},{5,1},{2,6},{6,2},{3,7},{7,3},{8,12},{12,8},{9,1... | collective-permute-start | bytes 589832 | tf_op jit(solution)/shard_map/ppermute | solution.py:24
  139.1 8.1 %collective-permute-start.7 = (bf16[2,128,384]{2,1,0:T(8,128)(2,1)S(1)}, bf16[2,128,384]{2,1,0:T(8,128)(2,1)S(1)}, u32[]{:S(2)}, u32[]{:S(2)}) collective-permute-start(bf16[2,128,384]{2,1,0:T(8,128)(2,1)S(1)} %get-tuple-element.33), channel_id=1, source_target_pairs={{0,4},{4,0},{1,5},{5,1},{2,6},{6,2},{3,7},{7,3},{8,12},{12,8},{9,1... | collective-permute-start | bytes 589832 | tf_op jit(solution)/shard_map/ppermute | solution.py:24
  147.2 0.0 collective-permute-done.5.beyond
  147.2 0.0 collective-permute-done.6.across
  147.3 5.1 %shard_map.81 = (bf16[256,1536]{1,0:T(8,128)(2,1)}, f32[2,128,768]{2,1,0:T(8,128)S(1)}, bf16[768,768]{1,0:T(8,128)(2,1)S(1)}, bf16[768,768]{1,0:T(8,128)(2,1)S(1)}) custom-call(s32[2]{0:T(128)S(1)} %pad_add_fusion.place.core, bf16[256,1536]{1,0:T(8,128)(2,1)S(1)} %bitcast.24, bf16[128,768]{1,0:T(8,128)(2,1)S(1)} %collective-permute-done.5.beyond, ...), custom_call_target="tpu_custom_call" | custom-call | flops 1207959552 | bytes 11796480 | tf_op jit(solution)/shard_map/pallas_call | solution.py:43
  152.4 0.0 collective-permute-done.9.mirror
  152.4 1.5 shard_map.83
  153.9 40.8 %collective-permute-start.10 = (bf16[128,768]{1,0:T(8,128)(2,1)S(1)}, bf16[128,768]{1,0:T(8,128)(2,1)S(1)}, u32[]{:S(2)}, u32[]{:S(2)}) collective-permute-start(bf16[128,768]{1,0:T(8,128)(2,1)S(1)} %get-tuple-element.29.edge), channel_id=1, source_target_pairs={{8,16},{24,32},{40,48},{56,64},{72,80},{88,96},{104,112},{120,128}... | collective-permute-start | bytes 589832 | tf_op jit(solution)/shard_map/ppermute | solution.py:20
  194.7 0.0 collective-permute-done.7.mirror
  194.7 1.5 shard_map.82
  196.3 1.9 collective-permute-start.8
  198.2 1.2 collective-permute-done.10.beyond
  199.4 3.2 %shard_map.84 = (bf16[128,768]{1,0:T(8,128)(2,1)S(1)}, f32[128,768]{1,0:T(8,128)S(1)}) custom-call(s32[2]{0:T(128)S(1)} %pad_add_fusion.place.core, bf16[4,256,384]{2,1,0:T(8,128)(2,1)S(1)} %pad_maximum_fusion.grads, bf16[128,768]{1,0:T(8,128)(2,1)S(1)} %collective-permute-done.10.beyond, bf16[128,768]{1,0:T(8,128)(2,1)S(1)} %get-tuple-element.29.edge, ...), custom_call_target="tpu_custom_call" | custom-call | flops 754974720 | bytes 8257536 | tf_op jit(solution)/shard_map/pallas_call | solution.py:43
  202.6 0.0 collective-permute-done.8.across
  202.6 2.0 shard_map.85
  (1 shorter events, 0.0 us)
Async XLA Ops:
  0.7 0.9 copy-start.2
  1.6 0.7 copy-start.3
  2.3 0.7 copy-start.4
  80.3 23.3 %collective-permute-start.4 = (bf16[4,768,512]{2,1,0:T(8,128)(2,1)S(1)}, bf16[4,768,512]{2,1,0:T(8,128)(2,1)}, u32[]{:S(2)}, u32[]{:S(2)}) collective-permute-start(bf16[4,768,512]{2,1,0:T(8,128)(2,1)S(1)} %bitcast.18), channel_id=1, source_target_pairs={{0,8},{8,0},{16,24},{24,16},{32,40},{40,32},{48,56},{56,48},{64,72... | collective-permute-start | bytes 9437192 | tf_op jit(solution)/shard_map/ppermute | solution.py:20
  82.3 11.2 %copy-start = (bf16[1,1,256,1536]{3,2,1,0:T(8,128)(2,1)S(1)}, bf16[1,1,256,1536]{3,2,1,0:T(8,128)(2,1)}, u32[]{:S(2)}) copy-start(bf16[1,1,256,1536]{3,2,1,0:T(8,128)(2,1)} %param.6) | copy-start | bytes 2359300
  82.3 19.9 %copy-start.5 = (s32[768]{0:T(1024)S(1)}, s32[768]{0:T(1024)}, u32[]{:S(2)}) copy-start(s32[768]{0:T(1024)} %param.11) | copy-start | bytes 9220
  84.5 17.8 %collective-permute-start.1 = (bf16[256,384]{1,0:T(8,128)(2,1)}, bf16[256,384]{1,0:T(8,128)(2,1)}, u32[]{:S(2)}, u32[]{:S(2)}) collective-permute-start(bf16[256,384]{1,0:T(8,128)(2,1)} %get-tuple-element.35), channel_id=1, source_target_pairs={{0,1},{1,0},{2,3},{3,2},{4,5},{5,4},{6,7},{7,6},{8,9},{9,8},{10,11... | collective-permute-start | bytes 589832 | tf_op jit(solution)/shard_map/ppermute | solution.py:213
  86.4 15.9 %collective-permute-start.3 = (bf16[256,384]{1,0:T(8,128)(2,1)}, bf16[256,384]{1,0:T(8,128)(2,1)}, u32[]{:S(2)}, u32[]{:S(2)}) collective-permute-start(bf16[256,384]{1,0:T(8,128)(2,1)} %get-tuple-element.36), channel_id=1, source_target_pairs={{0,3},{1,2},{2,1},{3,0},{4,7},{5,6},{6,5},{7,4},{8,11},{9,10},{10,... | collective-permute-start | bytes 589832 | tf_op jit(solution)/shard_map/ppermute | solution.py:213
  89.7 12.6 %collective-permute-start.2 = (bf16[256,384]{1,0:T(8,128)(2,1)}, bf16[256,384]{1,0:T(8,128)(2,1)}, u32[]{:S(2)}, u32[]{:S(2)}) collective-permute-start(bf16[256,384]{1,0:T(8,128)(2,1)} %get-tuple-element.37), channel_id=1, source_target_pairs={{0,2},{1,3},{2,0},{3,1},{4,6},{5,7},{6,4},{7,5},{8,10},{9,11},{10,... | collective-permute-start | bytes 589832 | tf_op jit(solution)/shard_map/ppermute | solution.py:213
  94.3 26.0 %collective-permute-start = (bf16[256,768]{1,0:T(8,128)(2,1)}, bf16[256,768]{1,0:T(8,128)(2,1)S(1)}, u32[]{:S(2)}, u32[]{:S(2)}) collective-permute-start(bf16[256,768]{1,0:T(8,128)(2,1)} %slice.4), channel_id=1, source_target_pairs={{0,4},{4,0},{1,5},{5,1},{2,6},{6,2},{3,7},{7,3},{8,12},{12,8},{9,1... | collective-permute-start | bytes 1179656 | tf_op jit(solution)/shard_map/ppermute | solution.py:24
  103.6 16.6 %copy-start.1 = (bf16[1,1,256,1536]{3,2,1,0:T(8,128)(2,1)S(1)}, bf16[1,1,256,1536]{3,2,1,0:T(8,128)(2,1)}, u32[]{:S(2)}) copy-start(bf16[1,1,256,1536]{3,2,1,0:T(8,128)(2,1)} %param.6) | copy-start | bytes 2359300
  121.6 25.6 %collective-permute-start.5 = (bf16[128,768]{1,0:T(8,128)(2,1)S(1)}, bf16[128,768]{1,0:T(8,128)(2,1)S(1)}, u32[]{:S(2)}, u32[]{:S(2)}) collective-permute-start(bf16[128,768]{1,0:T(8,128)(2,1)S(1)} %get-tuple-element.19.edge), channel_id=1, source_target_pairs={{8,16},{24,32},{40,48},{56,64},{72,80},{88,96},{104,112},{120,128}... | collective-permute-start | bytes 589832 | tf_op jit(solution)/shard_map/ppermute | solution.py:20
  131.2 16.0 %collective-permute-start.6 = (bf16[128,768]{1,0:T(8,128)(2,1)S(1)}, bf16[128,768]{1,0:T(8,128)(2,1)S(1)}, u32[]{:S(2)}, u32[]{:S(2)}) collective-permute-start(bf16[128,768]{1,0:T(8,128)(2,1)S(1)} %get-tuple-element.20.inner), channel_id=1, source_target_pairs={{0,8},{8,0},{16,24},{24,16},{32,40},{40,32},{48,56},{56,48},{64,72... | collective-permute-start | bytes 589832 | tf_op jit(solution)/shard_map/ppermute | solution.py:20
  133.2 19.2 %collective-permute-start.9 = (bf16[2,128,384]{2,1,0:T(8,128)(2,1)S(1)}, bf16[2,128,384]{2,1,0:T(8,128)(2,1)S(1)}, u32[]{:S(2)}, u32[]{:S(2)}) collective-permute-start(bf16[2,128,384]{2,1,0:T(8,128)(2,1)S(1)} %get-tuple-element.32), channel_id=1, source_target_pairs={{0,4},{4,0},{1,5},{5,1},{2,6},{6,2},{3,7},{7,3},{8,12},{12,8},{9,1... | collective-permute-start | bytes 589832 | tf_op jit(solution)/shard_map/ppermute | solution.py:24
  139.1 55.6 %collective-permute-start.7 = (bf16[2,128,384]{2,1,0:T(8,128)(2,1)S(1)}, bf16[2,128,384]{2,1,0:T(8,128)(2,1)S(1)}, u32[]{:S(2)}, u32[]{:S(2)}) collective-permute-start(bf16[2,128,384]{2,1,0:T(8,128)(2,1)S(1)} %get-tuple-element.33), channel_id=1, source_target_pairs={{0,4},{4,0},{1,5},{5,1},{2,6},{6,2},{3,7},{7,3},{8,12},{12,8},{9,1... | collective-permute-start | bytes 589832 | tf_op jit(solution)/shard_map/ppermute | solution.py:24
  153.9 45.5 %collective-permute-start.10 = (bf16[128,768]{1,0:T(8,128)(2,1)S(1)}, bf16[128,768]{1,0:T(8,128)(2,1)S(1)}, u32[]{:S(2)}, u32[]{:S(2)}) collective-permute-start(bf16[128,768]{1,0:T(8,128)(2,1)S(1)} %get-tuple-element.29.edge), channel_id=1, source_target_pairs={{8,16},{24,32},{40,48},{56,64},{72,80},{88,96},{104,112},{120,128}... | collective-permute-start | bytes 589832 | tf_op jit(solution)/shard_map/ppermute | solution.py:20
  196.3 6.3 %collective-permute-start.8 = (bf16[128,768]{1,0:T(8,128)(2,1)S(1)}, bf16[128,768]{1,0:T(8,128)(2,1)S(1)}, u32[]{:S(2)}, u32[]{:S(2)}) collective-permute-start(bf16[128,768]{1,0:T(8,128)(2,1)S(1)} %get-tuple-element.25.inner), channel_id=1, source_target_pairs={{0,8},{8,0},{16,24},{24,16},{32,40},{40,32},{48,56},{56,48},{64,72... | collective-permute-start | bytes 589832 | tf_op jit(solution)/shard_map/ppermute | solution.py:20

commit v3 on v2

v3 whole, which is shorter than its diff:
```python
import jax
import jax.numpy as jnp
from jax import lax
from jax.experimental import pallas as pl
from jax.experimental.pallas import tpu as pltpu
from jax.sharding import PartitionSpec as P

BF16, F32 = jnp.bfloat16, jnp.float32
LANES = 128


def pairwise(value, bit):
    count = lax.axis_size("seq")
    if bit == 0:
        pairs = [(i, i ^ 1) for i in range(count)]
    else:
        pairs = [(i, i + 1) for i in range(1, count - 1, 2)] + [(i + 1, i) for i in range(1, count - 1, 2)]
    return lax.ppermute(value, "seq", pairs)


def mirrored(value):
    return lax.ppermute(value, "strand", [(0, 1), (1, 0)])


def dot(a, b):
    return lax.dot_general(a, b, (((1,), (0,)), ((), ())), preferred_element_type=F32)


def dot_t(a, b):
    return lax.dot_general(a, b, (((1,), (1,)), ((), ())), preferred_element_type=F32)


def at(start, size):
    return pl.ds(pl.multiple_of(start, LANES), size)


def call(kernel, ins, outs, flops, scratch=(), limit=24, space=pltpu.VMEM):
    moved = sum(a.size * a.dtype.itemsize for a in ins) + sum(
        o.size * jnp.dtype(o.dtype).itemsize for o in outs
    )

    def body(*refs):
        kernel((lax.rem(lax.axis_index("seq"), 2), lax.axis_index("head")), *refs)

    return pl.pallas_call(
        body,
        out_shape=outs,
        in_specs=[pl.BlockSpec(memory_space=pltpu.VMEM)] * len(ins),
        out_specs=[pl.BlockSpec(memory_space=space)] * len(outs),
        scratch_shapes=list(scratch),
        compiler_params=pltpu.CompilerParams(vmem_limit_bytes=limit << 20),
        cost_estimate=pl.CostEstimate(flops=flops, bytes_accessed=moved, transcendentals=0),
    )(*ins)


def shape(dims, kind):
    return jax.ShapeDtypeStruct(dims, kind)


def split(place, taps, out, mix, sent):
    head = place[1]
    wide = sent.shape[3] - LANES
    carried = jnp.where(head == 3, out[...], taps[jnp.minimum(head, 2)])
    for c in range(2):
        column = (2 * jnp.minimum(head, 2) + c) * LANES
        sent[0, c, :, :wide] = carried[:, c * wide : (c + 1) * wide]
        sent[0, c, :, wide:] = mix[:, at(column, LANES)]
    for k in range(1, sent.shape[0]):
        sent[k] = sent[0]


def repack(place, line, sent):
    deep = line.shape[1]
    for z in range(sent.shape[1]):
        sent[0, z, :deep, :] = line[2 * z]
        sent[0, z, deep:, :] = line[2 * z + 1]
    for k in range(1, sent.shape[0]):
        sent[k] = sent[0]


def mirror_sum(core, perm, top, mirror, both):
    half = both.shape[2]
    hot = (lax.broadcasted_iota(jnp.int32, (half, half), 0) == perm[...]).astype(BF16)
    both[0] = (top[:, :half].astype(F32) + dot(mirror[...], hot)).astype(BF16)
    both[1] = top[:, half:]


def restore(core, paired, own, other, edge, inner):
    c = core[0]
    rows, half = edge.shape
    for k in range(half // (2 * LANES)):
        for place, pieces in ((c, own), (1 - c, other)):
            column = (2 * k + place) * LANES
            mixing = dot(paired[0], pieces[k])
            b = (paired[1, :, at(column, LANES)].astype(F32) - mixing).astype(BF16)

            @pl.when(c == 0)
            def _():
                edge[:, at(column, LANES)] = b[:rows]
                inner[:, at(column, LANES)] = b[rows:]

            @pl.when(c == 1)
            def _():
                edge[:, at(column, LANES)] = b[rows:]
                inner[:, at(column, LANES)] = b[:rows]


def turn(core, perm, grads, own, other, turned, base, mix):
    c, head = core[0], core[1]
    side = turned.shape[0]
    wide = side // 2
    hot = (lax.broadcasted_iota(jnp.int32, (side, side), 0) == perm[...]).astype(BF16)
    for place, pieces in ((c, own), (1 - c, other)):
        for k in range(side // (2 * LANES)):
            row = at((2 * k + place) * LANES, LANES)
            block = pieces[k]
            mix[row, :] = block.T
            turned[row, :] = dot(hot, block).astype(BF16).T
    backed = dot(grads[head ^ 2], mix[:wide, :]) + dot(grads[head ^ 3], mix[wide:, :])
    for k in range(2):
        lane = slice(k * wide, (k + 1) * wide)
        base[:, lane] = grads[head ^ k].astype(F32) + backed[:, lane]


def branch(core, beyond, edge, inner, across, own, other, hidden, slope, out):
    c = core[0]
    _, half = edge.shape
    before = jnp.concatenate([beyond[...], edge[...]], axis=0)
    here = jnp.concatenate([edge[...], inner[...]], axis=0)
    after = jnp.concatenate([inner[...], across[...]], axis=0)
    wide = half // 2
    root = 0.7978845608028654
    for place, taps in ((c, own), (1 - c, other)):
        lane = at(place * wide, wide)
        pre = (
            dot(before, taps[2 * c, :, :wide])
            + dot(here, taps[1, :, :wide])
            + dot(after, taps[2 - 2 * c, :, :wide])
        )
        squared = pre * pre
        bent = jnp.tanh(root * (pre + 0.044715 * (pre * squared)))
        share = 0.5 * (1.0 + bent)
        slope[:, lane] = share + pre * (0.5 * (1.0 - bent * bent)) * (
            root * (1.0 + 3.0 * 0.044715 * squared)
        )
        hidden[:, lane] = (pre * share).astype(BF16)
        out[lane, :] = taps[3, :, :wide].T


def emit(core, top, hidden, edge, inner, own, other, after, restored):
    c = core[0]
    rows, half = edge.shape
    wide = half // 2
    lines = (at(c * rows, rows), at((1 - c) * rows, rows))
    for place, pieces in ((c, own), (1 - c, other)):
        lane = at(place * wide, wide)
        made = dot(hidden[...], pieces[3, :, :wide])
        for k, line in enumerate(lines):
            restored[line, lane] = (
                top[line, lane].astype(F32) - made[k * rows : (k + 1) * rows]
            ).astype(BF16)
    restored[lines[0], half:] = edge[...]
    restored[lines[1], half:] = inner[...]


def pull(core, mirror, turned, base, slope, out, cot, edge, inner):
    c = core[0]
    rows = edge.shape[0]
    wide = mirror.shape[2]
    odd = core[1] & 1
    rounded = (
        base[...] + dot(mirror[odd], turned[:wide, :]) + dot(mirror[1 - odd], turned[wide:, :])
    ).astype(BF16)
    cot[...] = rounded
    pulled = dot(rounded, out[...])

    @pl.when(c == 0)
    def _():
        edge[...] = (pulled[:rows] * slope[:rows, :]).astype(BF16)
        inner[...] = (pulled[rows:] * slope[rows:, :]).astype(BF16)

    @pl.when(c == 1)
    def _():
        edge[...] = (pulled[rows:] * slope[:rows, :]).astype(BF16)
        inner[...] = (pulled[:rows] * slope[rows:, :]).astype(BF16)


def gather(core, grads, beyond, edge, inner, own, other, result, rest, near):
    c = core[0]
    rows, half = edge.shape
    wide = half // 2
    head = core[1]
    total = jnp.zeros((2 * rows, half), F32)
    low = jnp.zeros((rows, half), F32)
    for place, taps in ((c, own), (1 - c, other)):
        lane = at(place * wide, wide)
        e, i = edge[:, lane], inner[:, lane]
        total += dot_t(jnp.concatenate([e, i], axis=0), taps[1, :, :wide])
        total += dot_t(jnp.concatenate([beyond[:, lane], e], axis=0), taps[2 - 2 * c, :, :wide])
        low += dot_t(i, taps[2 * c, :, :wide])
        near[lane, :] = taps[2 * c, :, :wide].T
    lines = (at(c * rows, rows), at((1 - c) * rows, rows))
    plain = [
        jnp.concatenate([grads[head ^ 2, line, :], grads[head ^ 3, line, :]], axis=1).astype(F32)
        for line in lines
    ]
    result[...] = (plain[0] + total[:rows] + low).astype(BF16)
    rest[...] = plain[1] + total[rows:]


def finish(core, across, near, cot, edge_b, rest, result):
    c = core[0]
    rows = edge_b.shape[0]
    half = cot.shape[1]
    result[:, :half] = cot[...]
    result[at(c * rows, rows), half:] = edge_b[...]
    result[at((1 - c) * rows, rows), half:] = (rest[...] + dot(across[...], near[...])).astype(BF16)


def shards(top, grad_heads, tap_weight_grid, out_w, mix_w, rc_perm):
    half = top.shape[3] // 2
    rows = top.shape[2] // 2
    heads = lax.axis_size("head")
    ranks = 4
    lines = lax.axis_size("seq") // (2 * ranks)
    head = lax.axis_index("head")
    top = top[0, 0]

    deep = out_w.shape[0]
    (sent,) = call(
        split,
        (tap_weight_grid, out_w, mix_w),
        (shape((lines, 2, deep, half // 2 + LANES), BF16),),
        0,
        limit=60,
    )
    along = [[(y * lines + z) * 2 + c for z in range(lines) for c in range(2)] for y in range(ranks)]
    line = lax.all_to_all(
        sent.reshape(2 * lines, *sent.shape[2:]), "seq", 0, 0, axis_index_groups=along, tiled=True
    )
    ao = mirrored(top[:, :half])
    blocks = [lax.dynamic_index_in_dim(grad_heads[:, 0], head ^ k, 0, False) for k in range(heads)]
    grads = [blocks[0]]
    for k in range(1, heads):
        grads.append(lax.ppermute(blocks[k], "head", [(i, i ^ k) for i in range(heads)]))
    grads = jnp.stack(grads)

    go = mirrored(lax.dynamic_slice_in_dim(grads, 2 - (head // 2) * 2, 2, 0))
    plane = [
        [h * 2 * lines * ranks + (y * lines + z) * 2 + c for h in range(heads) for y in range(ranks)]
        for z in range(lines)
        for c in range(2)
    ]

    width = line.shape[2]
    (sent,) = call(repack, (line,), (shape((heads * ranks, lines, 2 * deep, width), BF16),), 0)
    both = lax.all_to_all(sent, ("head", "seq"), 0, 0, axis_index_groups=plane, tiled=True)
    both = both.reshape(heads, half, width)
    mine_mix = both[: half // (2 * LANES), :, half // 2 :]
    theirs_mix = pairwise(mine_mix, 0)
    mine = both
    theirs = pairwise(both, 0)

    unit = 2 * rows * half * half
    square, tall, chunk = (half, half), (2 * rows, half), (rows, half)
    perm = rc_perm[None, :]
    (paired,) = call(mirror_sum, (perm, top, ao), (shape((2, *tall), BF16),), 2 * unit)
    edge, inner = call(
        restore, (paired, mine_mix, theirs_mix), (shape(chunk, BF16), shape(chunk, BF16)), 2 * unit
    )
    beyond = pairwise(edge, 1)
    across = pairwise(inner, 0)
    turned, base = call(
        turn,
        (perm, grads, mine_mix, theirs_mix),
        (shape(square, BF16), shape(tall, F32)),
        6 * unit,
        scratch=(pltpu.VMEM(square, BF16),),
    )
    hidden, slope, out = call(
        branch,
        (beyond, edge, inner, across, mine, theirs),
        (shape(tall, BF16), shape(tall, F32), shape(square, BF16)),
        6 * unit,
    )
    cot, held_edge, held_inner = call(
        pull,
        (go, turned, base, slope, out),
        (shape(tall, BF16), shape(chunk, BF16), shape(chunk, BF16)),
        4 * unit,
    )
    cot_beyond = pairwise(held_edge, 1)
    cot_across = pairwise(held_inner, 0)
    (restored,) = call(
        emit,
        (top, hidden, edge, inner, mine, theirs, held_inner),
        (shape(top.shape, BF16),),
        2 * unit,
    )
    edge_b, rest, near = call(
        gather,
        (grads, cot_beyond, held_edge, held_inner, mine, theirs),
        (shape(chunk, BF16), shape(chunk, F32), shape(square, BF16)),
        5 * unit,
    )
    (result,) = call(
        finish,
        (cot_across, near, cot, edge_b, rest),
        (shape(top.shape, BF16),),
        unit,
    )
    return restored[None, None], result[None, None]


def solution(mesh):
    placed = (
        P("head", "strand", "seq", None),
        P(None, "strand", "seq", "head"),
        P(None, "seq", None),
        P("seq", None),
        P("seq", None),
        P(),
    )
    return jax.shard_map(
        shards,
        mesh=mesh,
        in_specs=placed,
        out_specs=(P("head", "strand", "seq", None), P("head", "strand", "seq", None)),
        check_vma=False,
    )
```

time: 205 us -> 205 us (level)
  the two profiles are of different devices: /device:TPU:1 before, /device:TPU:14 now
where the time goes in v3:
time: 205 us; the launch traced here: 204 us
  blocking collectives  71.9 us (35%)
  waiting for transfers between devices  56.9 us (28%)
  starting transfers between devices  45.2 us (22%)
  Pallas kernels  21.5 us (10%)
  local copies, waits for them, and re-layouts  5.96 us (3%)
    all_to_all x1, blocking collectives, shards(): lax.all_to_all(sent, ('head', 'seq'), 0, 0, axis_index_groups=plane, tile...  44.4 us
    ppermute x2, waiting for transfers between devices, mirrored(): return lax.ppermute(value, 'strand', [(0, 1), (1, 0)])  38.5 us
    all_to_all x1, blocking collectives, shards(): lax.all_to_all(sent.reshape(2 * lines, *sent.shape[2:]), 'seq', 0, 0, axi...  27.6 us
    pallas_call x10, Pallas kernels, call(): pl.pallas_call(body, out_shape=outs, in_specs=[pl.BlockSpec(memory_space=...  21.5 us
    ppermute x6, starting transfers between devices, pairwise(): return lax.ppermute(value, 'seq', pairs)  20.9 us
    ppermute x6, waiting for transfers between devices, pairwise(): return lax.ppermute(value, 'seq', pairs)  18.5 us
    ppermute x2, starting transfers between devices, mirrored(): return lax.ppermute(value, 'strand', [(0, 1), (1, 0)])  14.5 us
    ppermute x3, starting transfers between devices, shards(): lax.ppermute(blocks[k], 'head', [(i, i ^ k) for i in range(heads)])  9.81 us
  transfers between devices with their start and end apart: 11, of which 3 were waited for; matrix products, arithmetic and copies ran while one was open for 3% of the time, Pallas kernels for 9%

profile of v3, /device:TPU:14, one launch (start us, length us, event | category | flops | bytes accessed | tf_op | source)
XLA Modules:
  0.0 203.7 jit_solution(12231647499989111818)
XLA Ops:
  0.6 1.6 shard_map.78
  2.3 27.6 %all_to_all.10.refs_0_ = bf16[16,12,512]{2,1,0:T(8,128)(2,1)S(1)} all-to-all(bf16[16,12,512]{2,1,0:T(8,128)(2,1)} %bitcast.24), channel_id=1, replica_groups={{0,8,16,24,32,40,48,56,64,72,80,88,96,104,112,120},{128,136,144,152,160..., dimensions={0} | all-to-all | bytes 393216 | tf_op jit(solution)/shard_map/all_to_all | solution.py:238
  29.8 0.2 shard_map.79
  30.1 44.4 %all_to_all.11 = bf16[16,8,24,512]{3,2,1,0:T(8,128)(2,1)S(1)} all-to-all(bf16[16,8,24,512]{3,2,1,0:T(8,128)(2,1)S(1)} %shard_map.79), channel_id=1, replica_groups={{0,128,256,384,1,129,257,385,2,130,258,386,3,131,259,387},{8,136,264,39..., dimensions={0} | all-to-all | bytes 6291456 | tf_op jit(solution)/shard_map/all_to_all | solution.py:257
  74.4 0.0 copy-start.2
  74.4 3.1 %collective-permute-start.4 = (bf16[4,768,512]{2,1,0:T(8,128)(2,1)S(1)}, bf16[4,768,512]{2,1,0:T(8,128)(2,1)}, u32[]{:S(2)}, u32[]{:S(2)}) collective-permute-start(bf16[4,768,512]{2,1,0:T(8,128)(2,1)S(1)} %bitcast.16), channel_id=1, source_target_pairs={{0,8},{8,0},{16,24},{24,16},{32,40},{40,32},{48,56},{56,48},{64,72... | collective-permute-start | bytes 9437192 | tf_op jit(solution)/shard_map/ppermute | solution.py:18
  77.6 2.1 %dynamic-slice_bitcast_fusion.3 = (bf16[1,256,384]{2,1,0:T(8,128)(2,1)}, bf16[256,384]{1,0:T(8,128)(2,1)S(1)}, bf16[256,384]{1,0:T(8,128)(2,1)}, bf16[256,384]{1,0:T(8,128)(2,1)}) fusion(bf16[4,1,256,384]{3,2,1,0:T(8,128)(2,1)} %param.7, s32[]{:T(128)S(6)} %select_n.21, s32[]{:T(128)S(6)} %select_n.22, s32[]{:T(128)S(6)} %select_n.24, s32[]{:T(128)S(6)} %select_n.23), kind=kLoop, calls=%fused_computation.4 | loop fusion | bytes 1572880 | tf_op jit(solution)/shard_map/jit(dynamic_index_in_dim)/dynamic_slice | solution.py:242
  79.6 1.9 collective-permute-start.5
  81.5 0.9 slice.9.refs_1_.refs_2_
  82.5 1.9 collective-permute-start.1
  84.4 3.6 %collective-permute-start.7 = (bf16[256,384]{1,0:T(8,128)(2,1)}, bf16[256,384]{1,0:T(8,128)(2,1)}, u32[]{:S(2)}, u32[]{:S(2)}) collective-permute-start(bf16[256,384]{1,0:T(8,128)(2,1)} %get-tuple-element.30), channel_id=1, source_target_pairs={{0,3},{1,2},{2,1},{3,0},{4,7},{5,6},{6,5},{7,4},{8,11},{9,10},{10,... | collective-permute-start | bytes 589832 | tf_op jit(solution)/shard_map/ppermute | solution.py:245
  88.0 4.3 %collective-permute-start.6 = (bf16[256,384]{1,0:T(8,128)(2,1)}, bf16[256,384]{1,0:T(8,128)(2,1)}, u32[]{:S(2)}, u32[]{:S(2)}) collective-permute-start(bf16[256,384]{1,0:T(8,128)(2,1)} %get-tuple-element.31), channel_id=1, source_target_pairs={{0,2},{1,3},{2,0},{3,1},{4,6},{5,7},{6,4},{7,5},{8,10},{9,11},{10,... | collective-permute-start | bytes 589832 | tf_op jit(solution)/shard_map/ppermute | solution.py:245
  92.3 1.8 slice.8
  94.1 0.0 collective-permute-done.5
  94.1 8.2 %collective-permute-start = (bf16[256,768]{1,0:T(8,128)(2,1)}, bf16[256,768]{1,0:T(8,128)(2,1)S(1)}, u32[]{:S(2)}, u32[]{:S(2)}) collective-permute-start(bf16[256,768]{1,0:T(8,128)(2,1)} %slice.8), channel_id=1, source_target_pairs={{0,4},{4,0},{1,5},{5,1},{2,6},{6,2},{3,7},{7,3},{8,12},{12,8},{9,1... | collective-permute-start | bytes 1179656 | tf_op jit(solution)/shard_map/ppermute | solution.py:22
  102.3 0.0 collective-permute-done.7
  102.3 0.0 collective-permute-done.6
  102.3 1.3 pad_maximum_fusion.refs_1_.refs_0_
  103.7 0.1 constant_dynamic-slice_fusion
  103.7 6.3 %collective-permute-start.8 = (bf16[2,256,384]{2,1,0:T(8,128)(2,1)S(1)}, bf16[2,256,384]{2,1,0:T(8,128)(2,1)S(1)}, u32[]{:S(2)}, u32[]{:S(2)}) collective-permute-start(bf16[2,256,384]{2,1,0:T(8,128)(2,1)S(1)} %constant_dynamic-slice_fusion), channel_id=1, source_target_pairs={{0,4},{4,0},{1,5},{5,1},{2,6},{6,2},{3,7},{7,3},{8,12},{12,8},{9,1... | collective-permute-start | bytes 1179656 | tf_op jit(solution)/shard_map/ppermute | solution.py:22
  110.1 0.0 copy-done.2
  110.1 38.4 %collective-permute-done.refs_2_ = bf16[256,768]{1,0:T(8,128)(2,1)S(1)} collective-permute-done((bf16[256,768]{1,0:T(8,128)(2,1)}, bf16[256,768]{1,0:T(8,128)(2,1)S(1)}, u32[]{:S(2)}, u32[]{:S(2)}) %collective-permute-start) | collective-permute-done | bytes 393248 | tf_op jit(solution)/shard_map/ppermute | solution.py:22
  148.6 0.0 copy-start
  148.6 1.1 copy-done
  149.7 0.5 shard_map.77.refs_0_
  150.2 0.0 collective-permute-done.1.refs_2_.refs_3_
  150.2 3.0 %shard_map.80 = (bf16[128,768]{1,0:T(8,128)(2,1)S(1)}, bf16[128,768]{1,0:T(8,128)(2,1)S(1)}) custom-call(bf16[2,256,768]{2,1,0:T(8,128)(2,1)S(1)} %shard_map.77.refs_0_, bf16[3,768,128]{2,1,0:T(8,128)(2,1)} %slice.9.refs_1_.refs_2_, bf16[3,768,128]{2,1,0:T(8,128)(2,1)} %collective-permute-done.1.refs_2_.refs_3_), custom_call_target="tpu_custom_call" | custom-call | flops 301989888 | bytes 2359296 | tf_op jit(solution)/shard_map/pallas_call | solution.py:45
  153.2 5.6 %collective-permute-start.2 = (bf16[128,768]{1,0:T(8,128)(2,1)S(1)}, bf16[128,768]{1,0:T(8,128)(2,1)S(1)}, u32[]{:S(2)}, u32[]{:S(2)}) collective-permute-start(bf16[128,768]{1,0:T(8,128)(2,1)S(1)} %get-tuple-element.15.refs_1_.refs_2_), channel_id=1, source_target_pairs={{8,16},{24,32},{40,48},{56,64},{72,80},{88,96},{104,112},{120,128}... | collective-permute-start | bytes 589832 | tf_op jit(solution)/shard_map/ppermute | solution.py:18
  158.9 1.9 collective-permute-start.3
  160.8 3.7 %shard_map.82 = (bf16[768,768]{1,0:T(8,128)(2,1)S(1)}, f32[256,768]{1,0:T(8,128)S(1)}) custom-call(s32[1,768]{1,0:T(1,128)S(1)} %broadcast_in_dim.9.refs_0_, bf16[4,256,384]{2,1,0:T(8,128)(2,1)S(1)} %pad_maximum_fusion.refs_1_.refs_0_, bf16[3,768,128]{2,1,0:T(8,128)(2,1)} %slice.9.refs_1_.refs_2_, bf16[3,768,128]{2,1,0:T(8,128)(2,1)} %collective-permute-done.1.refs_2_.refs_3_), custom_call_target="tpu_custom_call" | custom-call | flops 905969664 | bytes 3935232 | tf_op jit(solution)/shard_map/pallas_call | solution.py:45
  164.5 15.7 %collective-permute-done.2.refs_0_ = bf16[128,768]{1,0:T(8,128)(2,1)S(1)} collective-permute-done((bf16[128,768]{1,0:T(8,128)(2,1)S(1)}, bf16[128,768]{1,0:T(8,128)(2,1)S(1)}, u32[]{:S(2)}, u32[]{:S(2)}) %collective-permute-start.2) | collective-permute-done | bytes 196640 | tf_op jit(solution)/shard_map/ppermute | solution.py:18
  180.1 0.0 collective-permute-done.3.refs_3_
  180.1 0.0 collective-permute-done.4.refs_5_
  180.2 3.6 %shard_map.81 = (bf16[256,768]{1,0:T(8,128)(2,1)S(1)}, f32[256,768]{1,0:T(8,128)S(1)}, bf16[768,768]{1,0:T(8,128)(2,1)S(1)}) custom-call(bf16[128,768]{1,0:T(8,128)(2,1)S(1)} %collective-permute-done.2.refs_0_, bf16[128,768]{1,0:T(8,128)(2,1)S(1)} %get-tuple-element.15.refs_1_.refs_2_, bf16[128,768]{1,0:T(8,128)(2,1)S(1)} %get-tuple-element.16.refs_2_.refs_3_, ...), custom_call_target="tpu_custom_call" | custom-call | flops 905969664 | bytes 9437184 | tf_op jit(solution)/shard_map/pallas_call | solution.py:45
  183.7 0.0 copy-start.1
  183.8 0.0 collective-permute-done.8.refs_0_
  183.8 1.1 shard_map.83
  184.8 6.4 %collective-permute-start.10 = (bf16[128,768]{1,0:T(8,128)(2,1)S(1)}, bf16[128,768]{1,0:T(8,128)(2,1)S(1)}, u32[]{:S(2)}, u32[]{:S(2)}) collective-permute-start(bf16[128,768]{1,0:T(8,128)(2,1)S(1)} %get-tuple-element.23.refs_2_), channel_id=1, source_target_pairs={{8,16},{24,32},{40,48},{56,64},{72,80},{88,96},{104,112},{120,128}... | collective-permute-start | bytes 589832 | tf_op jit(solution)/shard_map/ppermute | solution.py:18
  191.2 1.9 collective-permute-start.9
  193.2 0.0 copy-done.1
  193.2 3.4 %shard_map.84 = bf16[256,1536]{1,0:T(8,128)(2,1)} custom-call(bf16[256,1536]{1,0:T(8,128)(2,1)S(1)} %bitcast.23, bf16[256,768]{1,0:T(8,128)(2,1)S(1)} %get-tuple-element.17.refs_1_, bf16[128,768]{1,0:T(8,128)(2,1)S(1)} %get-tuple-element.15.refs_1_.refs_2_, bf16[128,768]{1,0:T(8,128)(2,1)S(1)} %get-tuple-element.16.refs_2_.refs_3_, ...), custom_call_target="tpu_custom_call" | custom-call | flops 301989888 | bytes 8847360 | tf_op jit(solution)/shard_map/pallas_call | solution.py:45
  196.5 2.8 %collective-permute-done.10.refs_1_ = bf16[128,768]{1,0:T(8,128)(2,1)S(1)} collective-permute-done((bf16[128,768]{1,0:T(8,128)(2,1)S(1)}, bf16[128,768]{1,0:T(8,128)(2,1)S(1)}, u32[]{:S(2)}, u32[]{:S(2)}) %collective-permute-start.10) | collective-permute-done | bytes 196640 | tf_op jit(solution)/shard_map/ppermute | solution.py:18
  199.3 3.2 %shard_map.85 = (bf16[128,768]{1,0:T(8,128)(2,1)S(1)}, f32[128,768]{1,0:T(8,128)S(1)}, bf16[768,768]{1,0:T(8,128)(2,1)S(1)}) custom-call(bf16[4,256,384]{2,1,0:T(8,128)(2,1)S(1)} %pad_maximum_fusion.refs_1_.refs_0_, bf16[128,768]{1,0:T(8,128)(2,1)S(1)} %collective-permute-done.10.refs_1_, bf16[128,768]{1,0:T(8,128)(2,1)S(1)} %get-tuple-element.23.refs_2_, ...), custom_call_target="tpu_custom_call" | custom-call | flops 754974720 | bytes 9437184 | tf_op jit(solution)/shard_map/pallas_call | solution.py:45
  202.5 0.0 collective-permute-done.9.refs_0_
  202.5 1.2 shard_map.86
  (1 shorter events, 0.0 us)
Async XLA Ops:
  74.4 35.6 %copy-start.2 = (s32[768]{0:T(1024)S(1)}, s32[768]{0:T(1024)}, u32[]{:S(2)}) copy-start(s32[768]{0:T(1024)} %param.11) | copy-start | bytes 9220
  74.4 105.7 %collective-permute-start.4 = (bf16[4,768,512]{2,1,0:T(8,128)(2,1)S(1)}, bf16[4,768,512]{2,1,0:T(8,128)(2,1)}, u32[]{:S(2)}, u32[]{:S(2)}) collective-permute-start(bf16[4,768,512]{2,1,0:T(8,128)(2,1)S(1)} %bitcast.16), channel_id=1, source_target_pairs={{0,8},{8,0},{16,24},{24,16},{32,40},{40,32},{48,56},{56,48},{64,72... | collective-permute-start | bytes 9437192 | tf_op jit(solution)/shard_map/ppermute | solution.py:18
  79.6 14.4 %collective-permute-start.5 = (bf16[256,384]{1,0:T(8,128)(2,1)S(1)}, bf16[256,384]{1,0:T(8,128)(2,1)}, u32[]{:S(2)}, u32[]{:S(2)}) collective-permute-start(bf16[256,384]{1,0:T(8,128)(2,1)S(1)} %get-tuple-element.29), channel_id=1, source_target_pairs={{0,1},{1,0},{2,3},{3,2},{4,5},{5,4},{6,7},{7,6},{8,9},{9,8},{10,11... | collective-permute-start | bytes 589832 | tf_op jit(solution)/shard_map/ppermute | solution.py:245
  82.5 67.7 %collective-permute-start.1 = (bf16[3,768,128]{2,1,0:T(8,128)(2,1)}, bf16[3,768,128]{2,1,0:T(8,128)(2,1)}, u32[]{:S(2)}, u32[]{:S(2)}) collective-permute-start(bf16[3,768,128]{2,1,0:T(8,128)(2,1)} %slice.9.refs_1_.refs_2_), channel_id=1, source_target_pairs={{0,8},{8,0},{16,24},{24,16},{32,40},{40,32},{48,56},{56,48},{64,72... | collective-permute-start | bytes 1769480 | tf_op jit(solution)/shard_map/ppermute | solution.py:18
  84.4 17.9 %collective-permute-start.7 = (bf16[256,384]{1,0:T(8,128)(2,1)}, bf16[256,384]{1,0:T(8,128)(2,1)}, u32[]{:S(2)}, u32[]{:S(2)}) collective-permute-start(bf16[256,384]{1,0:T(8,128)(2,1)} %get-tuple-element.30), channel_id=1, source_target_pairs={{0,3},{1,2},{2,1},{3,0},{4,7},{5,6},{6,5},{7,4},{8,11},{9,10},{10,... | collective-permute-start | bytes 589832 | tf_op jit(solution)/shard_map/ppermute | solution.py:245
  88.0 14.4 %collective-permute-start.6 = (bf16[256,384]{1,0:T(8,128)(2,1)}, bf16[256,384]{1,0:T(8,128)(2,1)}, u32[]{:S(2)}, u32[]{:S(2)}) collective-permute-start(bf16[256,384]{1,0:T(8,128)(2,1)} %get-tuple-element.31), channel_id=1, source_target_pairs={{0,2},{1,3},{2,0},{3,1},{4,6},{5,7},{6,4},{7,5},{8,10},{9,11},{10,... | collective-permute-start | bytes 589832 | tf_op jit(solution)/shard_map/ppermute | solution.py:245
  94.1 54.5 %collective-permute-start = (bf16[256,768]{1,0:T(8,128)(2,1)}, bf16[256,768]{1,0:T(8,128)(2,1)S(1)}, u32[]{:S(2)}, u32[]{:S(2)}) collective-permute-start(bf16[256,768]{1,0:T(8,128)(2,1)} %slice.8), channel_id=1, source_target_pairs={{0,4},{4,0},{1,5},{5,1},{2,6},{6,2},{3,7},{7,3},{8,12},{12,8},{9,1... | collective-permute-start | bytes 1179656 | tf_op jit(solution)/shard_map/ppermute | solution.py:22
  103.7 80.0 %collective-permute-start.8 = (bf16[2,256,384]{2,1,0:T(8,128)(2,1)S(1)}, bf16[2,256,384]{2,1,0:T(8,128)(2,1)S(1)}, u32[]{:S(2)}, u32[]{:S(2)}) collective-permute-start(bf16[2,256,384]{2,1,0:T(8,128)(2,1)S(1)} %constant_dynamic-slice_fusion), channel_id=1, source_target_pairs={{0,4},{4,0},{1,5},{5,1},{2,6},{6,2},{3,7},{7,3},{8,12},{12,8},{9,1... | collective-permute-start | bytes 1179656 | tf_op jit(solution)/shard_map/ppermute | solution.py:22
  148.6 1.1 copy-start
  153.2 26.9 %collective-permute-start.2 = (bf16[128,768]{1,0:T(8,128)(2,1)S(1)}, bf16[128,768]{1,0:T(8,128)(2,1)S(1)}, u32[]{:S(2)}, u32[]{:S(2)}) collective-permute-start(bf16[128,768]{1,0:T(8,128)(2,1)S(1)} %get-tuple-element.15.refs_1_.refs_2_), channel_id=1, source_target_pairs={{8,16},{24,32},{40,48},{56,64},{72,80},{88,96},{104,112},{120,128}... | collective-permute-start | bytes 589832 | tf_op jit(solution)/shard_map/ppermute | solution.py:18
  158.9 21.3 %collective-permute-start.3 = (bf16[128,768]{1,0:T(8,128)(2,1)S(1)}, bf16[128,768]{1,0:T(8,128)(2,1)S(1)}, u32[]{:S(2)}, u32[]{:S(2)}) collective-permute-start(bf16[128,768]{1,0:T(8,128)(2,1)S(1)} %get-tuple-element.16.refs_2_.refs_3_), channel_id=1, source_target_pairs={{0,8},{8,0},{16,24},{24,16},{32,40},{40,32},{48,56},{56,48},{64,72... | collective-permute-start | bytes 589832 | tf_op jit(solution)/shard_map/ppermute | solution.py:18
  183.7 9.4 %copy-start.1 = (bf16[1,1,256,1536]{3,2,1,0:T(8,128)(2,1)S(1)}, bf16[1,1,256,1536]{3,2,1,0:T(8,128)(2,1)}, u32[]{:S(2)}) copy-start(bf16[1,1,256,1536]{3,2,1,0:T(8,128)(2,1)} %param.6) | copy-start | bytes 2359300
  184.8 14.5 %collective-permute-start.10 = (bf16[128,768]{1,0:T(8,128)(2,1)S(1)}, bf16[128,768]{1,0:T(8,128)(2,1)S(1)}, u32[]{:S(2)}, u32[]{:S(2)}) collective-permute-start(bf16[128,768]{1,0:T(8,128)(2,1)S(1)} %get-tuple-element.23.refs_2_), channel_id=1, source_target_pairs={{8,16},{24,32},{40,48},{56,64},{72,80},{88,96},{104,112},{120,128}... | collective-permute-start | bytes 589832 | tf_op jit(solution)/shard_map/ppermute | solution.py:18
  191.2 11.3 %collective-permute-start.9 = (bf16[128,768]{1,0:T(8,128)(2,1)S(1)}, bf16[128,768]{1,0:T(8,128)(2,1)S(1)}, u32[]{:S(2)}, u32[]{:S(2)}) collective-permute-start(bf16[128,768]{1,0:T(8,128)(2,1)S(1)} %get-tuple-element.22.refs_6_.refs_3_), channel_id=1, source_target_pairs={{0,8},{8,0},{16,24},{24,16},{32,40},{40,32},{48,56},{56,48},{64,72... | collective-permute-start | bytes 589832 | tf_op jit(solution)/shard_map/ppermute | solution.py:18

commit v4 on v3

--- a/solution.py
+++ b/solution.py
@@ -1,3 +1,5 @@
+import functools
+
 import jax
 import jax.numpy as jnp
 from jax import lax
@@ -34,7 +36,7 @@
     return pl.ds(pl.multiple_of(start, LANES), size)
 
 
-def call(kernel, ins, outs, flops, scratch=(), limit=24, space=pltpu.VMEM):
+def call(kernel, ins, outs, flops, scratch=(), limit=14, space=pltpu.VMEM):
     moved = sum(a.size * a.dtype.itemsize for a in ins) + sum(
         o.size * jnp.dtype(o.dtype).itemsize for o in outs
     )
@@ -69,11 +71,11 @@
         sent[k] = sent[0]
 
 
-def repack(place, line, sent):
+def repack(lanes, place, line, sent):
     deep = line.shape[1]
     for z in range(sent.shape[1]):
-        sent[0, z, :deep, :] = line[2 * z]
-        sent[0, z, deep:, :] = line[2 * z + 1]
+        sent[0, z, :deep, :] = line[2 * z, :, lanes]
+        sent[0, z, deep:, :] = line[2 * z + 1, :, lanes]
     for k in range(1, sent.shape[0]):
         sent[k] = sent[0]
 
@@ -133,9 +135,9 @@
     for place, taps in ((c, own), (1 - c, other)):
         lane = at(place * wide, wide)
         pre = (
-            dot(before, taps[2 * c, :, :wide])
-            + dot(here, taps[1, :, :wide])
-            + dot(after, taps[2 - 2 * c, :, :wide])
+            dot(before, taps[2 * c])
+            + dot(here, taps[1])
+            + dot(after, taps[2 - 2 * c])
         )
         squared = pre * pre
         bent = jnp.tanh(root * (pre + 0.044715 * (pre * squared)))
@@ -144,7 +146,7 @@
             root * (1.0 + 3.0 * 0.044715 * squared)
         )
         hidden[:, lane] = (pre * share).astype(BF16)
-        out[lane, :] = taps[3, :, :wide].T
+        out[lane, :] = taps[3].T
 
 
 def emit(core, top, hidden, edge, inner, own, other, after, restored):
@@ -154,7 +156,7 @@
     lines = (at(c * rows, rows), at((1 - c) * rows, rows))
     for place, pieces in ((c, own), (1 - c, other)):
         lane = at(place * wide, wide)
-        made = dot(hidden[...], pieces[3, :, :wide])
+        made = dot(hidden[...], pieces[3])
         for k, line in enumerate(lines):
             restored[line, lane] = (
                 top[line, lane].astype(F32) - made[k * rows : (k + 1) * rows]
@@ -163,14 +165,14 @@
     restored[lines[1], half:] = inner[...]
 
 
-def pull(core, mirror, turned, base, slope, out, cot, edge, inner):
+def pull(core, upper, lower, turned, base, slope, out, cot, edge, inner):
     c = core[0]
     rows = edge.shape[0]
-    wide = mirror.shape[2]
+    wide = upper.shape[2]
     odd = core[1] & 1
-    rounded = (
-        base[...] + dot(mirror[odd], turned[:wide, :]) + dot(mirror[1 - odd], turned[wide:, :])
-    ).astype(BF16)
+    first = jnp.concatenate([upper[odd], lower[odd]], axis=0)
+    second = jnp.concatenate([upper[1 - odd], lower[1 - odd]], axis=0)
+    rounded = (base[...] + dot(first, turned[:wide, :]) + dot(second, turned[wide:, :])).astype(BF16)
     cot[...] = rounded
     pulled = dot(rounded, out[...])
 
@@ -195,10 +197,10 @@
     for place, taps in ((c, own), (1 - c, other)):
         lane = at(place * wide, wide)
         e, i = edge[:, lane], inner[:, lane]
-        total += dot_t(jnp.concatenate([e, i], axis=0), taps[1, :, :wide])
-        total += dot_t(jnp.concatenate([beyond[:, lane], e], axis=0), taps[2 - 2 * c, :, :wide])
-        low += dot_t(i, taps[2 * c, :, :wide])
-        near[lane, :] = taps[2 * c, :, :wide].T
+        total += dot_t(jnp.concatenate([e, i], axis=0), taps[1])
+        total += dot_t(jnp.concatenate([beyond[:, lane], e], axis=0), taps[2 - 2 * c])
+        low += dot_t(i, taps[2 * c])
+        near[lane, :] = taps[2 * c].T
     lines = (at(c * rows, rows), at((1 - c) * rows, rows))
     plain = [
         jnp.concatenate([grads[head ^ 2, line, :], grads[head ^ 3, line, :]], axis=1).astype(F32)
@@ -235,9 +237,7 @@
         limit=60,
     )
     along = [[(y * lines + z) * 2 + c for z in range(lines) for c in range(2)] for y in range(ranks)]
-    line = lax.all_to_all(
-        sent.reshape(2 * lines, *sent.shape[2:]), "seq", 0, 0, axis_index_groups=along, tiled=True
-    )
+    line = lax.all_to_all(sent.reshape(2 * lines, *sent.shape[2:]), "seq", 0, 0, axis_index_groups=along, tiled=True)
     ao = mirrored(top[:, :half])
     blocks = [lax.dynamic_index_in_dim(grad_heads[:, 0], head ^ k, 0, False) for k in range(heads)]
     grads = [blocks[0]]
@@ -245,21 +245,31 @@
         grads.append(lax.ppermute(blocks[k], "head", [(i, i ^ k) for i in range(heads)]))
     grads = jnp.stack(grads)
 
-    go = mirrored(lax.dynamic_slice_in_dim(grads, 2 - (head // 2) * 2, 2, 0))
+    go = []
+    for k in range(2):
+        start = (2 - (head // 2) * 2, k * rows, 0)
+        go.append(mirrored(lax.dynamic_slice(grads, start, (2, rows, half // 2))))
     plane = [
         [h * 2 * lines * ranks + (y * lines + z) * 2 + c for h in range(heads) for y in range(ranks)]
         for z in range(lines)
         for c in range(2)
     ]
 
-    width = line.shape[2]
-    (sent,) = call(repack, (line,), (shape((heads * ranks, lines, 2 * deep, width), BF16),), 0)
-    both = lax.all_to_all(sent, ("head", "seq"), 0, 0, axis_index_groups=plane, tiled=True)
-    both = both.reshape(heads, half, width)
-    mine_mix = both[: half // (2 * LANES), :, half // 2 :]
+
+    def planar(first, last):
+        (sent,) = call(
+            functools.partial(repack, slice(first, last)),
+            (line,),
+            (shape((heads * ranks, lines, 2 * deep, last - first), BF16),),
+            0,
+        )
+        found = lax.all_to_all(sent, ("head", "seq"), 0, 0, axis_index_groups=plane, tiled=True)
+        return found.reshape(heads, half, last - first)
+
+    mine_mix = planar(half // 2, half // 2 + LANES)
+    mine = planar(0, half // 2)
     theirs_mix = pairwise(mine_mix, 0)
-    mine = both
-    theirs = pairwise(both, 0)
+    theirs = pairwise(mine, 0)
 
     unit = 2 * rows * half * half
     square, tall, chunk = (half, half), (2 * rows, half), (rows, half)
@@ -285,7 +295,7 @@
     )
     cot, held_edge, held_inner = call(
         pull,
-        (go, turned, base, slope, out),
+        (*go, turned, base, slope, out),
         (shape(tall, BF16), shape(chunk, BF16), shape(chunk, BF16)),
         4 * unit,
     )

time: 205 us -> 212 us (1.034)
  the two profiles are of different devices: /device:TPU:14 before, /device:TPU:1 now
where the time goes in v4:
time: 212 us
  blocking collectives  84.4 us (40%)
  starting transfers between devices  82.7 us (39%)
  Pallas kernels  21.2 us (10%)
  waiting for transfers between devices  18.2 us (9%)
  local copies, waits for them, and re-layouts  2.89 us (1%)
    all_to_all x2, blocking collectives, planar(): lax.all_to_all(sent, ('head', 'seq'), 0, 0, axis_index_groups=plane, tile...  53.3 us
    ppermute x6, starting transfers between devices, pairwise(): return lax.ppermute(value, 'seq', pairs)  51.8 us
    all_to_all x1, blocking collectives, shards(): lax.all_to_all(sent.reshape(2 * lines, *sent.shape[2:]), 'seq', 0, 0, axi...  31 us
    ppermute x3, starting transfers between devices, mirrored(): return lax.ppermute(value, 'strand', [(0, 1), (1, 0)])  21.9 us
    pallas_call x11, Pallas kernels, call(): pl.pallas_call(body, out_shape=outs, in_specs=[pl.BlockSpec(memory_space=...  21.2 us
    ppermute x3, waiting for transfers between devices, mirrored(): return lax.ppermute(value, 'strand', [(0, 1), (1, 0)])  12.7 us
    ppermute x3, starting transfers between devices, shards(): lax.ppermute(blocks[k], 'head', [(i, i ^ k) for i in range(heads)])  8.97 us
    ppermute x3, waiting for transfers between devices, shards(): lax.ppermute(blocks[k], 'head', [(i, i ^ k) for i in range(heads)])  5.45 us
  transfers between devices with their start and end apart: 12, of which 4 were waited for; matrix products, arithmetic and copies ran while one was open for 2% of the time, Pallas kernels for 8%

profile of v4, /device:TPU:1, one launch (start us, length us, event | category | flops | bytes accessed | tf_op | source)
XLA Modules:
  0.0 211.5 jit_solution(7955908823008941002)
XLA Ops:
  0.6 1.6 shard_map.78
  2.3 31.0 %all_to_all.15.refs_0_ = bf16[16,12,512]{2,1,0:T(8,128)(2,1)S(1)} all-to-all(bf16[16,12,512]{2,1,0:T(8,128)(2,1)} %bitcast.24), channel_id=1, replica_groups={{0,8,16,24,32,40,48,56,64,72,80,88,96,104,112,120},{128,136,144,152,160..., dimensions={0} | all-to-all | bytes 393216 | tf_op jit(solution)/shard_map/all_to_all | solution.py:240
  33.3 0.2 shard_map.81
  33.5 36.7 %all_to_all.16 = bf16[16,8,24,384]{3,2,1,0:T(8,128)(2,1)S(1)} all-to-all(bf16[16,8,24,384]{3,2,1,0:T(8,128)(2,1)S(1)} %shard_map.81), channel_id=1, replica_groups={{0,128,256,384,1,129,257,385,2,130,258,386,3,131,259,387},{8,136,264,39..., dimensions={0} | all-to-all | bytes 4718592 | tf_op jit(solution)/shard_map/all_to_all | solution.py:266
  70.2 0.0 copy-start
  70.2 0.0 copy-start.1
  70.2 2.0 collective-permute-start.4
  72.2 0.1 shard_map.79
  72.4 16.7 %all_to_all.17 = bf16[16,8,24,128]{3,2,1,0:T(8,128)(2,1)} all-to-all(bf16[16,8,24,128]{3,2,1,0:T(8,128)(2,1)S(1)} %shard_map.79), channel_id=1, replica_groups={{0,128,256,384,1,129,257,385,2,130,258,386,3,131,259,387},{8,136,264,39..., dimensions={0} | all-to-all | bytes 1572864 | tf_op jit(solution)/shard_map/all_to_all | solution.py:266
  89.0 3.7 %collective-permute-start.1 = (bf16[4,768,128]{2,1,0:T(8,128)(2,1)}, bf16[4,768,128]{2,1,0:T(8,128)(2,1)}, u32[]{:S(2)}, u32[]{:S(2)}) collective-permute-start(bf16[4,768,128]{2,1,0:T(8,128)(2,1)} %bitcast.2.refs_1_.refs_2_), channel_id=1, source_target_pairs={{0,8},{8,0},{16,24},{24,16},{32,40},{40,32},{48,56},{56,48},{64,72... | collective-permute-start | bytes 2359304 | tf_op jit(solution)/shard_map/ppermute | solution.py:20
  92.8 2.1 dynamic-slice_bitcast_fusion.3
  94.8 1.9 collective-permute-start.5
  96.8 0.0 copy-done
  96.8 0.8 slice.4
  97.5 7.9 %collective-permute-start = (bf16[256,768]{1,0:T(8,128)(2,1)}, bf16[256,768]{1,0:T(8,128)(2,1)S(1)}, u32[]{:S(2)}, u32[]{:S(2)}) collective-permute-start(bf16[256,768]{1,0:T(8,128)(2,1)} %slice.4), channel_id=1, source_target_pairs={{0,4},{4,0},{1,5},{5,1},{2,6},{6,2},{3,7},{7,3},{8,12},{12,8},{9,1... | collective-permute-start | bytes 1179656 | tf_op jit(solution)/shard_map/ppermute | solution.py:24
  105.5 3.1 %collective-permute-start.7 = (bf16[256,384]{1,0:T(8,128)(2,1)}, bf16[256,384]{1,0:T(8,128)(2,1)}, u32[]{:S(2)}, u32[]{:S(2)}) collective-permute-start(bf16[256,384]{1,0:T(8,128)(2,1)} %get-tuple-element.32), channel_id=1, source_target_pairs={{0,3},{1,2},{2,1},{3,0},{4,7},{5,6},{6,5},{7,4},{8,11},{9,10},{10,... | collective-permute-start | bytes 589832 | tf_op jit(solution)/shard_map/ppermute | solution.py:245
  108.6 0.0 collective-permute-done.5
  108.6 3.9 %collective-permute-start.6 = (bf16[256,384]{1,0:T(8,128)(2,1)}, bf16[256,384]{1,0:T(8,128)(2,1)}, u32[]{:S(2)}, u32[]{:S(2)}) collective-permute-start(bf16[256,384]{1,0:T(8,128)(2,1)} %get-tuple-element.33), channel_id=1, source_target_pairs={{0,2},{1,3},{2,0},{3,1},{4,6},{5,7},{6,4},{7,5},{8,10},{9,11},{10,... | collective-permute-start | bytes 589832 | tf_op jit(solution)/shard_map/ppermute | solution.py:245
  112.6 0.0 copy-done.1
  112.6 2.2 %collective-permute-done.7 = bf16[256,384]{1,0:T(8,128)(2,1)} collective-permute-done((bf16[256,384]{1,0:T(8,128)(2,1)}, bf16[256,384]{1,0:T(8,128)(2,1)}, u32[]{:S(2)}, u32[]{:S(2)}) %collective-permute-start.7) | collective-permute-done | bytes 196640 | tf_op jit(solution)/shard_map/ppermute | solution.py:245
  114.9 3.2 %collective-permute-done.6 = bf16[256,384]{1,0:T(8,128)(2,1)} collective-permute-done((bf16[256,384]{1,0:T(8,128)(2,1)}, bf16[256,384]{1,0:T(8,128)(2,1)}, u32[]{:S(2)}, u32[]{:S(2)}) %collective-permute-start.6) | collective-permute-done | bytes 196640 | tf_op jit(solution)/shard_map/ppermute | solution.py:245
  118.1 1.3 pad_maximum_fusion.refs_1_.refs_0_
  119.4 9.1 %collective-permute-done.refs_2_ = bf16[256,768]{1,0:T(8,128)(2,1)S(1)} collective-permute-done((bf16[256,768]{1,0:T(8,128)(2,1)}, bf16[256,768]{1,0:T(8,128)(2,1)S(1)}, u32[]{:S(2)}, u32[]{:S(2)}) %collective-permute-start) | collective-permute-done | bytes 393248 | tf_op jit(solution)/shard_map/ppermute | solution.py:24
  128.5 0.5 shard_map.77.refs_0_
  129.0 0.0 collective-permute-done.1.refs_2_.refs_3_
  129.0 3.1 %shard_map.80 = (bf16[128,768]{1,0:T(8,128)(2,1)S(1)}, bf16[128,768]{1,0:T(8,128)(2,1)S(1)}) custom-call(bf16[2,256,768]{2,1,0:T(8,128)(2,1)S(1)} %shard_map.77.refs_0_, bf16[4,768,128]{2,1,0:T(8,128)(2,1)} %bitcast.2.refs_1_.refs_2_, bf16[4,768,128]{2,1,0:T(8,128)(2,1)} %collective-permute-done.1.refs_2_.refs_3_), custom_call_target="tpu_custom_call" | custom-call | flops 301989888 | bytes 2752512 | tf_op jit(solution)/shard_map/pallas_call | solution.py:47
  132.2 4.3 %collective-permute-start.2 = (bf16[128,768]{1,0:T(8,128)(2,1)S(1)}, bf16[128,768]{1,0:T(8,128)(2,1)S(1)}, u32[]{:S(2)}, u32[]{:S(2)}) collective-permute-start(bf16[128,768]{1,0:T(8,128)(2,1)S(1)} %get-tuple-element.15.refs_1_.refs_2_), channel_id=1, source_target_pairs={{8,16},{24,32},{40,48},{56,64},{72,80},{88,96},{104,112},{120,128}... | collective-permute-start | bytes 589832 | tf_op jit(solution)/shard_map/ppermute | solution.py:20
  136.5 2.6 %collective-permute-start.3 = (bf16[128,768]{1,0:T(8,128)(2,1)S(1)}, bf16[128,768]{1,0:T(8,128)(2,1)S(1)}, u32[]{:S(2)}, u32[]{:S(2)}) collective-permute-start(bf16[128,768]{1,0:T(8,128)(2,1)S(1)} %get-tuple-element.16.refs_2_.refs_3_), channel_id=1, source_target_pairs={{0,8},{8,0},{16,24},{24,16},{32,40},{40,32},{48,56},{56,48},{64,72... | collective-permute-start | bytes 589832 | tf_op jit(solution)/shard_map/ppermute | solution.py:20
  139.1 0.1 constant_dynamic-slice_fusion
  139.1 8.0 %collective-permute-start.9 = (bf16[2,128,384]{2,1,0:T(8,128)(2,1)S(1)}, bf16[2,128,384]{2,1,0:T(8,128)(2,1)S(1)}, u32[]{:S(2)}, u32[]{:S(2)}) collective-permute-start(bf16[2,128,384]{2,1,0:T(8,128)(2,1)S(1)} %get-tuple-element.28), channel_id=1, source_target_pairs={{0,4},{4,0},{1,5},{5,1},{2,6},{6,2},{3,7},{7,3},{8,12},{12,8},{9,1... | collective-permute-start | bytes 589832 | tf_op jit(solution)/shard_map/ppermute | solution.py:24
  147.1 6.0 %collective-permute-start.8 = (bf16[2,128,384]{2,1,0:T(8,128)(2,1)S(1)}, bf16[2,128,384]{2,1,0:T(8,128)(2,1)S(1)}, u32[]{:S(2)}, u32[]{:S(2)}) collective-permute-start(bf16[2,128,384]{2,1,0:T(8,128)(2,1)S(1)} %get-tuple-element.29), channel_id=1, source_target_pairs={{0,4},{4,0},{1,5},{5,1},{2,6},{6,2},{3,7},{7,3},{8,12},{12,8},{9,1... | collective-permute-start | bytes 589832 | tf_op jit(solution)/shard_map/ppermute | solution.py:24
  153.1 3.8 %shard_map.83 = (bf16[768,768]{1,0:T(8,128)(2,1)S(1)}, f32[256,768]{1,0:T(8,128)S(1)}) custom-call(s32[1,768]{1,0:T(1,128)S(1)} %broadcast_in_dim.9.refs_0_, bf16[4,256,384]{2,1,0:T(8,128)(2,1)S(1)} %pad_maximum_fusion.refs_1_.refs_0_, bf16[4,768,128]{2,1,0:T(8,128)(2,1)} %bitcast.2.refs_1_.refs_2_, bf16[4,768,128]{2,1,0:T(8,128)(2,1)} %collective-permute-done.1.refs_2_.refs_3_), custom_call_target="tpu_custom_call" | custom-call | flops 905969664 | bytes 4328448 | tf_op jit(solution)/shard_map/pallas_call | solution.py:47
  156.9 0.0 collective-permute-done.2.refs_0_
  157.0 0.0 collective-permute-done.3.refs_3_
  157.0 0.0 collective-permute-done.4.refs_5_
  157.0 3.4 %shard_map.82 = (bf16[256,768]{1,0:T(8,128)(2,1)S(1)}, f32[256,768]{1,0:T(8,128)S(1)}, bf16[768,768]{1,0:T(8,128)(2,1)S(1)}) custom-call(bf16[128,768]{1,0:T(8,128)(2,1)S(1)} %collective-permute-done.2.refs_0_, bf16[128,768]{1,0:T(8,128)(2,1)S(1)} %get-tuple-element.15.refs_1_.refs_2_, bf16[128,768]{1,0:T(8,128)(2,1)S(1)} %get-tuple-element.16.refs_2_.refs_3_, ...), custom_call_target="tpu_custom_call" | custom-call | flops 905969664 | bytes 7864320 | tf_op jit(solution)/shard_map/pallas_call | solution.py:47
  160.3 0.0 collective-permute-done.9.refs_1_
  160.3 3.6 %collective-permute-done.8.refs_0_ = bf16[2,128,384]{2,1,0:T(8,128)(2,1)S(1)} collective-permute-done((bf16[2,128,384]{2,1,0:T(8,128)(2,1)S(1)}, bf16[2,128,384]{2,1,0:T(8,128)(2,1)S(1)}, u32[]{:S(2)}, u32[]{:S(2)}) %collective-permute-start.8) | collective-permute-done | bytes 196640 | tf_op jit(solution)/shard_map/ppermute | solution.py:24
  164.0 1.1 shard_map.84
  165.0 37.2 %collective-permute-start.11 = (bf16[128,768]{1,0:T(8,128)(2,1)S(1)}, bf16[128,768]{1,0:T(8,128)(2,1)S(1)}, u32[]{:S(2)}, u32[]{:S(2)}) collective-permute-start(bf16[128,768]{1,0:T(8,128)(2,1)S(1)} %get-tuple-element.23.refs_2_), channel_id=1, source_target_pairs={{8,16},{24,32},{40,48},{56,64},{72,80},{88,96},{104,112},{120,128}... | collective-permute-start | bytes 589832 | tf_op jit(solution)/shard_map/ppermute | solution.py:20
  202.3 1.9 collective-permute-start.10
  204.2 3.1 %shard_map.85 = bf16[256,1536]{1,0:T(8,128)(2,1)} custom-call(bf16[256,1536]{1,0:T(8,128)(2,1)S(1)} %bitcast.23, bf16[256,768]{1,0:T(8,128)(2,1)S(1)} %get-tuple-element.17.refs_1_, bf16[128,768]{1,0:T(8,128)(2,1)S(1)} %get-tuple-element.15.refs_1_.refs_2_, bf16[128,768]{1,0:T(8,128)(2,1)S(1)} %get-tuple-element.16.refs_2_.refs_3_, ...), custom_call_target="tpu_custom_call" | custom-call | flops 301989888 | bytes 7274496 | tf_op jit(solution)/shard_map/pallas_call | solution.py:47
  207.4 0.0 collective-permute-done.11.refs_1_
  207.4 3.0 %shard_map.86 = (bf16[128,768]{1,0:T(8,128)(2,1)S(1)}, f32[128,768]{1,0:T(8,128)S(1)}, bf16[768,768]{1,0:T(8,128)(2,1)S(1)}) custom-call(bf16[4,256,384]{2,1,0:T(8,128)(2,1)S(1)} %pad_maximum_fusion.refs_1_.refs_0_, bf16[128,768]{1,0:T(8,128)(2,1)S(1)} %collective-permute-done.11.refs_1_, bf16[128,768]{1,0:T(8,128)(2,1)S(1)} %get-tuple-element.23.refs_2_, ...), custom_call_target="tpu_custom_call" | custom-call | flops 754974720 | bytes 7864320 | tf_op jit(solution)/shard_map/pallas_call | solution.py:47
  210.3 0.0 collective-permute-done.10.refs_0_
  210.3 1.2 shard_map.87
  (1 shorter events, 0.0 us)
Async XLA Ops:
  70.2 26.6 %copy-start = (bf16[1,1,256,1536]{3,2,1,0:T(8,128)(2,1)S(1)}, bf16[1,1,256,1536]{3,2,1,0:T(8,128)(2,1)}, u32[]{:S(2)}) copy-start(bf16[1,1,256,1536]{3,2,1,0:T(8,128)(2,1)} %param.6) | copy-start | bytes 2359300
  70.2 42.4 %copy-start.1 = (s32[768]{0:T(1024)S(1)}, s32[768]{0:T(1024)}, u32[]{:S(2)}) copy-start(s32[768]{0:T(1024)} %param.11) | copy-start | bytes 9220
  70.2 86.8 %collective-permute-start.4 = (bf16[4,768,384]{2,1,0:T(8,128)(2,1)S(1)}, bf16[4,768,384]{2,1,0:T(8,128)(2,1)}, u32[]{:S(2)}, u32[]{:S(2)}) collective-permute-start(bf16[4,768,384]{2,1,0:T(8,128)(2,1)S(1)} %bitcast.17), channel_id=1, source_target_pairs={{0,8},{8,0},{16,24},{24,16},{32,40},{40,32},{48,56},{56,48},{64,72... | collective-permute-start | bytes 7077896 | tf_op jit(solution)/shard_map/ppermute | solution.py:20
  89.0 40.0 %collective-permute-start.1 = (bf16[4,768,128]{2,1,0:T(8,128)(2,1)}, bf16[4,768,128]{2,1,0:T(8,128)(2,1)}, u32[]{:S(2)}, u32[]{:S(2)}) collective-permute-start(bf16[4,768,128]{2,1,0:T(8,128)(2,1)} %bitcast.2.refs_1_.refs_2_), channel_id=1, source_target_pairs={{0,8},{8,0},{16,24},{24,16},{32,40},{40,32},{48,56},{56,48},{64,72... | collective-permute-start | bytes 2359304 | tf_op jit(solution)/shard_map/ppermute | solution.py:20
  94.8 13.8 %collective-permute-start.5 = (bf16[256,384]{1,0:T(8,128)(2,1)S(1)}, bf16[256,384]{1,0:T(8,128)(2,1)}, u32[]{:S(2)}, u32[]{:S(2)}) collective-permute-start(bf16[256,384]{1,0:T(8,128)(2,1)S(1)} %get-tuple-element.31), channel_id=1, source_target_pairs={{0,1},{1,0},{2,3},{3,2},{4,5},{5,4},{6,7},{7,6},{8,9},{9,8},{10,11... | collective-permute-start | bytes 589832 | tf_op jit(solution)/shard_map/ppermute | solution.py:245
  97.5 30.9 %collective-permute-start = (bf16[256,768]{1,0:T(8,128)(2,1)}, bf16[256,768]{1,0:T(8,128)(2,1)S(1)}, u32[]{:S(2)}, u32[]{:S(2)}) collective-permute-start(bf16[256,768]{1,0:T(8,128)(2,1)} %slice.4), channel_id=1, source_target_pairs={{0,4},{4,0},{1,5},{5,1},{2,6},{6,2},{3,7},{7,3},{8,12},{12,8},{9,1... | collective-permute-start | bytes 1179656 | tf_op jit(solution)/shard_map/ppermute | solution.py:24
  105.5 9.4 %collective-permute-start.7 = (bf16[256,384]{1,0:T(8,128)(2,1)}, bf16[256,384]{1,0:T(8,128)(2,1)}, u32[]{:S(2)}, u32[]{:S(2)}) collective-permute-start(bf16[256,384]{1,0:T(8,128)(2,1)} %get-tuple-element.32), channel_id=1, source_target_pairs={{0,3},{1,2},{2,1},{3,0},{4,7},{5,6},{6,5},{7,4},{8,11},{9,10},{10,... | collective-permute-start | bytes 589832 | tf_op jit(solution)/shard_map/ppermute | solution.py:245
  108.6 9.4 %collective-permute-start.6 = (bf16[256,384]{1,0:T(8,128)(2,1)}, bf16[256,384]{1,0:T(8,128)(2,1)}, u32[]{:S(2)}, u32[]{:S(2)}) collective-permute-start(bf16[256,384]{1,0:T(8,128)(2,1)} %get-tuple-element.33), channel_id=1, source_target_pairs={{0,2},{1,3},{2,0},{3,1},{4,6},{5,7},{6,4},{7,5},{8,10},{9,11},{10,... | collective-permute-start | bytes 589832 | tf_op jit(solution)/shard_map/ppermute | solution.py:245
  132.2 24.8 %collective-permute-start.2 = (bf16[128,768]{1,0:T(8,128)(2,1)S(1)}, bf16[128,768]{1,0:T(8,128)(2,1)S(1)}, u32[]{:S(2)}, u32[]{:S(2)}) collective-permute-start(bf16[128,768]{1,0:T(8,128)(2,1)S(1)} %get-tuple-element.15.refs_1_.refs_2_), channel_id=1, source_target_pairs={{8,16},{24,32},{40,48},{56,64},{72,80},{88,96},{104,112},{120,128}... | collective-permute-start | bytes 589832 | tf_op jit(solution)/shard_map/ppermute | solution.py:20
  136.5 20.5 %collective-permute-start.3 = (bf16[128,768]{1,0:T(8,128)(2,1)S(1)}, bf16[128,768]{1,0:T(8,128)(2,1)S(1)}, u32[]{:S(2)}, u32[]{:S(2)}) collective-permute-start(bf16[128,768]{1,0:T(8,128)(2,1)S(1)} %get-tuple-element.16.refs_2_.refs_3_), channel_id=1, source_target_pairs={{0,8},{8,0},{16,24},{24,16},{32,40},{40,32},{48,56},{56,48},{64,72... | collective-permute-start | bytes 589832 | tf_op jit(solution)/shard_map/ppermute | solution.py:20
  139.1 21.2 %collective-permute-start.9 = (bf16[2,128,384]{2,1,0:T(8,128)(2,1)S(1)}, bf16[2,128,384]{2,1,0:T(8,128)(2,1)S(1)}, u32[]{:S(2)}, u32[]{:S(2)}) collective-permute-start(bf16[2,128,384]{2,1,0:T(8,128)(2,1)S(1)} %get-tuple-element.28), channel_id=1, source_target_pairs={{0,4},{4,0},{1,5},{5,1},{2,6},{6,2},{3,7},{7,3},{8,12},{12,8},{9,1... | collective-permute-start | bytes 589832 | tf_op jit(solution)/shard_map/ppermute | solution.py:24
  147.1 16.8 %collective-permute-start.8 = (bf16[2,128,384]{2,1,0:T(8,128)(2,1)S(1)}, bf16[2,128,384]{2,1,0:T(8,128)(2,1)S(1)}, u32[]{:S(2)}, u32[]{:S(2)}) collective-permute-start(bf16[2,128,384]{2,1,0:T(8,128)(2,1)S(1)} %get-tuple-element.29), channel_id=1, source_target_pairs={{0,4},{4,0},{1,5},{5,1},{2,6},{6,2},{3,7},{7,3},{8,12},{12,8},{9,1... | collective-permute-start | bytes 589832 | tf_op jit(solution)/shard_map/ppermute | solution.py:24
  165.0 42.3 %collective-permute-start.11 = (bf16[128,768]{1,0:T(8,128)(2,1)S(1)}, bf16[128,768]{1,0:T(8,128)(2,1)S(1)}, u32[]{:S(2)}, u32[]{:S(2)}) collective-permute-start(bf16[128,768]{1,0:T(8,128)(2,1)S(1)} %get-tuple-element.23.refs_2_), channel_id=1, source_target_pairs={{8,16},{24,32},{40,48},{56,64},{72,80},{88,96},{104,112},{120,128}... | collective-permute-start | bytes 589832 | tf_op jit(solution)/shard_map/ppermute | solution.py:20
  202.3 8.0 %collective-permute-start.10 = (bf16[128,768]{1,0:T(8,128)(2,1)S(1)}, bf16[128,768]{1,0:T(8,128)(2,1)S(1)}, u32[]{:S(2)}, u32[]{:S(2)}) collective-permute-start(bf16[128,768]{1,0:T(8,128)(2,1)S(1)} %get-tuple-element.22.refs_6_.refs_3_), channel_id=1, source_target_pairs={{0,8},{8,0},{16,24},{24,16},{32,40},{40,32},{48,56},{56,48},{64,72... | collective-permute-start | bytes 589832 | tf_op jit(solution)/shard_map/ppermute | solution.py:20

commit v5 on v4

--- a/solution.py
+++ b/solution.py
@@ -9,6 +9,7 @@
 
 BF16, F32 = jnp.bfloat16, jnp.float32
 LANES = 128
+LATE = 192
 
 
 def pairwise(value, bit):
@@ -187,36 +188,35 @@
         inner[...] = (pulled[:rows] * slope[rows:, :]).astype(BF16)
 
 
-def gather(core, grads, beyond, edge, inner, own, other, result, rest, near):
+def gather(core, grads, edge, inner, own, other, edge_rest, inner_rest, near, far):
     c = core[0]
     rows, half = edge.shape
     wide = half // 2
-    head = core[1]
     total = jnp.zeros((2 * rows, half), F32)
     low = jnp.zeros((rows, half), F32)
+    high = jnp.zeros((rows, half), F32)
     for place, taps in ((c, own), (1 - c, other)):
         lane = at(place * wide, wide)
         e, i = edge[:, lane], inner[:, lane]
         total += dot_t(jnp.concatenate([e, i], axis=0), taps[1])
-        total += dot_t(jnp.concatenate([beyond[:, lane], e], axis=0), taps[2 - 2 * c])
         low += dot_t(i, taps[2 * c])
+        high += dot_t(e, taps[2 - 2 * c])
         near[lane, :] = taps[2 * c].T
-    lines = (at(c * rows, rows), at((1 - c) * rows, rows))
-    plain = [
-        jnp.concatenate([grads[head ^ 2, line, :], grads[head ^ 3, line, :]], axis=1).astype(F32)
-        for line in lines
-    ]
-    result[...] = (plain[0] + total[:rows] + low).astype(BF16)
-    rest[...] = plain[1] + total[rows:]
-
-
-def finish(core, across, near, cot, edge_b, rest, result):
-    c = core[0]
-    rows = edge_b.shape[0]
-    half = cot.shape[1]
+        far[lane, :] = taps[2 - 2 * c].T
+    first, second = (
+        jnp.concatenate([grads[core[1] ^ 2, line, :], grads[core[1] ^ 3, line, :]], axis=1).astype(F32)
+        for line in (at(c * rows, rows), at((1 - c) * rows, rows))
+    )
+    edge_rest[...] = first + total[:rows] + low
+    inner_rest[...] = second + total[rows:] + high
+
+
+def finish(core, across, beyond, near, far, cot, edge_rest, inner_rest, result):
+    c = core[0]
+    rows, half = edge_rest.shape
     result[:, :half] = cot[...]
-    result[at(c * rows, rows), half:] = edge_b[...]
-    result[at((1 - c) * rows, rows), half:] = (rest[...] + dot(across[...], near[...])).astype(BF16)
+    result[at(c * rows, rows), half:] = (edge_rest[...] + dot(beyond[...], far[...])).astype(BF16)
+    result[at((1 - c) * rows, rows), half:] = (inner_rest[...] + dot(across[...], near[...])).astype(BF16)
 
 
 def shards(top, grad_heads, tap_weight_grid, out_w, mix_w, rc_perm):
@@ -246,9 +246,9 @@
     grads = jnp.stack(grads)
 
     go = []
-    for k in range(2):
-        start = (2 - (head // 2) * 2, k * rows, 0)
-        go.append(mirrored(lax.dynamic_slice(grads, start, (2, rows, half // 2))))
+    for first, count in ((0, 2 * rows - LATE), (2 * rows - LATE, LATE)):
+        start = (2 - (head // 2) * 2, first, 0)
+        go.append(mirrored(lax.dynamic_slice(grads, start, (2, count, half // 2))))
     plane = [
         [h * 2 * lines * ranks + (y * lines + z) * 2 + c for h in range(heads) for y in range(ranks)]
         for z in range(lines)
@@ -307,17 +307,17 @@
         (shape(top.shape, BF16),),
         2 * unit,
     )
-    edge_b, rest, near = call(
+    edge_rest, inner_rest, near, far = call(
         gather,
-        (grads, cot_beyond, held_edge, held_inner, mine, theirs),
-        (shape(chunk, BF16), shape(chunk, F32), shape(square, BF16)),
-        5 * unit,
+        (grads, held_edge, held_inner, mine, theirs),
+        (shape(chunk, F32), shape(chunk, F32), shape(square, BF16), shape(square, BF16)),
+        4 * unit,
     )
     (result,) = call(
         finish,
-        (cot_across, near, cot, edge_b, rest),
+        (cot_across, cot_beyond, near, far, cot, edge_rest, inner_rest),
         (shape(top.shape, BF16),),
-        unit,
+        2 * unit,
     )
     return restored[None, None], result[None, None]
 

time: 212 us -> 214 us (level)
  waiting for transfers between devices: 18.2 us -> 31 us
  starting transfers between devices: 82.7 us -> 71.9 us
    ppermute x6, waiting for transfers between devices: 0.02 us -> 16 us  [pairwise(): return lax.ppermute(value, 'seq', pairs)]
    ppermute x6, starting transfers between devices: 51.8 us -> 39.4 us  [pairwise(): return lax.ppermute(value, 'seq', pairs)]
    ppermute x3, waiting for transfers between devices: 5.45 us -> 0.01 us  [shards(): lax.ppermute(blocks[k], 'head', [(i, i ^ k) for i in range(heads)])]
    ppermute x3, waiting for transfers between devices: 12.7 us -> 15 us  [mirrored(): return lax.ppermute(value, 'strand', [(0, 1), (1, 0)])]
  transfers between devices with their start and end apart: 12 -> 12, of which waited for: 4 -> 2; matrix products, arithmetic and copies ran while one was open for 2% -> 2% of each run, Pallas kernels for 8% -> 8%
where the time goes in v5:
time: 214 us
  blocking collectives  84.4 us (39%)
  starting transfers between devices  71.9 us (34%)
  waiting for transfers between devices  31 us (14%)
  Pallas kernels  21.2 us (10%)
  local copies, waits for them, and re-layouts  2.9 us (1%)
    all_to_all x2, blocking collectives, planar(): lax.all_to_all(sent, ('head', 'seq'), 0, 0, axis_index_groups=plane, tile...  53.3 us
    ppermute x6, starting transfers between devices, pairwise(): return lax.ppermute(value, 'seq', pairs)  39.4 us
    all_to_all x1, blocking collectives, shards(): lax.all_to_all(sent.reshape(2 * lines, *sent.shape[2:]), 'seq', 0, 0, axi...  31 us
    ppermute x3, starting transfers between devices, mirrored(): return lax.ppermute(value, 'strand', [(0, 1), (1, 0)])  23.5 us
    pallas_call x11, Pallas kernels, call(): pl.pallas_call(body, out_shape=outs, in_specs=[pl.BlockSpec(memory_space=...  21.2 us
    ppermute x6, waiting for transfers between devices, pairwise(): return lax.ppermute(value, 'seq', pairs)  16 us
    ppermute x3, waiting for transfers between devices, mirrored(): return lax.ppermute(value, 'strand', [(0, 1), (1, 0)])  15 us
    ppermute x3, starting transfers between devices, shards(): lax.ppermute(blocks[k], 'head', [(i, i ^ k) for i in range(heads)])  8.97 us
  transfers between devices with their start and end apart: 12, of which 2 were waited for; matrix products, arithmetic and copies ran while one was open for 2% of the time, Pallas kernels for 8%

profile of v5, /device:TPU:1, one launch (start us, length us, event | category | flops | bytes accessed | tf_op | source)
XLA Modules:
  0.0 213.6 jit_solution(4754133710884260064)
XLA Ops:
  0.6 1.6 shard_map.78
  2.3 31.0 %all_to_all.15.refs_0_ = bf16[16,12,512]{2,1,0:T(8,128)(2,1)S(1)} all-to-all(bf16[16,12,512]{2,1,0:T(8,128)(2,1)} %bitcast.24), channel_id=1, replica_groups={{0,8,16,24,32,40,48,56,64,72,80,88,96,104,112,120},{128,136,144,152,160..., dimensions={0} | all-to-all | bytes 393216 | tf_op jit(solution)/shard_map/all_to_all | solution.py:240
  33.3 0.2 shard_map.81
  33.5 36.7 %all_to_all.16 = bf16[16,8,24,384]{3,2,1,0:T(8,128)(2,1)S(1)} all-to-all(bf16[16,8,24,384]{3,2,1,0:T(8,128)(2,1)S(1)} %shard_map.81), channel_id=1, replica_groups={{0,128,256,384,1,129,257,385,2,130,258,386,3,131,259,387},{8,136,264,39..., dimensions={0} | all-to-all | bytes 4718592 | tf_op jit(solution)/shard_map/all_to_all | solution.py:266
  70.2 1.9 collective-permute-start.4
  72.1 0.1 shard_map.79
  72.2 16.7 %all_to_all.17 = bf16[16,8,24,128]{3,2,1,0:T(8,128)(2,1)} all-to-all(bf16[16,8,24,128]{3,2,1,0:T(8,128)(2,1)S(1)} %shard_map.79), channel_id=1, replica_groups={{0,128,256,384,1,129,257,385,2,130,258,386,3,131,259,387},{8,136,264,39..., dimensions={0} | all-to-all | bytes 1572864 | tf_op jit(solution)/shard_map/all_to_all | solution.py:266
  88.9 0.0 copy-start
  88.9 3.9 %collective-permute-start.1 = (bf16[4,768,128]{2,1,0:T(8,128)(2,1)}, bf16[4,768,128]{2,1,0:T(8,128)(2,1)}, u32[]{:S(2)}, u32[]{:S(2)}) collective-permute-start(bf16[4,768,128]{2,1,0:T(8,128)(2,1)} %bitcast.2.refs_1_.refs_2_), channel_id=1, source_target_pairs={{0,8},{8,0},{16,24},{24,16},{32,40},{40,32},{48,56},{56,48},{64,72... | collective-permute-start | bytes 2359304 | tf_op jit(solution)/shard_map/ppermute | solution.py:21
  92.8 0.0 copy-start.1
  92.8 2.1 dynamic-slice_bitcast_fusion.3
  94.9 1.9 collective-permute-start.5
  96.8 3.1 %collective-permute-start.7 = (bf16[256,384]{1,0:T(8,128)(2,1)}, bf16[256,384]{1,0:T(8,128)(2,1)}, u32[]{:S(2)}, u32[]{:S(2)}) collective-permute-start(bf16[256,384]{1,0:T(8,128)(2,1)} %get-tuple-element.32), channel_id=1, source_target_pairs={{0,3},{1,2},{2,1},{3,0},{4,7},{5,6},{6,5},{7,4},{8,11},{9,10},{10,... | collective-permute-start | bytes 589832 | tf_op jit(solution)/shard_map/ppermute | solution.py:245
  99.9 3.9 %collective-permute-start.6 = (bf16[256,384]{1,0:T(8,128)(2,1)}, bf16[256,384]{1,0:T(8,128)(2,1)}, u32[]{:S(2)}, u32[]{:S(2)}) collective-permute-start(bf16[256,384]{1,0:T(8,128)(2,1)} %get-tuple-element.33), channel_id=1, source_target_pairs={{0,2},{1,3},{2,0},{3,1},{4,6},{5,7},{6,4},{7,5},{8,10},{9,11},{10,... | collective-permute-start | bytes 589832 | tf_op jit(solution)/shard_map/ppermute | solution.py:245
  103.9 0.0 copy-done
  103.9 0.8 slice.4
  104.6 0.0 collective-permute-done.5
  104.6 7.9 %collective-permute-start = (bf16[256,768]{1,0:T(8,128)(2,1)}, bf16[256,768]{1,0:T(8,128)(2,1)S(1)}, u32[]{:S(2)}, u32[]{:S(2)}) collective-permute-start(bf16[256,768]{1,0:T(8,128)(2,1)} %slice.4), channel_id=1, source_target_pairs={{0,4},{4,0},{1,5},{5,1},{2,6},{6,2},{3,7},{7,3},{8,12},{12,8},{9,1... | collective-permute-start | bytes 1179656 | tf_op jit(solution)/shard_map/ppermute | solution.py:25
  112.6 0.0 copy-done.1
  112.6 0.0 collective-permute-done.7
  112.6 0.0 collective-permute-done.6
  112.6 1.3 pad_maximum_fusion.refs_1_.refs_0_
  114.0 6.1 %collective-permute-start.9 = (bf16[2,192,384]{2,1,0:T(8,128)(2,1)S(1)}, bf16[2,192,384]{2,1,0:T(8,128)(2,1)S(1)}, u32[]{:S(2)}, u32[]{:S(2)}) collective-permute-start(bf16[2,192,384]{2,1,0:T(8,128)(2,1)S(1)} %constant_dynamic-slice_fusion), channel_id=1, source_target_pairs={{0,4},{4,0},{1,5},{5,1},{2,6},{6,2},{3,7},{7,3},{8,12},{12,8},{9,1... | collective-permute-start | bytes 884744 | tf_op jit(solution)/shard_map/ppermute | solution.py:25
  120.1 14.9 %collective-permute-done.refs_2_ = bf16[256,768]{1,0:T(8,128)(2,1)S(1)} collective-permute-done((bf16[256,768]{1,0:T(8,128)(2,1)}, bf16[256,768]{1,0:T(8,128)(2,1)S(1)}, u32[]{:S(2)}, u32[]{:S(2)}) %collective-permute-start) | collective-permute-done | bytes 393248 | tf_op jit(solution)/shard_map/ppermute | solution.py:25
  135.0 0.5 shard_map.77.refs_0_
  135.6 0.0 collective-permute-done.1.refs_2_.refs_3_
  135.6 3.1 %shard_map.80 = (bf16[128,768]{1,0:T(8,128)(2,1)S(1)}, bf16[128,768]{1,0:T(8,128)(2,1)S(1)}) custom-call(bf16[2,256,768]{2,1,0:T(8,128)(2,1)S(1)} %shard_map.77.refs_0_, bf16[4,768,128]{2,1,0:T(8,128)(2,1)} %bitcast.2.refs_1_.refs_2_, bf16[4,768,128]{2,1,0:T(8,128)(2,1)} %collective-permute-done.1.refs_2_.refs_3_), custom_call_target="tpu_custom_call" | custom-call | flops 301989888 | bytes 2752512 | tf_op jit(solution)/shard_map/pallas_call | solution.py:48
  138.7 8.4 %collective-permute-start.2 = (bf16[128,768]{1,0:T(8,128)(2,1)S(1)}, bf16[128,768]{1,0:T(8,128)(2,1)S(1)}, u32[]{:S(2)}, u32[]{:S(2)}) collective-permute-start(bf16[128,768]{1,0:T(8,128)(2,1)S(1)} %get-tuple-element.16.refs_1_.refs_2_), channel_id=1, source_target_pairs={{8,16},{24,32},{40,48},{56,64},{72,80},{88,96},{104,112},{120,128}... | collective-permute-start | bytes 589832 | tf_op jit(solution)/shard_map/ppermute | solution.py:21
  147.2 1.9 collective-permute-start.3
  149.1 9.5 %collective-permute-start.8 = (bf16[2,64,384]{2,1,0:T(8,128)(2,1)S(1)}, bf16[2,64,384]{2,1,0:T(8,128)(2,1)S(1)}, u32[]{:S(2)}, u32[]{:S(2)}) collective-permute-start(bf16[2,64,384]{2,1,0:T(8,128)(2,1)S(1)} %constant_dynamic-slice_fusion.1), channel_id=1, source_target_pairs={{0,4},{4,0},{1,5},{5,1},{2,6},{6,2},{3,7},{7,3},{8,12},{12,8},{9,1... | collective-permute-start | bytes 294920 | tf_op jit(solution)/shard_map/ppermute | solution.py:25
  158.6 3.8 %shard_map.83 = (bf16[768,768]{1,0:T(8,128)(2,1)S(1)}, f32[256,768]{1,0:T(8,128)S(1)}) custom-call(s32[1,768]{1,0:T(1,128)S(1)} %broadcast_in_dim.9.refs_0_, bf16[4,256,384]{2,1,0:T(8,128)(2,1)S(1)} %pad_maximum_fusion.refs_1_.refs_0_, bf16[4,768,128]{2,1,0:T(8,128)(2,1)} %bitcast.2.refs_1_.refs_2_, bf16[4,768,128]{2,1,0:T(8,128)(2,1)} %collective-permute-done.1.refs_2_.refs_3_), custom_call_target="tpu_custom_call" | custom-call | flops 905969664 | bytes 4328448 | tf_op jit(solution)/shard_map/pallas_call | solution.py:48
  162.4 16.0 %collective-permute-done.2.refs_0_ = bf16[128,768]{1,0:T(8,128)(2,1)S(1)} collective-permute-done((bf16[128,768]{1,0:T(8,128)(2,1)S(1)}, bf16[128,768]{1,0:T(8,128)(2,1)S(1)}, u32[]{:S(2)}, u32[]{:S(2)}) %collective-permute-start.2) | collective-permute-done | bytes 196640 | tf_op jit(solution)/shard_map/ppermute | solution.py:21
  178.4 0.0 collective-permute-done.3.refs_3_
  178.4 0.0 collective-permute-done.4.refs_5_.refs_4_
  178.4 3.4 %shard_map.82 = (bf16[256,768]{1,0:T(8,128)(2,1)S(1)}, f32[256,768]{1,0:T(8,128)S(1)}, bf16[768,768]{1,0:T(8,128)(2,1)S(1)}) custom-call(bf16[128,768]{1,0:T(8,128)(2,1)S(1)} %collective-permute-done.2.refs_0_, bf16[128,768]{1,0:T(8,128)(2,1)S(1)} %get-tuple-element.16.refs_1_.refs_2_, bf16[128,768]{1,0:T(8,128)(2,1)S(1)} %get-tuple-element.17.refs_2_.refs_3_, ...), custom_call_target="tpu_custom_call" | custom-call | flops 905969664 | bytes 7864320 | tf_op jit(solution)/shard_map/pallas_call | solution.py:48
  181.8 0.0 collective-permute-done.8.refs_0_
  181.8 0.0 collective-permute-done.9.refs_1_
  181.8 1.1 shard_map.84
  182.9 21.4 %collective-permute-start.11 = (bf16[128,768]{1,0:T(8,128)(2,1)S(1)}, bf16[128,768]{1,0:T(8,128)(2,1)S(1)}, u32[]{:S(2)}, u32[]{:S(2)}) collective-permute-start(bf16[128,768]{1,0:T(8,128)(2,1)S(1)} %get-tuple-element.24.refs_1_), channel_id=1, source_target_pairs={{8,16},{24,32},{40,48},{56,64},{72,80},{88,96},{104,112},{120,128}... | collective-permute-start | bytes 589832 | tf_op jit(solution)/shard_map/ppermute | solution.py:21
  204.3 1.9 collective-permute-start.10
  206.2 3.1 %shard_map.85 = bf16[256,1536]{1,0:T(8,128)(2,1)} custom-call(bf16[256,1536]{1,0:T(8,128)(2,1)S(1)} %bitcast.23, bf16[256,768]{1,0:T(8,128)(2,1)S(1)} %get-tuple-element.18.refs_1_, bf16[128,768]{1,0:T(8,128)(2,1)S(1)} %get-tuple-element.16.refs_1_.refs_2_, bf16[128,768]{1,0:T(8,128)(2,1)S(1)} %get-tuple-element.17.refs_2_.refs_3_, ...), custom_call_target="tpu_custom_call" | custom-call | flops 301989888 | bytes 7274496 | tf_op jit(solution)/shard_map/pallas_call | solution.py:48
  209.4 2.9 %shard_map.86 = (f32[128,768]{1,0:T(8,128)S(1)}, f32[128,768]{1,0:T(8,128)S(1)}, bf16[768,768]{1,0:T(8,128)(2,1)S(1)}, bf16[768,768]{1,0:T(8,128)(2,1)S(1)}) custom-call(bf16[4,256,384]{2,1,0:T(8,128)(2,1)S(1)} %pad_maximum_fusion.refs_1_.refs_0_, bf16[128,768]{1,0:T(8,128)(2,1)S(1)} %get-tuple-element.24.refs_1_, ...), custom_call_target="tpu_custom_call" | custom-call | flops 603979776 | bytes 9043968 | tf_op jit(solution)/shard_map/pallas_call | solution.py:48
  212.2 0.0 collective-permute-done.11.refs_1_
  212.2 0.0 collective-permute-done.10.refs_0_
  212.2 1.4 shard_map.87
  (3 shorter events, 0.1 us)
Async XLA Ops:
  70.2 108.2 %collective-permute-start.4 = (bf16[4,768,384]{2,1,0:T(8,128)(2,1)S(1)}, bf16[4,768,384]{2,1,0:T(8,128)(2,1)}, u32[]{:S(2)}, u32[]{:S(2)}) collective-permute-start(bf16[4,768,384]{2,1,0:T(8,128)(2,1)S(1)} %bitcast.17), channel_id=1, source_target_pairs={{0,8},{8,0},{16,24},{24,16},{32,40},{40,32},{48,56},{56,48},{64,72... | collective-permute-start | bytes 7077896 | tf_op jit(solution)/shard_map/ppermute | solution.py:21
  88.9 14.9 %copy-start = (bf16[1,1,256,1536]{3,2,1,0:T(8,128)(2,1)S(1)}, bf16[1,1,256,1536]{3,2,1,0:T(8,128)(2,1)}, u32[]{:S(2)}) copy-start(bf16[1,1,256,1536]{3,2,1,0:T(8,128)(2,1)} %param.6) | copy-start | bytes 2359300
  88.9 46.7 %collective-permute-start.1 = (bf16[4,768,128]{2,1,0:T(8,128)(2,1)}, bf16[4,768,128]{2,1,0:T(8,128)(2,1)}, u32[]{:S(2)}, u32[]{:S(2)}) collective-permute-start(bf16[4,768,128]{2,1,0:T(8,128)(2,1)} %bitcast.2.refs_1_.refs_2_), channel_id=1, source_target_pairs={{0,8},{8,0},{16,24},{24,16},{32,40},{40,32},{48,56},{56,48},{64,72... | collective-permute-start | bytes 2359304 | tf_op jit(solution)/shard_map/ppermute | solution.py:21
  92.8 19.8 %copy-start.1 = (s32[768]{0:T(1024)S(1)}, s32[768]{0:T(1024)}, u32[]{:S(2)}) copy-start(s32[768]{0:T(1024)} %param.11) | copy-start | bytes 9220
  94.9 9.8 %collective-permute-start.5 = (bf16[256,384]{1,0:T(8,128)(2,1)S(1)}, bf16[256,384]{1,0:T(8,128)(2,1)}, u32[]{:S(2)}, u32[]{:S(2)}) collective-permute-start(bf16[256,384]{1,0:T(8,128)(2,1)S(1)} %get-tuple-element.31), channel_id=1, source_target_pairs={{0,1},{1,0},{2,3},{3,2},{4,5},{5,4},{6,7},{7,6},{8,9},{9,8},{10,11... | collective-permute-start | bytes 589832 | tf_op jit(solution)/shard_map/ppermute | solution.py:245
  96.8 15.8 %collective-permute-start.7 = (bf16[256,384]{1,0:T(8,128)(2,1)}, bf16[256,384]{1,0:T(8,128)(2,1)}, u32[]{:S(2)}, u32[]{:S(2)}) collective-permute-start(bf16[256,384]{1,0:T(8,128)(2,1)} %get-tuple-element.32), channel_id=1, source_target_pairs={{0,3},{1,2},{2,1},{3,0},{4,7},{5,6},{6,5},{7,4},{8,11},{9,10},{10,... | collective-permute-start | bytes 589832 | tf_op jit(solution)/shard_map/ppermute | solution.py:245
  99.9 12.7 %collective-permute-start.6 = (bf16[256,384]{1,0:T(8,128)(2,1)}, bf16[256,384]{1,0:T(8,128)(2,1)}, u32[]{:S(2)}, u32[]{:S(2)}) collective-permute-start(bf16[256,384]{1,0:T(8,128)(2,1)} %get-tuple-element.33), channel_id=1, source_target_pairs={{0,2},{1,3},{2,0},{3,1},{4,6},{5,7},{6,4},{7,5},{8,10},{9,11},{10,... | collective-permute-start | bytes 589832 | tf_op jit(solution)/shard_map/ppermute | solution.py:245
  104.6 30.4 %collective-permute-start = (bf16[256,768]{1,0:T(8,128)(2,1)}, bf16[256,768]{1,0:T(8,128)(2,1)S(1)}, u32[]{:S(2)}, u32[]{:S(2)}) collective-permute-start(bf16[256,768]{1,0:T(8,128)(2,1)} %slice.4), channel_id=1, source_target_pairs={{0,4},{4,0},{1,5},{5,1},{2,6},{6,2},{3,7},{7,3},{8,12},{12,8},{9,1... | collective-permute-start | bytes 1179656 | tf_op jit(solution)/shard_map/ppermute | solution.py:25
  114.0 67.8 %collective-permute-start.9 = (bf16[2,192,384]{2,1,0:T(8,128)(2,1)S(1)}, bf16[2,192,384]{2,1,0:T(8,128)(2,1)S(1)}, u32[]{:S(2)}, u32[]{:S(2)}) collective-permute-start(bf16[2,192,384]{2,1,0:T(8,128)(2,1)S(1)} %constant_dynamic-slice_fusion), channel_id=1, source_target_pairs={{0,4},{4,0},{1,5},{5,1},{2,6},{6,2},{3,7},{7,3},{8,12},{12,8},{9,1... | collective-permute-start | bytes 884744 | tf_op jit(solution)/shard_map/ppermute | solution.py:25
  138.7 39.7 %collective-permute-start.2 = (bf16[128,768]{1,0:T(8,128)(2,1)S(1)}, bf16[128,768]{1,0:T(8,128)(2,1)S(1)}, u32[]{:S(2)}, u32[]{:S(2)}) collective-permute-start(bf16[128,768]{1,0:T(8,128)(2,1)S(1)} %get-tuple-element.16.refs_1_.refs_2_), channel_id=1, source_target_pairs={{8,16},{24,32},{40,48},{56,64},{72,80},{88,96},{104,112},{120,128}... | collective-permute-start | bytes 589832 | tf_op jit(solution)/shard_map/ppermute | solution.py:21
  147.2 31.2 %collective-permute-start.3 = (bf16[128,768]{1,0:T(8,128)(2,1)S(1)}, bf16[128,768]{1,0:T(8,128)(2,1)S(1)}, u32[]{:S(2)}, u32[]{:S(2)}) collective-permute-start(bf16[128,768]{1,0:T(8,128)(2,1)S(1)} %get-tuple-element.17.refs_2_.refs_3_), channel_id=1, source_target_pairs={{0,8},{8,0},{16,24},{24,16},{32,40},{40,32},{48,56},{56,48},{64,72... | collective-permute-start | bytes 589832 | tf_op jit(solution)/shard_map/ppermute | solution.py:21
  149.1 32.7 %collective-permute-start.8 = (bf16[2,64,384]{2,1,0:T(8,128)(2,1)S(1)}, bf16[2,64,384]{2,1,0:T(8,128)(2,1)S(1)}, u32[]{:S(2)}, u32[]{:S(2)}) collective-permute-start(bf16[2,64,384]{2,1,0:T(8,128)(2,1)S(1)} %constant_dynamic-slice_fusion.1), channel_id=1, source_target_pairs={{0,4},{4,0},{1,5},{5,1},{2,6},{6,2},{3,7},{7,3},{8,12},{12,8},{9,1... | collective-permute-start | bytes 294920 | tf_op jit(solution)/shard_map/ppermute | solution.py:25
  182.9 29.4 %collective-permute-start.11 = (bf16[128,768]{1,0:T(8,128)(2,1)S(1)}, bf16[128,768]{1,0:T(8,128)(2,1)S(1)}, u32[]{:S(2)}, u32[]{:S(2)}) collective-permute-start(bf16[128,768]{1,0:T(8,128)(2,1)S(1)} %get-tuple-element.24.refs_1_), channel_id=1, source_target_pairs={{8,16},{24,32},{40,48},{56,64},{72,80},{88,96},{104,112},{120,128}... | collective-permute-start | bytes 589832 | tf_op jit(solution)/shard_map/ppermute | solution.py:21
  204.3 8.0 %collective-permute-start.10 = (bf16[128,768]{1,0:T(8,128)(2,1)S(1)}, bf16[128,768]{1,0:T(8,128)(2,1)S(1)}, u32[]{:S(2)}, u32[]{:S(2)}) collective-permute-start(bf16[128,768]{1,0:T(8,128)(2,1)S(1)} %get-tuple-element.23.refs_6_.refs_2_), channel_id=1, source_target_pairs={{0,8},{8,0},{16,24},{24,16},{32,40},{40,32},{48,56},{56,48},{64,72... | collective-permute-start | bytes 589832 | tf_op jit(solution)/shard_map/ppermute | solution.py:21

commit v6 on v5

--- a/solution.py
+++ b/solution.py
@@ -81,21 +81,20 @@
         sent[k] = sent[0]
 
 
-def mirror_sum(core, perm, top, mirror, both):
-    half = both.shape[2]
+def mirror_sum(core, perm, top, mirror, paired):
+    half = paired.shape[1]
     hot = (lax.broadcasted_iota(jnp.int32, (half, half), 0) == perm[...]).astype(BF16)
-    both[0] = (top[:, :half].astype(F32) + dot(mirror[...], hot)).astype(BF16)
-    both[1] = top[:, half:]
-
-
-def restore(core, paired, own, other, edge, inner):
+    paired[...] = (top[:, :half].astype(F32) + dot(mirror[...], hot)).astype(BF16)
+
+
+def restore(core, top, paired, own, other, edge, inner):
     c = core[0]
     rows, half = edge.shape
     for k in range(half // (2 * LANES)):
         for place, pieces in ((c, own), (1 - c, other)):
             column = (2 * k + place) * LANES
-            mixing = dot(paired[0], pieces[k])
-            b = (paired[1, :, at(column, LANES)].astype(F32) - mixing).astype(BF16)
+            mixing = dot(paired[...], pieces[k])
+            b = (top[:, at(half + column, LANES)].astype(F32) - mixing).astype(BF16)
 
             @pl.when(c == 0)
             def _():
@@ -274,9 +273,9 @@
     unit = 2 * rows * half * half
     square, tall, chunk = (half, half), (2 * rows, half), (rows, half)
     perm = rc_perm[None, :]
-    (paired,) = call(mirror_sum, (perm, top, ao), (shape((2, *tall), BF16),), 2 * unit)
+    (paired,) = call(mirror_sum, (perm, top, ao), (shape(tall, BF16),), 2 * unit)
     edge, inner = call(
-        restore, (paired, mine_mix, theirs_mix), (shape(chunk, BF16), shape(chunk, BF16)), 2 * unit
+        restore, (top, paired, mine_mix, theirs_mix), (shape(chunk, BF16), shape(chunk, BF16)), 2 * unit
     )
     beyond = pairwise(edge, 1)
     across = pairwise(inner, 0)

time: 214 us -> 214 us (level)
  no operation moved by 1% of the time
where the time goes in v6:
time: 214 us
  blocking collectives  84.4 us (39%)
  starting transfers between devices  71.8 us (34%)
  waiting for transfers between devices  31 us (14%)
  Pallas kernels  21.2 us (10%)
  local copies, waits for them, and re-layouts  2.9 us (1%)
    all_to_all x2, blocking collectives, planar(): lax.all_to_all(sent, ('head', 'seq'), 0, 0, axis_index_groups=plane, tile...  53.3 us
    ppermute x6, starting transfers between devices, pairwise(): return lax.ppermute(value, 'seq', pairs)  39.4 us
    all_to_all x1, blocking collectives, shards(): lax.all_to_all(sent.reshape(2 * lines, *sent.shape[2:]), 'seq', 0, 0, axi...  31 us
    ppermute x3, starting transfers between devices, mirrored(): return lax.ppermute(value, 'strand', [(0, 1), (1, 0)])  23.5 us
    pallas_call x11, Pallas kernels, call(): pl.pallas_call(body, out_shape=outs, in_specs=[pl.BlockSpec(memory_space=...  21.2 us
    ppermute x6, waiting for transfers between devices, pairwise(): return lax.ppermute(value, 'seq', pairs)  16 us
    ppermute x3, waiting for transfers between devices, mirrored(): return lax.ppermute(value, 'strand', [(0, 1), (1, 0)])  15 us
    ppermute x3, starting transfers between devices, shards(): lax.ppermute(blocks[k], 'head', [(i, i ^ k) for i in range(heads)])  8.97 us
  transfers between devices with their start and end apart: 12, of which 2 were waited for; matrix products, arithmetic and copies ran while one was open for 2% of the time, Pallas kernels for 8%

profile of v6, /device:TPU:1, one launch (start us, length us, event | category | flops | bytes accessed | tf_op | source)
XLA Modules:
  0.0 213.6 jit_solution(8751582017551458261)
XLA Ops:
  0.6 1.6 shard_map.78
  2.3 31.0 %all_to_all.15.refs_0_ = bf16[16,12,512]{2,1,0:T(8,128)(2,1)S(1)} all-to-all(bf16[16,12,512]{2,1,0:T(8,128)(2,1)} %bitcast.25), channel_id=1, replica_groups={{0,8,16,24,32,40,48,56,64,72,80,88,96,104,112,120},{128,136,144,152,160..., dimensions={0} | all-to-all | bytes 393216 | tf_op jit(solution)/shard_map/all_to_all | solution.py:239
  33.3 0.2 shard_map.81
  33.5 36.7 %all_to_all.16 = bf16[16,8,24,384]{3,2,1,0:T(8,128)(2,1)S(1)} all-to-all(bf16[16,8,24,384]{3,2,1,0:T(8,128)(2,1)S(1)} %shard_map.81), channel_id=1, replica_groups={{0,128,256,384,1,129,257,385,2,130,258,386,3,131,259,387},{8,136,264,39..., dimensions={0} | all-to-all | bytes 4718592 | tf_op jit(solution)/shard_map/all_to_all | solution.py:265
  70.2 1.9 collective-permute-start.4
  72.1 0.1 shard_map.79
  72.2 16.7 %all_to_all.17 = bf16[16,8,24,128]{3,2,1,0:T(8,128)(2,1)} all-to-all(bf16[16,8,24,128]{3,2,1,0:T(8,128)(2,1)S(1)} %shard_map.79), channel_id=1, replica_groups={{0,128,256,384,1,129,257,385,2,130,258,386,3,131,259,387},{8,136,264,39..., dimensions={0} | all-to-all | bytes 1572864 | tf_op jit(solution)/shard_map/all_to_all | solution.py:265
  88.9 0.0 copy-start
  88.9 3.9 %collective-permute-start.1 = (bf16[4,768,128]{2,1,0:T(8,128)(2,1)}, bf16[4,768,128]{2,1,0:T(8,128)(2,1)}, u32[]{:S(2)}, u32[]{:S(2)}) collective-permute-start(bf16[4,768,128]{2,1,0:T(8,128)(2,1)} %bitcast.2.refs_2_), channel_id=1, source_target_pairs={{0,8},{8,0},{16,24},{24,16},{32,40},{40,32},{48,56},{56,48},{64,72... | collective-permute-start | bytes 2359304 | tf_op jit(solution)/shard_map/ppermute | solution.py:21
  92.8 0.0 copy-start.1
  92.8 2.1 dynamic-slice_bitcast_fusion.3
  94.9 1.9 collective-permute-start.5
  96.8 3.1 %collective-permute-start.7 = (bf16[256,384]{1,0:T(8,128)(2,1)}, bf16[256,384]{1,0:T(8,128)(2,1)}, u32[]{:S(2)}, u32[]{:S(2)}) collective-permute-start(bf16[256,384]{1,0:T(8,128)(2,1)} %get-tuple-element.32), channel_id=1, source_target_pairs={{0,3},{1,2},{2,1},{3,0},{4,7},{5,6},{6,5},{7,4},{8,11},{9,10},{10,... | collective-permute-start | bytes 589832 | tf_op jit(solution)/shard_map/ppermute | solution.py:244
  99.9 3.9 %collective-permute-start.6 = (bf16[256,384]{1,0:T(8,128)(2,1)}, bf16[256,384]{1,0:T(8,128)(2,1)}, u32[]{:S(2)}, u32[]{:S(2)}) collective-permute-start(bf16[256,384]{1,0:T(8,128)(2,1)} %get-tuple-element.33), channel_id=1, source_target_pairs={{0,2},{1,3},{2,0},{3,1},{4,6},{5,7},{6,4},{7,5},{8,10},{9,11},{10,... | collective-permute-start | bytes 589832 | tf_op jit(solution)/shard_map/ppermute | solution.py:244
  103.9 0.0 copy-done
  103.9 0.8 slice.4
  104.6 0.0 collective-permute-done.5
  104.6 7.9 %collective-permute-start = (bf16[256,768]{1,0:T(8,128)(2,1)}, bf16[256,768]{1,0:T(8,128)(2,1)S(1)}, u32[]{:S(2)}, u32[]{:S(2)}) collective-permute-start(bf16[256,768]{1,0:T(8,128)(2,1)} %slice.4), channel_id=1, source_target_pairs={{0,4},{4,0},{1,5},{5,1},{2,6},{6,2},{3,7},{7,3},{8,12},{12,8},{9,1... | collective-permute-start | bytes 1179656 | tf_op jit(solution)/shard_map/ppermute | solution.py:25
  112.6 0.0 copy-done.1
  112.6 0.0 collective-permute-done.7
  112.6 0.0 collective-permute-done.6
  112.6 1.3 pad_maximum_fusion.refs_1_.refs_0_
  114.0 6.1 %collective-permute-start.9 = (bf16[2,192,384]{2,1,0:T(8,128)(2,1)S(1)}, bf16[2,192,384]{2,1,0:T(8,128)(2,1)S(1)}, u32[]{:S(2)}, u32[]{:S(2)}) collective-permute-start(bf16[2,192,384]{2,1,0:T(8,128)(2,1)S(1)} %constant_dynamic-slice_fusion), channel_id=1, source_target_pairs={{0,4},{4,0},{1,5},{5,1},{2,6},{6,2},{3,7},{7,3},{8,12},{12,8},{9,1... | collective-permute-start | bytes 884744 | tf_op jit(solution)/shard_map/ppermute | solution.py:25
  120.1 14.9 %collective-permute-done.refs_2_ = bf16[256,768]{1,0:T(8,128)(2,1)S(1)} collective-permute-done((bf16[256,768]{1,0:T(8,128)(2,1)}, bf16[256,768]{1,0:T(8,128)(2,1)S(1)}, u32[]{:S(2)}, u32[]{:S(2)}) %collective-permute-start) | collective-permute-done | bytes 393248 | tf_op jit(solution)/shard_map/ppermute | solution.py:25
  135.0 0.5 shard_map.77.refs_1_
  135.6 0.0 collective-permute-done.1.refs_3_
  135.6 3.1 %shard_map.80 = (bf16[128,768]{1,0:T(8,128)(2,1)S(1)}, bf16[128,768]{1,0:T(8,128)(2,1)S(1)}) custom-call(bf16[256,1536]{1,0:T(8,128)(2,1)S(1)} %bitcast.23, bf16[256,768]{1,0:T(8,128)(2,1)S(1)} %shard_map.77.refs_1_, bf16[4,768,128]{2,1,0:T(8,128)(2,1)} %bitcast.2.refs_2_, bf16[4,768,128]{2,1,0:T(8,128)(2,1)} %collective-permute-done.1.refs_3_), custom_call_target="tpu_custom_call" | custom-call | flops 301989888 | bytes 3145728 | tf_op jit(solution)/shard_map/pallas_call | solution.py:48
  138.7 8.4 %collective-permute-start.2 = (bf16[128,768]{1,0:T(8,128)(2,1)S(1)}, bf16[128,768]{1,0:T(8,128)(2,1)S(1)}, u32[]{:S(2)}, u32[]{:S(2)}) collective-permute-start(bf16[128,768]{1,0:T(8,128)(2,1)S(1)} %get-tuple-element.16.refs_1_.refs_2_), channel_id=1, source_target_pairs={{8,16},{24,32},{40,48},{56,64},{72,80},{88,96},{104,112},{120,128}... | collective-permute-start | bytes 589832 | tf_op jit(solution)/shard_map/ppermute | solution.py:21
  147.2 1.9 collective-permute-start.3
  149.1 9.5 %collective-permute-start.8 = (bf16[2,64,384]{2,1,0:T(8,128)(2,1)S(1)}, bf16[2,64,384]{2,1,0:T(8,128)(2,1)S(1)}, u32[]{:S(2)}, u32[]{:S(2)}) collective-permute-start(bf16[2,64,384]{2,1,0:T(8,128)(2,1)S(1)} %constant_dynamic-slice_fusion.1), channel_id=1, source_target_pairs={{0,4},{4,0},{1,5},{5,1},{2,6},{6,2},{3,7},{7,3},{8,12},{12,8},{9,1... | collective-permute-start | bytes 294920 | tf_op jit(solution)/shard_map/ppermute | solution.py:25
  158.6 3.8 %shard_map.83 = (bf16[768,768]{1,0:T(8,128)(2,1)S(1)}, f32[256,768]{1,0:T(8,128)S(1)}) custom-call(s32[1,768]{1,0:T(1,128)S(1)} %broadcast_in_dim.9.refs_0_, bf16[4,256,384]{2,1,0:T(8,128)(2,1)S(1)} %pad_maximum_fusion.refs_1_.refs_0_, bf16[4,768,128]{2,1,0:T(8,128)(2,1)} %bitcast.2.refs_2_, bf16[4,768,128]{2,1,0:T(8,128)(2,1)} %collective-permute-done.1.refs_3_), custom_call_target="tpu_custom_call" | custom-call | flops 905969664 | bytes 4328448 | tf_op jit(solution)/shard_map/pallas_call | solution.py:48
  162.4 16.0 %collective-permute-done.2.refs_0_ = bf16[128,768]{1,0:T(8,128)(2,1)S(1)} collective-permute-done((bf16[128,768]{1,0:T(8,128)(2,1)S(1)}, bf16[128,768]{1,0:T(8,128)(2,1)S(1)}, u32[]{:S(2)}, u32[]{:S(2)}) %collective-permute-start.2) | collective-permute-done | bytes 196640 | tf_op jit(solution)/shard_map/ppermute | solution.py:21
  178.4 0.0 collective-permute-done.3.refs_3_
  178.4 0.0 collective-permute-done.4.refs_5_.refs_4_
  178.4 3.4 %shard_map.82 = (bf16[256,768]{1,0:T(8,128)(2,1)S(1)}, f32[256,768]{1,0:T(8,128)S(1)}, bf16[768,768]{1,0:T(8,128)(2,1)S(1)}) custom-call(bf16[128,768]{1,0:T(8,128)(2,1)S(1)} %collective-permute-done.2.refs_0_, bf16[128,768]{1,0:T(8,128)(2,1)S(1)} %get-tuple-element.16.refs_1_.refs_2_, bf16[128,768]{1,0:T(8,128)(2,1)S(1)} %get-tuple-element.17.refs_2_.refs_3_, ...), custom_call_target="tpu_custom_call" | custom-call | flops 905969664 | bytes 7864320 | tf_op jit(solution)/shard_map/pallas_call | solution.py:48
  181.8 0.0 collective-permute-done.8.refs_0_
  181.8 0.0 collective-permute-done.9.refs_1_
  181.8 1.1 shard_map.84
  182.9 21.4 %collective-permute-start.11 = (bf16[128,768]{1,0:T(8,128)(2,1)S(1)}, bf16[128,768]{1,0:T(8,128)(2,1)S(1)}, u32[]{:S(2)}, u32[]{:S(2)}) collective-permute-start(bf16[128,768]{1,0:T(8,128)(2,1)S(1)} %get-tuple-element.24.refs_1_), channel_id=1, source_target_pairs={{8,16},{24,32},{40,48},{56,64},{72,80},{88,96},{104,112},{120,128}... | collective-permute-start | bytes 589832 | tf_op jit(solution)/shard_map/ppermute | solution.py:21
  204.3 1.9 collective-permute-start.10
  206.2 3.1 %shard_map.85 = bf16[256,1536]{1,0:T(8,128)(2,1)} custom-call(bf16[256,1536]{1,0:T(8,128)(2,1)S(1)} %bitcast.24, bf16[256,768]{1,0:T(8,128)(2,1)S(1)} %get-tuple-element.18.refs_1_, bf16[128,768]{1,0:T(8,128)(2,1)S(1)} %get-tuple-element.16.refs_1_.refs_2_, bf16[128,768]{1,0:T(8,128)(2,1)S(1)} %get-tuple-element.17.refs_2_.refs_3_, ...), custom_call_target="tpu_custom_call" | custom-call | flops 301989888 | bytes 7274496 | tf_op jit(solution)/shard_map/pallas_call | solution.py:48
  209.3 2.9 %shard_map.86 = (f32[128,768]{1,0:T(8,128)S(1)}, f32[128,768]{1,0:T(8,128)S(1)}, bf16[768,768]{1,0:T(8,128)(2,1)S(1)}, bf16[768,768]{1,0:T(8,128)(2,1)S(1)}) custom-call(bf16[4,256,384]{2,1,0:T(8,128)(2,1)S(1)} %pad_maximum_fusion.refs_1_.refs_0_, bf16[128,768]{1,0:T(8,128)(2,1)S(1)} %get-tuple-element.24.refs_1_, ...), custom_call_target="tpu_custom_call" | custom-call | flops 603979776 | bytes 9043968 | tf_op jit(solution)/shard_map/pallas_call | solution.py:48
  212.2 0.0 collective-permute-done.11.refs_1_
  212.2 0.0 collective-permute-done.10.refs_0_
  212.2 1.4 shard_map.87
  (3 shorter events, 0.1 us)
Async XLA Ops:
  70.2 108.2 %collective-permute-start.4 = (bf16[4,768,384]{2,1,0:T(8,128)(2,1)S(1)}, bf16[4,768,384]{2,1,0:T(8,128)(2,1)}, u32[]{:S(2)}, u32[]{:S(2)}) collective-permute-start(bf16[4,768,384]{2,1,0:T(8,128)(2,1)S(1)} %bitcast.17), channel_id=1, source_target_pairs={{0,8},{8,0},{16,24},{24,16},{32,40},{40,32},{48,56},{56,48},{64,72... | collective-permute-start | bytes 7077896 | tf_op jit(solution)/shard_map/ppermute | solution.py:21
  88.9 14.9 %copy-start = (bf16[1,1,256,1536]{3,2,1,0:T(8,128)(2,1)S(1)}, bf16[1,1,256,1536]{3,2,1,0:T(8,128)(2,1)}, u32[]{:S(2)}) copy-start(bf16[1,1,256,1536]{3,2,1,0:T(8,128)(2,1)} %param.6) | copy-start | bytes 2359300
  88.9 46.7 %collective-permute-start.1 = (bf16[4,768,128]{2,1,0:T(8,128)(2,1)}, bf16[4,768,128]{2,1,0:T(8,128)(2,1)}, u32[]{:S(2)}, u32[]{:S(2)}) collective-permute-start(bf16[4,768,128]{2,1,0:T(8,128)(2,1)} %bitcast.2.refs_2_), channel_id=1, source_target_pairs={{0,8},{8,0},{16,24},{24,16},{32,40},{40,32},{48,56},{56,48},{64,72... | collective-permute-start | bytes 2359304 | tf_op jit(solution)/shard_map/ppermute | solution.py:21
  92.8 19.8 %copy-start.1 = (s32[768]{0:T(1024)S(1)}, s32[768]{0:T(1024)}, u32[]{:S(2)}) copy-start(s32[768]{0:T(1024)} %param.11) | copy-start | bytes 9220
  94.9 9.8 %collective-permute-start.5 = (bf16[256,384]{1,0:T(8,128)(2,1)S(1)}, bf16[256,384]{1,0:T(8,128)(2,1)}, u32[]{:S(2)}, u32[]{:S(2)}) collective-permute-start(bf16[256,384]{1,0:T(8,128)(2,1)S(1)} %get-tuple-element.31), channel_id=1, source_target_pairs={{0,1},{1,0},{2,3},{3,2},{4,5},{5,4},{6,7},{7,6},{8,9},{9,8},{10,11... | collective-permute-start | bytes 589832 | tf_op jit(solution)/shard_map/ppermute | solution.py:244
  96.8 15.8 %collective-permute-start.7 = (bf16[256,384]{1,0:T(8,128)(2,1)}, bf16[256,384]{1,0:T(8,128)(2,1)}, u32[]{:S(2)}, u32[]{:S(2)}) collective-permute-start(bf16[256,384]{1,0:T(8,128)(2,1)} %get-tuple-element.32), channel_id=1, source_target_pairs={{0,3},{1,2},{2,1},{3,0},{4,7},{5,6},{6,5},{7,4},{8,11},{9,10},{10,... | collective-permute-start | bytes 589832 | tf_op jit(solution)/shard_map/ppermute | solution.py:244
  99.9 12.7 %collective-permute-start.6 = (bf16[256,384]{1,0:T(8,128)(2,1)}, bf16[256,384]{1,0:T(8,128)(2,1)}, u32[]{:S(2)}, u32[]{:S(2)}) collective-permute-start(bf16[256,384]{1,0:T(8,128)(2,1)} %get-tuple-element.33), channel_id=1, source_target_pairs={{0,2},{1,3},{2,0},{3,1},{4,6},{5,7},{6,4},{7,5},{8,10},{9,11},{10,... | collective-permute-start | bytes 589832 | tf_op jit(solution)/shard_map/ppermute | solution.py:244
  104.6 30.4 %collective-permute-start = (bf16[256,768]{1,0:T(8,128)(2,1)}, bf16[256,768]{1,0:T(8,128)(2,1)S(1)}, u32[]{:S(2)}, u32[]{:S(2)}) collective-permute-start(bf16[256,768]{1,0:T(8,128)(2,1)} %slice.4), channel_id=1, source_target_pairs={{0,4},{4,0},{1,5},{5,1},{2,6},{6,2},{3,7},{7,3},{8,12},{12,8},{9,1... | collective-permute-start | bytes 1179656 | tf_op jit(solution)/shard_map/ppermute | solution.py:25
  114.0 67.8 %collective-permute-start.9 = (bf16[2,192,384]{2,1,0:T(8,128)(2,1)S(1)}, bf16[2,192,384]{2,1,0:T(8,128)(2,1)S(1)}, u32[]{:S(2)}, u32[]{:S(2)}) collective-permute-start(bf16[2,192,384]{2,1,0:T(8,128)(2,1)S(1)} %constant_dynamic-slice_fusion), channel_id=1, source_target_pairs={{0,4},{4,0},{1,5},{5,1},{2,6},{6,2},{3,7},{7,3},{8,12},{12,8},{9,1... | collective-permute-start | bytes 884744 | tf_op jit(solution)/shard_map/ppermute | solution.py:25
  138.7 39.7 %collective-permute-start.2 = (bf16[128,768]{1,0:T(8,128)(2,1)S(1)}, bf16[128,768]{1,0:T(8,128)(2,1)S(1)}, u32[]{:S(2)}, u32[]{:S(2)}) collective-permute-start(bf16[128,768]{1,0:T(8,128)(2,1)S(1)} %get-tuple-element.16.refs_1_.refs_2_), channel_id=1, source_target_pairs={{8,16},{24,32},{40,48},{56,64},{72,80},{88,96},{104,112},{120,128}... | collective-permute-start | bytes 589832 | tf_op jit(solution)/shard_map/ppermute | solution.py:21
  147.2 31.2 %collective-permute-start.3 = (bf16[128,768]{1,0:T(8,128)(2,1)S(1)}, bf16[128,768]{1,0:T(8,128)(2,1)S(1)}, u32[]{:S(2)}, u32[]{:S(2)}) collective-permute-start(bf16[128,768]{1,0:T(8,128)(2,1)S(1)} %get-tuple-element.17.refs_2_.refs_3_), channel_id=1, source_target_pairs={{0,8},{8,0},{16,24},{24,16},{32,40},{40,32},{48,56},{56,48},{64,72... | collective-permute-start | bytes 589832 | tf_op jit(solution)/shard_map/ppermute | solution.py:21
  149.1 32.7 %collective-permute-start.8 = (bf16[2,64,384]{2,1,0:T(8,128)(2,1)S(1)}, bf16[2,64,384]{2,1,0:T(8,128)(2,1)S(1)}, u32[]{:S(2)}, u32[]{:S(2)}) collective-permute-start(bf16[2,64,384]{2,1,0:T(8,128)(2,1)S(1)} %constant_dynamic-slice_fusion.1), channel_id=1, source_target_pairs={{0,4},{4,0},{1,5},{5,1},{2,6},{6,2},{3,7},{7,3},{8,12},{12,8},{9,1... | collective-permute-start | bytes 294920 | tf_op jit(solution)/shard_map/ppermute | solution.py:25
  182.9 29.3 %collective-permute-start.11 = (bf16[128,768]{1,0:T(8,128)(2,1)S(1)}, bf16[128,768]{1,0:T(8,128)(2,1)S(1)}, u32[]{:S(2)}, u32[]{:S(2)}) collective-permute-start(bf16[128,768]{1,0:T(8,128)(2,1)S(1)} %get-tuple-element.24.refs_1_), channel_id=1, source_target_pairs={{8,16},{24,32},{40,48},{56,64},{72,80},{88,96},{104,112},{120,128}... | collective-permute-start | bytes 589832 | tf_op jit(solution)/shard_map/ppermute | solution.py:21
  204.3 8.0 %collective-permute-start.10 = (bf16[128,768]{1,0:T(8,128)(2,1)S(1)}, bf16[128,768]{1,0:T(8,128)(2,1)S(1)}, u32[]{:S(2)}, u32[]{:S(2)}) collective-permute-start(bf16[128,768]{1,0:T(8,128)(2,1)S(1)} %get-tuple-element.23.refs_6_.refs_2_), channel_id=1, source_target_pairs={{0,8},{8,0},{16,24},{24,16},{32,40},{40,32},{48,56},{56,48},{64,72... | collective-permute-start | bytes 589832 | tf_op jit(solution)/shard_map/ppermute | solution.py:21
